TPU v7x, 128 devices: a whole 4x4x4 slice. The times are simulated.
128 devices in a mesh: ctx: 8 (over y, x_lo), tp: 16 (over x_hi, z, core).
Axes of the slice: x: 4 (x_hi: 2, x_lo: 2; x = x_hi * 2 + x_lo), y: 4, z: 4, core: 2. Of those that a mesh axis runs over, the one named last changes fastest.
Arguments:
- tokens: bfloat16 [4096, 4096], P(('ctx', 'tp')), may hold values from -16 to 16
- upstream: bfloat16 [4096, 4096], P('ctx', 'tp'), may hold values from -6 to 6
- w_query: bfloat16 [4096, 4096], P('ctx', 'tp')
- w_keyval: bfloat16 [4096, 2048], P('ctx', 'tp')
- positions: int32 [4096], replicated, may hold values from 0 to 4095, as said below
- documents: int32 [4096], replicated, may hold values from 0 to 3, never falling along the last dimension, each value on 1 to 2048 neighbouring positions
Outputs:
- token_grad: bfloat16 [4096, 4096], P(('ctx', 'tp'))
- query_grad: float32 [4096, 4096], P('ctx', 'tp')
- keyval_grad: float32 [4096, 2048], P('ctx', 'tp')
Inputs may be any that keep to these rules, and one draw needn't show every extreme that they name: Each stored run of 512 tokens holds consecutive increasing positions; the two runs of the tokens of one context rank are the blocks k and 15 - k of the sequence for some k; all runs together hold every position once.
All inputs are finite; a program needn't handle non-finite values.
Results may differ from a plain program's by a relative error of at most 0.02.
The roundings to bfloat16 on the way count: a program that leaves them out, or rounds other values in their place, can miss the bound.
Values may be sent and summed in bfloat16 or wider, within the bound.
A program may use at most 128 MiB of HBM per device.

v0:
```python
import jax
import jax.numpy as jnp
from jax import lax
from jax.sharding import PartitionSpec as P

KEY_VALUE_HEADS = 8
HEAD_DIMENSION = 128


rope_base = 500000.0


def side_by_side(arrays, axis, dim, along):
    both = jnp.concatenate(arrays, axis=along)
    filled, at, gathered = (lax.all_gather(both, axis, axis=dim, tiled=True), 0, [])
    for a in arrays:
        gathered.append(lax.slice_in_dim(filled, at, at + a.shape[along], axis=along))
        at += a.shape[along]
    return tuple(gathered)


def partner_2(block, axis, bit):
    count = lax.axis_size(axis)
    route = []
    for low in range(count):
        high = low | 1 << bit
        if high != low and high < count:
            route += [(low, high), (high, low)]
    return lax.ppermute(block, axis, route)


def copy_for_each(x, axis):
    count = lax.axis_size(axis)
    return lax.all_to_all(jnp.broadcast_to(x[None], (count, *x.shape)), axis, 0, 0, tiled=True)


def laid_out(blocks, dim):
    lengths = list(blocks.shape[1:])
    lengths[dim] *= blocks.shape[0]
    return jnp.moveaxis(blocks, 0, dim).reshape(lengths)


def gathered_copies(x, axis, dim):
    blocks = copy_for_each(x, axis)
    return laid_out(blocks, dim)


def cut_along(x, dim, count):
    lengths = x.shape
    blocks = x.reshape(*lengths[:dim], count, lengths[dim] // count, *lengths[dim + 1 :])
    return jnp.moveaxis(blocks, dim, 0)


def summed_on_arrival(x, axis, dim):
    count = lax.axis_size(axis)
    blocks = lax.all_to_all(cut_along(x, dim, count), axis, 0, 0, tiled=True)
    return jnp.sum(blocks.astype(jnp.float32), axis=0)


def rotation_tables(positions):
    half_width = HEAD_DIMENSION // 2
    frequency = rope_base ** (-(jnp.arange(half_width, dtype=jnp.float32) * 2.0 / HEAD_DIMENSION))
    angles = positions.astype(jnp.float32)[:, None] * frequency[None, :]
    cosine = jnp.concatenate([jnp.cos(angles), jnp.cos(angles)], axis=1)
    sine = jnp.concatenate([jnp.sin(angles), jnp.sin(angles)], axis=1)
    return (cosine, sine)


def rotate(values, cosine, sine):
    half_width = values.shape[-1] // 2
    turned = jnp.concatenate([-values[..., half_width:], values[..., :half_width]], axis=-1)
    return values * cosine[:, None, :] + turned * sine[:, None, :]


def rotate_back(gradient, cosine, sine):
    half_width = gradient.shape[-1] // 2
    scaled = gradient * sine[:, None, :]
    turned = jnp.concatenate([scaled[..., half_width:], -scaled[..., :half_width]], axis=-1)
    return gradient * cosine[:, None, :] + turned


def attend(
    query_rows, grad_out, keys_all, values_all, query_pos, query_doc, key_pos, key_doc, scaling
):
    f32 = jnp.float32
    tok_rows, head_count, head_width = query_rows.shape
    block_rows = min(tok_rows, 128)
    block_count = tok_rows // block_rows
    seq_len = keys_all.shape[0]

    def advance(totals, inputs):
        key_total, value_total = totals
        query_block, grad_block, pos_block, doc_block = inputs
        scores = (
            jnp.einsum("qhd,kd->hqk", query_block, keys_all, preferred_element_type=f32) * scaling
        )
        visible = (key_pos[None, :] <= pos_block[:, None]) & (
            key_doc[None, :] == doc_block[:, None]
        )
        scores = jnp.where(visible[None], scores, -1e30)
        row_peak = jnp.max(scores, axis=-1, keepdims=True)
        exponent = jnp.exp(scores - row_peak)
        probs = exponent / jnp.sum(exponent, axis=-1, keepdims=True)
        probs_half = probs.astype(jnp.bfloat16)
        output = jnp.einsum("hqk,kd->qhd", probs_half, values_all, preferred_element_type=f32)
        deltas = jnp.sum(grad_block.astype(f32) * output, axis=-1)
        prob_grad = jnp.einsum("qhd,kd->hqk", grad_block, values_all, preferred_element_type=f32)
        score_grad = (probs * (prob_grad - deltas.T[:, :, None])).astype(jnp.bfloat16)
        dquery = (
            jnp.einsum("hqk,kd->qhd", score_grad, keys_all, preferred_element_type=f32) * scaling
        )
        key_total = (
            key_total
            + jnp.einsum("hqk,qhd->kd", score_grad, query_block, preferred_element_type=f32)
            * scaling
        )
        value_total = value_total + jnp.einsum(
            "hqk,qhd->kd", probs_half, grad_block, preferred_element_type=f32
        )
        return ((key_total, value_total), dquery)

    blank_keys = jnp.zeros((seq_len, head_width), f32)
    inputs = (
        query_rows.reshape(block_count, block_rows, head_count, head_width),
        grad_out.reshape(block_count, block_rows, head_count, head_width),
        query_pos.reshape(block_count, block_rows),
        query_doc.reshape(block_count, block_rows),
    )
    (key_total, value_total), dquery = lax.scan(advance, (blank_keys, blank_keys), inputs)
    return (dquery.reshape(tok_rows, head_count, head_width), key_total, value_total)


def shards(tokens, upstream, w_query, w_keyval, positions, documents):
    f32 = jnp.float32
    ctx_rank = lax.axis_index("ctx")
    tp_rank = lax.axis_index("tp")
    tensor_split_count = lax.axis_size("tp")
    gathered = lax.all_gather(tokens, "tp", axis=0, tiled=True)
    tok_rows = gathered.shape[0]
    query_cols = w_query.shape[1]
    head_count = query_cols // HEAD_DIMENSION
    pairing_flags = (tensor_split_count // KEY_VALUE_HEADS).bit_length() - 1
    doc_all = jnp.take(documents, positions)
    cosine_all, sine_all = rotation_tables(positions)
    row_offset = ctx_rank * tok_rows
    my_pos = lax.dynamic_slice_in_dim(positions, row_offset, tok_rows, 0)
    my_doc = lax.dynamic_slice_in_dim(doc_all, row_offset, tok_rows, 0)
    my_cos = lax.dynamic_slice_in_dim(cosine_all, row_offset, tok_rows, 0)
    my_sin = lax.dynamic_slice_in_dim(sine_all, row_offset, tok_rows, 0)
    query_full, keyval_full = side_by_side((w_query, w_keyval), "ctx", 0, 1)
    query_raw = jnp.dot(gathered, query_full, preferred_element_type=f32)
    keyval_raw = jnp.dot(gathered, keyval_full, preferred_element_type=f32)
    query_rot = rotate(
        query_raw.reshape(tok_rows, head_count, HEAD_DIMENSION), my_cos, my_sin
    ).astype(jnp.bfloat16)
    head_kv = keyval_raw.astype(jnp.bfloat16)
    bit_index = 0
    partner = partner_2(head_kv, "tp", bit_index)
    is_lower = tp_rank // (1 << bit_index) % 2 == 0
    head_kv = jnp.where(
        is_lower,
        jnp.concatenate([head_kv, partner], axis=1),
        jnp.concatenate([partner, head_kv], axis=1),
    )
    key_rot = rotate(head_kv[:, None, :HEAD_DIMENSION].astype(f32), my_cos, my_sin)[:, 0].astype(
        jnp.bfloat16
    )
    local_kv = jnp.concatenate([key_rot, head_kv[:, HEAD_DIMENSION:]], axis=1)
    key_value = gathered_copies(local_kv, "ctx", 0)
    grad_query, grad_key, grad_value = attend(
        query_rot,
        upstream.reshape(tok_rows, head_count, HEAD_DIMENSION),
        key_value[:, :HEAD_DIMENSION],
        key_value[:, HEAD_DIMENSION:],
        my_pos,
        my_doc,
        positions,
        doc_all,
        HEAD_DIMENSION ** (-0.5),
    )
    query_back = (
        rotate_back(grad_query, my_cos, my_sin).astype(jnp.bfloat16).reshape(tok_rows, query_cols)
    )
    key_backward = rotate_back(grad_key[:, None, :], cosine_all, sine_all)[:, 0]
    key_terms = jnp.concatenate([key_backward, grad_value], axis=1)
    head_grad = summed_on_arrival(key_terms.astype(jnp.bfloat16), "ctx", 0)
    for bit_index in reversed(range(pairing_flags)):
        half_width = head_grad.shape[1] // 2
        lower_half = head_grad[:, :half_width]
        upper_half = head_grad[:, half_width:]
        is_lower = tp_rank // (1 << bit_index) % 2 == 0
        retained = jnp.where(is_lower, lower_half, upper_half)
        outgoing = jnp.where(is_lower, upper_half, lower_half)
        head_grad = retained + partner_2(outgoing.astype(jnp.bfloat16), "tp", bit_index).astype(
            outgoing.dtype
        )
    key_value_backward = head_grad.astype(jnp.bfloat16)
    row_grads = jnp.concatenate([query_back, key_value_backward], axis=1)
    part_query = lax.dot_general(
        row_grads[:, :query_cols], query_full, (((1,), (1,)), ((), ())), preferred_element_type=f32
    )
    part_keyval = lax.dot_general(
        row_grads[:, query_cols:], keyval_full, (((1,), (1,)), ((), ())), preferred_element_type=f32
    )
    token_grad = lax.psum_scatter(
        (part_query + part_keyval).astype(jnp.bfloat16), "tp", scatter_dimension=0, tiled=True
    )
    weight_grad = summed_on_arrival(
        lax.dot_general(
            gathered, row_grads, (((0,), (0,)), ((), ())), preferred_element_type=f32
        ).astype(jnp.bfloat16),
        "ctx",
        0,
    )
    return (token_grad, weight_grad[:, :query_cols], weight_grad[:, query_cols:])


def solution(mesh):
    return jax.shard_map(
        shards,
        mesh=mesh,
        in_specs=(P(("ctx", "tp"), None), P("ctx", "tp"), P("ctx", "tp"), P("ctx", "tp"), P(), P()),
        out_specs=(P(("ctx", "tp"), None), P("ctx", "tp"), P("ctx", "tp")),
        check_vma=False,
    )
```

profile of v0, /device:TPU:0, one launch (start us, length us, event | category | flops | bytes accessed | tf_op | source)
XLA Modules:
  0.0 420.5 jit_solution(1429676096698661029)
XLA Ops:
  7.2 1.8 pad_maximum_fusion.3
  10.5 23.0 %gather_fusion = s32[4096]{0:T(1024)S(1)} fusion(s32[4096]{0:T(1024)S(1)} %copy-done, s32[4096]{0:T(1024)S(1)} %fusion.68), kind=kCustom, calls=%fused_computation | custom fusion | bytes 49152 | tf_op jit(solution)/shard_map/jit(_take)/gather | solution.py:143
  33.6 50.6 %all-gather.3.cloned.1.call-done = bf16[4096,384]{1,0:T(8,128)(2,1)} async-done(((bf16[512,384]{1,0:T(8,128)(2,1)}), bf16[4096,384]{1,0:T(8,128)(2,1)}) %all-gather.3.cloned.1.call-update) | async-done | bytes 3145744 | tf_op jit(solution)/shard_map/all_gather | solution.py:15
  84.2 57.0 %all-gather.5.cloned.1.call-done = bf16[512,4096]{1,0:T(8,128)(2,1)} async-done(((bf16[32,4096]{1,0:T(8,128)(2,1)}), bf16[512,4096]{1,0:T(8,128)(2,1)}) %all-gather.5.cloned.1.call-update) | async-done | bytes 4194320 | tf_op jit(solution)/shard_map/all_gather | solution.py:138
  141.2 4.0 fusion.52
  145.5 3.7 multiply_cosine_fusion
  152.2 4.4 %all-to-all-start = ((bf16[8,512,256]{1,2,0:T(8,128)(2,1)}), bf16[8,512,256]{1,2,0:T(8,128)(2,1)S(1)}, u32[]{:S(2)}, u32[]{:S(2)}) async-start(bf16[8,512,256]{1,2,0:T(8,128)(2,1)} %broadcast_in_dim.33), calls=%async_computation | async-start | bytes 4194304 | tf_op jit(solution)/shard_map/all_to_all | solution.py:34
  157.5 4.1 fusion.50
  167.4 2.0 fusion.59
  169.4 1.8 copy.73
  171.2 12.9 %all-to-all-done = bf16[8,512,256]{1,2,0:T(8,128)(2,1)S(1)} async-done(((bf16[8,512,256]{1,2,0:T(8,128)(2,1)}), bf16[8,512,256]{1,2,0:T(8,128)(2,1)S(1)}, u32[]{:S(2)}, u32[]{:S(2)}) %all-to-all-start) | async-done | bytes 2097184 | tf_op jit(solution)/shard_map/all_to_all | solution.py:34
  184.1 2.4 copy.72
  186.5 2.6 fusion.77
  189.6 89.4 %while.15 = (s32[]{:T(128)}, f32[4096,128]{1,0:T(8,128)}, f32[4096,128]{1,0:T(8,128)}, f32[4,128,2,128]{3,1,2,0:T(8,128)}, s32[4096]{0:T(1024)S(1)}, /*index=5*/...) while((s32[]{:T(128)}, f32[4096,128]{1,0:T(8,128)}, ...), condition=%wide.region_4.5_spmd.clone, body=%wide.region_0.4_spmd.clone.sunk | while | flops 1625427712 | bytes 64595660 | solution.py:129
  190.1 4.9 %fusion.118 = (f32[2,128]{1,0:T(2,128)S(1)}, f32[2,128,4096]{2,1,0:T(8,128)}) fusion(pred[128,4096]{1,0:T(8,128)(4,1)S(1)} %compare_and_fusion.2, bf16[4096,128]{1,0:T(8,128)(2,1)} %get-tuple-element.330, bf16[4,128,2,128]{3,1,2,0:T(8,128)(2,1)} %get-tuple-element.329, s32[]{:T(128)} %get-tuple-element.307), kind=kOutput, calls=%fused_computation.112.clone.1 | convolution fusion | flops 272633856 | bytes 5834240 | tf_op jit(solution)/shard_map/while/body/eval_jaxpr/sub | solution.py:102
  195.1 2.8 fusion.119
  199.6 2.1 fusion.121
  201.6 4.0 fusion.122
  205.6 2.6 fusion.124
  208.2 2.1 fusion.123
  210.8 4.9 %fusion.118 = (f32[2,128]{1,0:T(2,128)S(1)}, f32[2,128,4096]{2,1,0:T(8,128)}) fusion(pred[128,4096]{1,0:T(8,128)(4,1)S(1)} %compare_and_fusion.2, bf16[4096,128]{1,0:T(8,128)(2,1)} %get-tuple-element.330, bf16[4,128,2,128]{3,1,2,0:T(8,128)(2,1)} %get-tuple-element.329, s32[]{:T(128)} %get-tuple-element.307), kind=kOutput, calls=%fused_computation.112.clone.1 | convolution fusion | flops 272633856 | bytes 5834240 | tf_op jit(solution)/shard_map/while/body/eval_jaxpr/sub | solution.py:102
  215.7 2.8 fusion.119
  220.2 2.1 fusion.121
  222.3 4.6 %fusion.122 = f32[4096,128]{1,0:T(8,128)} fusion(bf16[2,128,4096]{2,1,0:T(8,128)(2,1)} %fusion.121, f32[4096,128]{1,0:T(8,128)} %get-tuple-element.308, pred[]{:T(512)S(6)} %compare.5, bf16[4,128,2,128]{3,1,2,0:T(8,128)(2,1)} %get-tuple-element.329, s32[]{:T(128)} %get-tuple-element.307), kind=kOutput, calls=%fused_computation.14.clone.1 | convolution fusion | flops 270008320 | bytes 6357505 | tf_op jit(solution)/shard_map/while/body/eval_jaxpr/hqk,qhd->kd/dot_general | solution.py:114
  226.9 2.6 fusion.124
  229.5 3.7 fusion.123
  233.7 4.9 %fusion.118 = (f32[2,128]{1,0:T(2,128)S(1)}, f32[2,128,4096]{2,1,0:T(8,128)}) fusion(pred[128,4096]{1,0:T(8,128)(4,1)S(1)} %compare_and_fusion.2, bf16[4096,128]{1,0:T(8,128)(2,1)} %get-tuple-element.330, bf16[4,128,2,128]{3,1,2,0:T(8,128)(2,1)} %get-tuple-element.329, s32[]{:T(128)} %get-tuple-element.307), kind=kOutput, calls=%fused_computation.112.clone.1 | convolution fusion | flops 272633856 | bytes 5834240 | tf_op jit(solution)/shard_map/while/body/eval_jaxpr/sub | solution.py:102
  238.6 2.8 fusion.119
  243.1 2.1 fusion.121
  245.2 4.6 %fusion.122 = f32[4096,128]{1,0:T(8,128)} fusion(bf16[2,128,4096]{2,1,0:T(8,128)(2,1)} %fusion.121, f32[4096,128]{1,0:T(8,128)} %get-tuple-element.308, pred[]{:T(512)S(6)} %compare.5, bf16[4,128,2,128]{3,1,2,0:T(8,128)(2,1)} %get-tuple-element.329, s32[]{:T(128)} %get-tuple-element.307), kind=kOutput, calls=%fused_computation.14.clone.1 | convolution fusion | flops 270008320 | bytes 6357505 | tf_op jit(solution)/shard_map/while/body/eval_jaxpr/hqk,qhd->kd/dot_general | solution.py:114
  249.8 2.6 fusion.124
  252.4 3.7 fusion.123
  256.6 4.9 %fusion.118 = (f32[2,128]{1,0:T(2,128)S(1)}, f32[2,128,4096]{2,1,0:T(8,128)}) fusion(pred[128,4096]{1,0:T(8,128)(4,1)S(1)} %compare_and_fusion.2, bf16[4096,128]{1,0:T(8,128)(2,1)} %get-tuple-element.330, bf16[4,128,2,128]{3,1,2,0:T(8,128)(2,1)} %get-tuple-element.329, s32[]{:T(128)} %get-tuple-element.307), kind=kOutput, calls=%fused_computation.112.clone.1 | convolution fusion | flops 272633856 | bytes 5834240 | tf_op jit(solution)/shard_map/while/body/eval_jaxpr/sub | solution.py:102
  261.5 2.8 fusion.119
  266.0 2.1 fusion.121
  268.1 4.6 %fusion.122 = f32[4096,128]{1,0:T(8,128)} fusion(bf16[2,128,4096]{2,1,0:T(8,128)(2,1)} %fusion.121, f32[4096,128]{1,0:T(8,128)} %get-tuple-element.308, pred[]{:T(512)S(6)} %compare.5, bf16[4,128,2,128]{3,1,2,0:T(8,128)(2,1)} %get-tuple-element.329, s32[]{:T(128)} %get-tuple-element.307), kind=kOutput, calls=%fused_computation.14.clone.1 | convolution fusion | flops 270008320 | bytes 6357505 | tf_op jit(solution)/shard_map/while/body/eval_jaxpr/hqk,qhd->kd/dot_general | solution.py:114
  272.7 2.6 fusion.124
  275.3 3.7 fusion.123
  279.0 2.0 copy.81
  284.2 1.8 convert.9
  286.3 2.4 copy.84
  288.7 3.7 all-to-all-start.1
  294.0 24.9 %all-to-all-done.1 = bf16[8,512,256]{1,2,0:T(8,128)(2,1)S(1)} async-done(((bf16[8,512,256]{1,2,0:T(8,128)(2,1)}), bf16[8,512,256]{1,2,0:T(8,128)(2,1)S(1)}, u32[]{:S(2)}, u32[]{:S(2)}) %all-to-all-start.1) | async-done | bytes 2097184 | tf_op jit(solution)/shard_map/all_to_all | solution.py:56
  319.3 2.9 fusion.48
  322.3 4.5 %add_convert_fusion = bf16[512,4096]{1,0:T(8,128)(2,1)} fusion(f32[512,4096]{1,0:T(8,128)S(1)} %fusion.48, bf16[512,128]{0,1:T(8,128)(2,1)S(1)} %add_convert_fusion.1, bf16[4096,384]{1,0:T(8,128)(2,1)} %all-gather.3.cloned.1.call-done), kind=kOutput, calls=%fused_computation.47 | convolution fusion | flops 541065216 | bytes 13762560 | tf_op jit(solution)/shard_map/dot_general | solution.py:202
  327.0 4.0 convolution_convert_fusion
  331.3 52.4 %all_to_all.15 = bf16[8,512,384]{1,2,0:T(8,128)(2,1)S(1)} all-to-all(bf16[8,512,384]{1,2,0:T(8,128)(2,1)S(1)} %bitcast.184), channel_id=1, replica_groups=mesh['ctx'=8,'tp'=16] {'ctx'}, dimensions={0} | all-to-all | bytes 6291456 | tf_op jit(solution)/shard_map/all_to_all | solution.py:56
  386.0 27.9 %reduce-scatter.2.cloned.1.call-done = bf16[32,4096]{1,0:T(8,128)(2,1)} async-done(((bf16[512,4096]{1,0:T(8,128)(2,1)}), bf16[32,4096]{1,0:T(8,128)(2,1)}) %reduce-scatter.2.cloned.1.call-update) | async-done | bytes 262160 | tf_op jit(solution)/shard_map/reduce_scatter | solution.py:205
  (112 shorter events, 28.7 us)
Async XLA Ops:
  7.2 3.4 copy-start
  7.2 77.0 %all-gather.3.cloned.1.call-start = ((), (), s32[]{:S(2)}) async-start(), calls=%async_computation.4 | async-start | bytes 3538944 | tf_op jit(solution)/shard_map/all_gather | solution.py:15
  9.1 132.1 %all-gather.5.cloned.1.call-start = ((), (), s32[]{:S(2)}) async-start(), calls=%async_computation.5 | async-start | bytes 4456448 | tf_op jit(solution)/shard_map/all_gather | solution.py:138
  10.5 23.1 %copy-start.13 = (s32[4096]{0:T(1024)S(1)}, s32[4096]{0:T(1024)}, u32[]{:S(2)}) copy-start(s32[4096]{0:T(1024)} %param.12) | copy-start | bytes 49156
  145.2 4.1 collective-permute-start
  149.2 1.3 copy-start.4
  149.2 1.5 copy-start.6
  152.2 4.5 %copy-start.14 = (bf16[512,256]{1,0:T(8,128)(2,1)S(1)}, bf16[512,256]{1,0:T(8,128)(2,1)}, u32[]{:S(2)}) copy-start(bf16[512,256]{1,0:T(8,128)(2,1)} %param.9) | copy-start | bytes 786436
  152.2 31.8 %all-to-all-start = ((bf16[8,512,256]{1,2,0:T(8,128)(2,1)}), bf16[8,512,256]{1,2,0:T(8,128)(2,1)S(1)}, u32[]{:S(2)}, u32[]{:S(2)}) async-start(bf16[8,512,256]{1,2,0:T(8,128)(2,1)} %broadcast_in_dim.33), calls=%async_computation | async-start | bytes 4194304 | tf_op jit(solution)/shard_map/all_to_all | solution.py:34
  163.5 3.9 copy-start.12
  166.5 19.9 %copy-start.9 = (f32[512,128]{1,0:T(8,128)}, f32[512,128]{1,0:T(8,128)S(1)}, u32[]{:S(2)}) copy-start(f32[512,128]{1,0:T(8,128)S(1)} %copy.70) | copy-start | bytes 786436
  195.1 4.5 %copy-start.3 = (f32[2,128,4096]{2,1,0:T(8,128)S(1)}, f32[2,128,4096]{2,1,0:T(8,128)}, u32[]{:S(2)}) copy-start(f32[2,128,4096]{2,1,0:T(8,128)} %get-tuple-element.291) | copy-start | bytes 12582916 | tf_op jit(solution)/shard_map/while
  201.6 4.0 copy-start.2
  215.7 4.5 %copy-start.3 = (f32[2,128,4096]{2,1,0:T(8,128)S(1)}, f32[2,128,4096]{2,1,0:T(8,128)}, u32[]{:S(2)}) copy-start(f32[2,128,4096]{2,1,0:T(8,128)} %get-tuple-element.291) | copy-start | bytes 12582916 | tf_op jit(solution)/shard_map/while
  222.3 4.6 %copy-start.2 = (bf16[2,128,4096]{2,1,0:T(8,128)(2,1)S(1)}, bf16[2,128,4096]{2,1,0:T(8,128)(2,1)}, u32[]{:S(2)}) copy-start(bf16[2,128,4096]{2,1,0:T(8,128)(2,1)} %fusion.121) | copy-start | bytes 6291460 | tf_op jit(solution)/shard_map/while
  238.6 4.5 %copy-start.3 = (f32[2,128,4096]{2,1,0:T(8,128)S(1)}, f32[2,128,4096]{2,1,0:T(8,128)}, u32[]{:S(2)}) copy-start(f32[2,128,4096]{2,1,0:T(8,128)} %get-tuple-element.291) | copy-start | bytes 12582916 | tf_op jit(solution)/shard_map/while
  245.2 4.6 %copy-start.2 = (bf16[2,128,4096]{2,1,0:T(8,128)(2,1)S(1)}, bf16[2,128,4096]{2,1,0:T(8,128)(2,1)}, u32[]{:S(2)}) copy-start(bf16[2,128,4096]{2,1,0:T(8,128)(2,1)} %fusion.121) | copy-start | bytes 6291460 | tf_op jit(solution)/shard_map/while
  261.5 4.5 %copy-start.3 = (f32[2,128,4096]{2,1,0:T(8,128)S(1)}, f32[2,128,4096]{2,1,0:T(8,128)}, u32[]{:S(2)}) copy-start(f32[2,128,4096]{2,1,0:T(8,128)} %get-tuple-element.291) | copy-start | bytes 12582916 | tf_op jit(solution)/shard_map/while
  268.1 4.6 %copy-start.2 = (bf16[2,128,4096]{2,1,0:T(8,128)(2,1)S(1)}, bf16[2,128,4096]{2,1,0:T(8,128)(2,1)}, u32[]{:S(2)}) copy-start(bf16[2,128,4096]{2,1,0:T(8,128)(2,1)} %fusion.121) | copy-start | bytes 6291460 | tf_op jit(solution)/shard_map/while
  279.0 2.0 copy-start.5
  281.2 1.2 copy-start.7
  284.2 1.9 copy-start.8
  288.7 4.0 copy-start.11
  288.7 30.2 %all-to-all-start.1 = ((bf16[8,512,256]{1,2,0:T(8,128)(2,1)}), bf16[8,512,256]{1,2,0:T(8,128)(2,1)S(1)}, u32[]{:S(2)}, u32[]{:S(2)}) async-start(bf16[8,512,256]{1,2,0:T(8,128)(2,1)} %copy.84), calls=%async_computation.1 | async-start | bytes 4194304 | tf_op jit(solution)/shard_map/all_to_all | solution.py:56
  292.4 1.0 copy-start.10
  292.4 121.5 %reduce-scatter.2.cloned.1.call-start = ((), (), s32[]{:S(2)}) async-start(), calls=%async_computation.6 | async-start | bytes 4456448 | tf_op jit(solution)/shard_map/reduce_scatter | solution.py:205
  319.2 3.0 collective-permute-start.1
  383.6 30.3 %copy-start.1 = (s32[4096]{0:T(1024)S(1)}, s32[4096]{0:T(1024)}, u32[]{:S(2)}) copy-start(s32[4096]{0:T(1024)} %param.13) | copy-start | bytes 49156
Sparse Core Ops, SparseCore 0:
  10.2 73.9 all-gather.2
  86.7 54.4 all-gather.4
  327.0 86.9 reduce-scatter.1
where the time goes:
time: 422 us; the launch traced here: 420 us
  waiting for transfers between devices  174 us (41%)
  matrix products  92 us (22%)
  blocking collectives  52.4 us (12%)
  local copies, waits for them, and re-layouts  52.2 us (12%)
  other arithmetic  26.7 us (6%)
  between operations  14.2 us (3%)
  starting transfers between devices  8.92 us (2%)
    all_gather x1, waiting for transfers between devices, shards(): gathered = lax.all_gather(tokens, 'tp', axis=0, tiled=True)  57 us
    all_to_all x1, blocking collectives, summed_on_arrival(): blocks = lax.all_to_all(cut_along(x, dim, count), axis, 0, 0, tiled=True)  52.4 us
    all_gather x1, waiting for transfers between devices, side_by_side(): lax.all_gather(both, axis, axis=dim, tiled=True)  50.6 us
    reduce_scatter x1, waiting for transfers between devices, shards(): lax.psum_scatter((part_query + part_keyval).astype(jnp.bfloat16), 'tp', s...  27.9 us
    all_to_all x1, waiting for transfers between devices, summed_on_arrival(): blocks = lax.all_to_all(cut_along(x, dim, count), axis, 0, 0, tiled=True)  24.9 us
    gather x1, local copies, waits for them, and re-layouts, shards(): doc_all = jnp.take(documents, positions)  23 us
    sub x4, matrix products, advance(): exponent = jnp.exp(scores - row_peak)  19.7 us
    dot_general x4, matrix products, advance(): jnp.einsum('hqk,qhd->kd', score_grad, query_block, preferred_element_type...  17.7 us
  transfers between devices with their start and end apart: 7, of which 5 were waited for; matrix products, arithmetic and copies ran while one was open for 13% of the time, Pallas kernels for 0%

commit v1 on v0

--- a/solution.py
+++ b/solution.py
@@ -1,6 +1,8 @@
 import jax
 import jax.numpy as jnp
 from jax import lax
+from jax.experimental import pallas as pl
+from jax.experimental.pallas import tpu as pltpu
 from jax.sharding import PartitionSpec as P
 
 KEY_VALUE_HEADS = 8
@@ -79,55 +81,122 @@
     return gradient * cosine[:, None, :] + turned
 
 
-def attend(
-    query_rows, grad_out, keys_all, values_all, query_pos, query_doc, key_pos, key_doc, scaling
-):
+def attend_kernel(pos_ref, doc_ref, q_ref, up_ref, k_ref, v_ref, cos_ref, sin_ref, qb_ref, dkv_ref,
+                  score_sc, grad_sc, q2_sc, up2_sc, dq_sc, dk_sc, dv_sc, where_sm):
     f32 = jnp.float32
-    tok_rows, head_count, head_width = query_rows.shape
-    block_rows = min(tok_rows, 128)
-    block_count = tok_rows // block_rows
-    seq_len = keys_all.shape[0]
-
-    def advance(totals, inputs):
-        key_total, value_total = totals
-        query_block, grad_block, pos_block, doc_block = inputs
-        scores = (
-            jnp.einsum("qhd,kd->hqk", query_block, keys_all, preferred_element_type=f32) * scaling
-        )
-        visible = (key_pos[None, :] <= pos_block[:, None]) & (
-            key_doc[None, :] == doc_block[:, None]
-        )
-        scores = jnp.where(visible[None], scores, -1e30)
-        row_peak = jnp.max(scores, axis=-1, keepdims=True)
-        exponent = jnp.exp(scores - row_peak)
-        probs = exponent / jnp.sum(exponent, axis=-1, keepdims=True)
-        probs_half = probs.astype(jnp.bfloat16)
-        output = jnp.einsum("hqk,kd->qhd", probs_half, values_all, preferred_element_type=f32)
-        deltas = jnp.sum(grad_block.astype(f32) * output, axis=-1)
-        prob_grad = jnp.einsum("qhd,kd->hqk", grad_block, values_all, preferred_element_type=f32)
-        score_grad = (probs * (prob_grad - deltas.T[:, :, None])).astype(jnp.bfloat16)
-        dquery = (
-            jnp.einsum("hqk,kd->qhd", score_grad, keys_all, preferred_element_type=f32) * scaling
-        )
-        key_total = (
-            key_total
-            + jnp.einsum("hqk,qhd->kd", score_grad, query_block, preferred_element_type=f32)
-            * scaling
-        )
-        value_total = value_total + jnp.einsum(
-            "hqk,qhd->kd", probs_half, grad_block, preferred_element_type=f32
-        )
-        return ((key_total, value_total), dquery)
-
-    blank_keys = jnp.zeros((seq_len, head_width), f32)
-    inputs = (
-        query_rows.reshape(block_count, block_rows, head_count, head_width),
-        grad_out.reshape(block_count, block_rows, head_count, head_width),
-        query_pos.reshape(block_count, block_rows),
-        query_doc.reshape(block_count, block_rows),
-    )
-    (key_total, value_total), dquery = lax.scan(advance, (blank_keys, blank_keys), inputs)
-    return (dquery.reshape(tok_rows, head_count, head_width), key_total, value_total)
+    bf16 = jnp.bfloat16
+    run = 256
+    rows = 2 * run
+    scaling = HEAD_DIMENSION ** (-0.5)
+    log2e = 1.4426950408889634
+    nt = (((1,), (1,)), ((), ()))
+    tn = (((0,), (0,)), ((), ()))
+    nn = (((1,), (0,)), ((), ()))
+    ctx = lax.axis_index("ctx")
+
+    for s in range(16):
+        where_sm[lax.shift_right_logical(pos_ref[s * run], 8)] = s
+    doc = doc_ref[...]
+    starts = [jnp.sum(jnp.where(doc < d, 1.0, 0.0)).astype(jnp.int32) for d in (1, 2, 3)]
+    dk_sc[...] = jnp.zeros_like(dk_sc)
+    dv_sc[...] = jnp.zeros_like(dv_sc)
+
+    def one_run(t, carry):
+        base = pos_ref[(ctx * 2 + t) * run]
+        mine = pl.ds(pl.multiple_of(t * run, run), run)
+        first = jnp.int32(0)
+        for start in starts:
+            first = jnp.where(start <= base, jnp.maximum(first, start), first)
+        low = lax.shift_right_logical(first, 8)
+        high = lax.shift_right_logical(base, 8) + 1
+        q_pos = base + (lax.broadcasted_iota(jnp.int32, (1, rows), 1) & (run - 1))
+        q_low = jnp.zeros_like(q_pos)
+        for start in starts:
+            q_low = jnp.where(start <= q_pos, jnp.maximum(q_low, start), q_low)
+        for h in range(2):
+            q2_sc[h * run:(h + 1) * run, :] = q_ref[mine, h * 128:(h + 1) * 128]
+            up2_sc[h * run:(h + 1) * run, :] = up_ref[mine, h * 128:(h + 1) * 128]
+
+        def keys_at(j):
+            return pl.ds(pl.multiple_of(where_sm[j] * run, run), run)
+
+        def scan_scores(j, peak):
+            at = keys_at(j)
+            score = lax.dot_general(k_ref[at, :], q2_sc[...], nt, preferred_element_type=f32)
+            k_pos = j * run + lax.broadcasted_iota(jnp.int32, (run, 1), 0)
+            score = jnp.where((k_pos >= q_low) & (k_pos <= q_pos), score, -1e30)
+            score_sc[j - low] = score
+            grad_sc[j - low] = lax.dot_general(v_ref[at, :], up2_sc[...], nt, preferred_element_type=f32)
+            return jnp.maximum(peak, jnp.max(score, axis=0, keepdims=True))
+
+        peak = lax.fori_loop(low, high, scan_scores, jnp.full((1, rows), -1e30, f32))
+
+        def scan_sums(j, sums):
+            total, delta = sums
+            exponent = jnp.exp2((score_sc[j - low] - peak) * (scaling * log2e))
+            score_sc[j - low] = exponent
+            total = total + jnp.sum(exponent, axis=0, keepdims=True)
+            delta = delta + jnp.sum(exponent * grad_sc[j - low], axis=0, keepdims=True)
+            return total, delta
+
+        zero = jnp.zeros((1, rows), f32)
+        total, delta = lax.fori_loop(low, high, scan_sums, (zero, zero))
+        inverse = 1.0 / total
+        delta = delta * inverse
+        dq_sc[...] = jnp.zeros_like(dq_sc)
+
+        def scan_grads(j, c):
+            at = keys_at(j)
+            probs = score_sc[j - low] * inverse
+            score_grad = (probs * (grad_sc[j - low] - delta)).astype(bf16)
+            dv_sc[at, :] += lax.dot_general(probs.astype(bf16), up2_sc[...], nn, preferred_element_type=f32)
+            dk_sc[at, :] += lax.dot_general(score_grad, q2_sc[...], nn, preferred_element_type=f32)
+            dq_sc[...] += lax.dot_general(k_ref[at, :], score_grad, tn, preferred_element_type=f32)
+            return c
+
+        lax.fori_loop(low, high, scan_grads, 0)
+        cosine, sine = cos_ref[mine, :], sin_ref[mine, :]
+        for h in range(2):
+            grad = dq_sc[:, h * run:(h + 1) * run].T * scaling
+            back = grad * cosine - pltpu.roll(grad, 64, 1) * sine
+            qb_ref[mine, h * 128:(h + 1) * 128] = back.astype(bf16)
+        return carry
+
+    lax.fori_loop(0, 2, one_run, 0)
+
+    def put_out(i, carry):
+        at = pl.ds(pl.multiple_of(i * run, run), run)
+        dkv_ref[0, at, :] = (dk_sc[at, :] * scaling).astype(bf16)
+        dkv_ref[1, at, :] = dv_sc[at, :].astype(bf16)
+        return carry
+
+    lax.fori_loop(0, 16, put_out, 0)
+
+
+def attend(positions, documents, query, upstream, keys, values, cosine, sine):
+    f32 = jnp.float32
+    vmem = pl.BlockSpec(memory_space=pltpu.VMEM)
+    return pl.pallas_call(
+        attend_kernel,
+        out_shape=(
+            jax.ShapeDtypeStruct((512, 256), jnp.bfloat16),
+            jax.ShapeDtypeStruct((2, 4096, 128), jnp.bfloat16),
+        ),
+        in_specs=[pl.BlockSpec(memory_space=pltpu.SMEM)] + [vmem] * 7,
+        out_specs=(vmem, vmem),
+        scratch_shapes=[
+            pltpu.VMEM((16, 256, 512), f32),
+            pltpu.VMEM((16, 256, 512), f32),
+            pltpu.VMEM((512, 128), jnp.bfloat16),
+            pltpu.VMEM((512, 128), jnp.bfloat16),
+            pltpu.VMEM((128, 512), f32),
+            pltpu.VMEM((4096, 128), f32),
+            pltpu.VMEM((4096, 128), f32),
+            pltpu.SMEM((16,), jnp.int32),
+        ],
+        compiler_params=pltpu.CompilerParams(vmem_limit_bytes=50 * 1024 * 1024),
+        name="attend",
+    )(positions, documents.reshape(32, 128), query, upstream, keys, values, cosine, sine)
 
 
 def shards(tokens, upstream, w_query, w_keyval, positions, documents):
@@ -140,11 +209,8 @@
     query_cols = w_query.shape[1]
     head_count = query_cols // HEAD_DIMENSION
     pairing_flags = (tensor_split_count // KEY_VALUE_HEADS).bit_length() - 1
-    doc_all = jnp.take(documents, positions)
     cosine_all, sine_all = rotation_tables(positions)
     row_offset = ctx_rank * tok_rows
-    my_pos = lax.dynamic_slice_in_dim(positions, row_offset, tok_rows, 0)
-    my_doc = lax.dynamic_slice_in_dim(doc_all, row_offset, tok_rows, 0)
     my_cos = lax.dynamic_slice_in_dim(cosine_all, row_offset, tok_rows, 0)
     my_sin = lax.dynamic_slice_in_dim(sine_all, row_offset, tok_rows, 0)
     query_full, keyval_full = side_by_side((w_query, w_keyval), "ctx", 0, 1)
@@ -167,22 +233,19 @@
     )
     local_kv = jnp.concatenate([key_rot, head_kv[:, HEAD_DIMENSION:]], axis=1)
     key_value = gathered_copies(local_kv, "ctx", 0)
-    grad_query, grad_key, grad_value = attend(
-        query_rot,
-        upstream.reshape(tok_rows, head_count, HEAD_DIMENSION),
+    sign = jnp.where(jnp.arange(HEAD_DIMENSION) < HEAD_DIMENSION // 2, -1.0, 1.0)
+    query_back, key_grads = attend(
+        positions,
+        documents,
+        query_rot.reshape(tok_rows, query_cols),
+        upstream,
         key_value[:, :HEAD_DIMENSION],
         key_value[:, HEAD_DIMENSION:],
-        my_pos,
-        my_doc,
-        positions,
-        doc_all,
-        HEAD_DIMENSION ** (-0.5),
-    )
-    query_back = (
-        rotate_back(grad_query, my_cos, my_sin).astype(jnp.bfloat16).reshape(tok_rows, query_cols)
-    )
-    key_backward = rotate_back(grad_key[:, None, :], cosine_all, sine_all)[:, 0]
-    key_terms = jnp.concatenate([key_backward, grad_value], axis=1)
+        my_cos,
+        my_sin * sign,
+    )
+    key_backward = rotate_back(key_grads[0].astype(f32)[:, None, :], cosine_all, sine_all)[:, 0]
+    key_terms = jnp.concatenate([key_backward, key_grads[1].astype(f32)], axis=1)
     head_grad = summed_on_arrival(key_terms.astype(jnp.bfloat16), "ctx", 0)
     for bit_index in reversed(range(pairing_flags)):
         half_width = head_grad.shape[1] // 2

time: 422 us -> 328 us (0.78)
  matrix products: 92 us -> 17.4 us
  local copies, waits for them, and re-layouts: 52.2 us -> 8.42 us
  blocking collectives: 52.4 us -> 86.9 us
  waiting for transfers between devices: 174 us -> 162 us
  Pallas kernels: 0 us -> 7.04 us
    dot_general x20 -> x0, matrix products: 52.8 us -> none  [the longest x4 17.7 us: advance(): jnp.einsum('hqk,qhd->kd', score_grad, query_block, preferred_element_type...]
    all_to_all x1 -> x2, blocking collectives: 52.4 us -> 86.9 us  [summed_on_arrival(): blocks = lax.all_to_all(cut_along(x, dim, count), axis, 0, 0, tiled=True)]
    all_to_all x1 -> x0, waiting for transfers between devices: 24.9 us -> none  [summed_on_arrival(): blocks = lax.all_to_all(cut_along(x, dim, count), axis, 0, 0, tiled=True)]
    gather x1 -> x0, local copies, waits for them, and re-layouts: 23 us -> none  [shards(): doc_all = jnp.take(documents, positions)]
    sub x4 -> x0, matrix products: 19.7 us -> none  [advance(): exponent = jnp.exp(scores - row_peak)]
    all_gather x1, waiting for transfers between devices: 50.6 us -> 64.3 us  [side_by_side(): lax.all_gather(both, axis, axis=dim, tiled=True)]
    concatenate x2, other arithmetic: 0.4 us -> 9.57 us  [the longest x1 9.32 us: rotation_tables(): sine = jnp.concatenate([jnp.sin(angles), jnp.sin(angles)], axis=1)]
    convert_element_type x5 -> x2, other arithmetic: 11.4 us -> 2.62 us  [the longest x1 1.89 us: shards(): key_grads[0].astype(f32)[:, None, :]]
  transfers between devices with their start and end apart: 7 -> 6, of which waited for: 5 -> 5; matrix products, arithmetic and copies ran while one was open for 13% -> 10% of each run, Pallas kernels for 0% -> 0%
where the time goes in v1:
time: 328 us
  waiting for transfers between devices  162 us (49%)
  blocking collectives  86.9 us (26%)
  other arithmetic  27.5 us (8%)
  matrix products  17.4 us (5%)
  between operations  14 us (4%)
  local copies, waits for them, and re-layouts  8.42 us (3%)
  Pallas kernels  7.04 us (2%)
  starting transfers between devices  5.28 us (2%)
    all_to_all x2, blocking collectives, summed_on_arrival(): blocks = lax.all_to_all(cut_along(x, dim, count), axis, 0, 0, tiled=True)  86.9 us
    all_gather x1, waiting for transfers between devices, side_by_side(): lax.all_gather(both, axis, axis=dim, tiled=True)  64.3 us
    all_gather x1, waiting for transfers between devices, shards(): gathered = lax.all_gather(tokens, 'tp', axis=0, tiled=True)  57 us
    reduce_scatter x1, waiting for transfers between devices, shards(): lax.psum_scatter((part_query + part_keyval).astype(jnp.bfloat16), 'tp', s...  27.5 us
    all_to_all x1, waiting for transfers between devices, copy_for_each(): lax.all_to_all(jnp.broadcast_to(x[None], (count, *x.shape)), axis, 0, 0,...  11.5 us
    concatenate x1, other arithmetic, rotation_tables(): sine = jnp.concatenate([jnp.sin(angles), jnp.sin(angles)], axis=1)  9.32 us
    cos x1, other arithmetic, rotation_tables(): cosine = jnp.concatenate([jnp.cos(angles), jnp.cos(angles)], axis=1)  8.11 us
    pallas_call x1, Pallas kernels, attend(): pl.pallas_call(attend_kernel, out_shape=(jax.ShapeDtypeStruct((512, 256),...  7.04 us
  transfers between devices with their start and end apart: 6, of which 5 were waited for; matrix products, arithmetic and copies ran while one was open for 10% of the time, Pallas kernels for 0%

profile of v1, /device:TPU:0, one launch (start us, length us, event | category | flops | bytes accessed | tf_op | source)
XLA Modules:
  0.0 328.4 jit_solution(2366973228101368642)
XLA Ops:
  7.2 0.0 all-gather.3.cloned.1.call-start
  7.2 1.8 pad_maximum_fusion.1
  9.0 0.0 all-gather.5.cloned.1.call-start
  9.1 0.7 all-gather.5.cloned.1.call-update
  9.8 0.7 convert_element_type.74
  10.6 9.3 %fusion.12 = (f32[4096,1,64]{2,0,1:T(8,128)S(1)}, f32[4096,64]{1,0:T(8,128)}, f32[4096,64]{1,0:T(8,128)}) fusion(f32[64]{0:T(128)S(1)} %negate_power_fusion, f32[4096]{0:T(1024)S(1)} %convert_element_type.74), kind=kLoop, calls=%fused_computation.28 | loop fusion | flops 262144 | bytes 3162368 | tf_op jit(solution)/shard_map/concatenate | solution.py:67
  19.9 64.3 %all-gather.3.cloned.1.call-done = bf16[4096,384]{1,0:T(8,128)(2,1)} async-done(((bf16[512,384]{1,0:T(8,128)(2,1)}), bf16[4096,384]{1,0:T(8,128)(2,1)}) %all-gather.3.cloned.1.call-update) | async-done | bytes 3145744 | tf_op jit(solution)/shard_map/all_gather | solution.py:17
  84.2 57.0 %all-gather.5.cloned.1.call-done = bf16[512,4096]{1,0:T(8,128)(2,1)} async-done(((bf16[32,4096]{1,0:T(8,128)(2,1)}), bf16[512,4096]{1,0:T(8,128)(2,1)}) %all-gather.5.cloned.1.call-update) | async-done | bytes 4194320 | tf_op jit(solution)/shard_map/all_gather | solution.py:207
  141.1 3.9 %fusion.9 = bf16[512,128]{1,0:T(8,128)(2,1)S(1)} fusion(bf16[512,4096]{1,0:T(8,128)(2,1)} %all-gather.5.cloned.1.call-done, bf16[4096,384]{1,0:T(8,128)(2,1)} %all-gather.3.cloned.1.call-done), kind=kOutput, calls=%fused_computation.24 | convolution fusion | flops 536936448 | bytes 5373952 | tf_op jit(solution)/shard_map/dot_general | solution.py:218
  145.0 0.3 collective-permute-start
  145.4 0.1 broadcast_multiply_fusion
  145.5 0.9 collective-permute-done
  146.4 0.1 maximum_select_fusion
  146.6 0.1 fusion.21
  146.7 0.2 copy-done.3
  146.9 0.2 fusion.18
  147.2 1.6 broadcast_in_dim.8
  148.8 4.3 %all-to-all-start = ((bf16[8,512,256]{2,1,0:T(8,128)(2,1)}), bf16[8,512,256]{2,1,0:T(8,128)(2,1)}, u32[]{:S(2)}, u32[]{:S(2)}) async-start(bf16[8,512,256]{2,1,0:T(8,128)(2,1)} %broadcast_in_dim.8), calls=%async_computation | async-start | bytes 4194304 | tf_op jit(solution)/shard_map/all_to_all | solution.py:36
  153.1 0.2 reduce-scatter.2.cloned.1.call-start
  153.4 8.1 %multiply_cosine_fusion.1 = f32[8,512,64]{2,1,0:T(8,128)} fusion(f32[64]{0:T(128)S(1)} %negate_power_fusion, f32[8,512]{1,0:T(8,128)S(1)} %mul.108), kind=kLoop, calls=%fused_computation.17 | loop fusion | flops 262144 | bytes 1065216 | tf_op jit(solution)/shard_map/cos | solution.py:66
  161.5 4.9 %fusion.6 = f32[512,256]{1,0:T(8,128)} fusion(bf16[512,4096]{1,0:T(8,128)(2,1)} %all-gather.5.cloned.1.call-done, bf16[4096,384]{1,0:T(8,128)(2,1)} %all-gather.3.cloned.1.call-done), kind=kOutput, calls=%fused_computation.22 | convolution fusion | flops 1073741824 | bytes 6815744 | tf_op jit(solution)/shard_map/dot_general | solution.py:217
  166.4 1.3 reshape.167
  167.7 0.6 slice_negate_fusion.1
  168.3 0.6 maximum_multiply_fusion.2
  169.0 0.2 mul.98
  169.2 0.1 fusion.13.q_ref
  169.3 11.5 %all-to-all-done = bf16[8,512,256]{2,1,0:T(8,128)(2,1)} async-done(((bf16[8,512,256]{2,1,0:T(8,128)(2,1)}), bf16[8,512,256]{2,1,0:T(8,128)(2,1)}, u32[]{:S(2)}, u32[]{:S(2)}) %all-to-all-start) | async-done | bytes 2097184 | tf_op jit(solution)/shard_map/all_to_all | solution.py:36
  180.8 1.7 fusion.26
  182.6 7.0 %attend.1 = (bf16[512,256]{1,0:T(8,128)(2,1)S(1)}, bf16[2,4096,128]{2,1,0:T(8,128)(2,1)}) custom-call(s32[4096]{0:T(1024)S(1)} %copy-done.1, s32[32,128]{1,0:T(8,128)S(1)} %bitcast.40, bf16[512,256]{1,0:T(8,128)(2,1)S(1)} %fusion.13.q_ref, bf16[512,256]{1,0:T(8,128)(2,1)S(1)} %copy-done, bf16[4096,128]{1,0:T(8,128)(2,1)S(1)} %get-tuple-element.19.k_ref, ...), custom_call_target="tpu_custom_call" | custom-call | tf_op jit(solution)/shard_map/attend/pallas_call | solution.py:179
  189.6 1.9 slice_convert_fusion
  191.5 0.3 copy-done.6
  191.8 0.7 maximum_multiply_fusion.1
  192.5 0.7 fusion.25
  193.2 0.9 copy-done.5
  194.1 1.1 fusion.1
  195.3 0.3 pad_maximum_fusion
  195.5 34.1 %all_to_all.15 = bf16[8,512,256]{2,1,0:T(8,128)(2,1)S(1)} all-to-all(bf16[8,512,256]{2,1,0:T(8,128)(2,1)S(1)} %pad_maximum_fusion), channel_id=1, replica_groups=mesh['ctx'=8,'tp'=16] {'ctx'}, dimensions={0} | all-to-all | bytes 4194304 | tf_op jit(solution)/shard_map/all_to_all | solution.py:58
  229.6 0.3 convert_reduce_fusion.1
  230.0 0.3 collective-permute-start.1
  230.3 1.3 fusion.2
  231.7 3.3 %add_convert_fusion = bf16[512,4096]{1,0:T(8,128)(2,1)} fusion(f32[512,4096]{1,0:T(8,128)S(1)} %fusion.2, bf16[512,128]{1,0:T(8,128)(2,1)S(1)} %add_convert_fusion.1, bf16[4096,384]{1,0:T(8,128)(2,1)S(1)} %copy-done.7), kind=kOutput, calls=%fused_computation | convolution fusion | flops 541065216 | bytes 13762560 | tf_op jit(solution)/shard_map/dot_general | solution.py:265
  235.0 4.0 %convolution_convert_fusion = bf16[384,4096]{1,0:T(8,128)(2,1)S(1)} fusion(bf16[512,4096]{1,0:T(8,128)(2,1)} %all-gather.5.cloned.1.call-done, bf16[512,128]{1,0:T(8,128)(2,1)S(1)} %add_convert_fusion.1, bf16[512,256]{1,0:T(8,128)(2,1)S(1)} %get-tuple-element.5), kind=kOutput, calls=%fused_computation.2 | convolution fusion | flops 1612972032 | bytes 7733248 | tf_op jit(solution)/shard_map/dot_general | solution.py:272
  239.0 0.3 copy.28
  239.3 52.8 %all_to_all.16 = bf16[8,512,384]{1,2,0:T(8,128)(2,1)S(1)} all-to-all(bf16[8,512,384]{1,2,0:T(8,128)(2,1)S(1)} %bitcast.41), channel_id=1, replica_groups=mesh['ctx'=8,'tp'=16] {'ctx'}, dimensions={0} | all-to-all | bytes 6291456 | tf_op jit(solution)/shard_map/all_to_all | solution.py:58
  292.1 0.5 convert_reduce_fusion
  292.6 1.0 copy.15
  293.6 0.8 copy.16
  294.4 27.5 %reduce-scatter.2.cloned.1.call-done = bf16[32,4096]{1,0:T(8,128)(2,1)} async-done(((bf16[512,4096]{1,0:T(8,128)(2,1)}), bf16[32,4096]{1,0:T(8,128)(2,1)}) %reduce-scatter.2.cloned.1.call-update) | async-done | bytes 262160 | tf_op jit(solution)/shard_map/reduce_scatter | solution.py:268
  (27 shorter events, 0.3 us)
Async XLA Ops:
  7.2 77.0 %all-gather.3.cloned.1.call-start = ((), (), s32[]{:S(2)}) async-start(), calls=%async_computation.4 | async-start | bytes 3538944 | tf_op jit(solution)/shard_map/all_gather | solution.py:17
  9.0 132.1 %all-gather.5.cloned.1.call-start = ((), (), s32[]{:S(2)}) async-start(), calls=%async_computation.5 | async-start | bytes 4456448 | tf_op jit(solution)/shard_map/all_gather | solution.py:207
  141.1 4.2 %copy-start.4 = (f32[4096,64]{1,0:T(8,128)S(1)}, f32[4096,64]{1,0:T(8,128)}, u32[]{:S(2)}) copy-start(f32[4096,64]{1,0:T(8,128)} %get-tuple-element.27) | copy-start | bytes 3145732
  145.0 1.4 collective-permute-start
  145.4 1.6 copy-start.3
  148.8 32.1 %all-to-all-start = ((bf16[8,512,256]{2,1,0:T(8,128)(2,1)}), bf16[8,512,256]{2,1,0:T(8,128)(2,1)}, u32[]{:S(2)}, u32[]{:S(2)}) async-start(bf16[8,512,256]{2,1,0:T(8,128)(2,1)} %broadcast_in_dim.8), calls=%async_computation | async-start | bytes 4194304 | tf_op jit(solution)/shard_map/all_to_all | solution.py:36
  153.1 168.8 %reduce-scatter.2.cloned.1.call-start = ((), (), s32[]{:S(2)}) async-start(), calls=%async_computation.6 | async-start | bytes 4456448 | tf_op jit(solution)/shard_map/reduce_scatter | solution.py:268
  167.7 1.5 copy-start.8
  180.8 1.7 copy-start
  180.8 1.7 copy-start.1
  180.8 1.7 copy-start.2
  189.6 2.2 copy-start.6
  192.5 1.6 copy-start.5
  195.5 34.8 %copy-start.7 = (bf16[4096,384]{1,0:T(8,128)(2,1)S(1)}, bf16[4096,384]{1,0:T(8,128)(2,1)}, u32[]{:S(2)}) copy-start(bf16[4096,384]{1,0:T(8,128)(2,1)} %all-gather.3.cloned.1.call-done) | copy-start | bytes 9437188
  230.0 1.6 collective-permute-start.1
Sparse Core Ops, SparseCore 0:
  10.2 73.9 all-gather.2
  86.6 54.4 all-gather.4
  235.1 86.7 reduce-scatter.1

commit v2 on v1

v2 whole, which is shorter than its diff:
```python
import jax
import jax.numpy as jnp
from jax import lax
from jax.experimental import pallas as pl
from jax.experimental.pallas import tpu as pltpu
from jax.sharding import PartitionSpec as P

HEAD_DIMENSION = 128


rope_base = 500000.0


def rotation_tables(positions):
    half_width = HEAD_DIMENSION // 2
    frequency = rope_base ** (-(jnp.arange(half_width, dtype=jnp.float32) * 2.0 / HEAD_DIMENSION))
    angles = positions.astype(jnp.float32)[:, None] * frequency[None, :]
    cosine = jnp.concatenate([jnp.cos(angles), jnp.cos(angles)], axis=1)
    sine = jnp.concatenate([jnp.sin(angles), jnp.sin(angles)], axis=1)
    return (cosine, sine)


def attend_kernel(pos_ref, doc_ref, q_ref, up_ref, kv_ref, cos_ref, sin_ref, qb_ref, dkv_ref,
                  score_sc, grad_sc, q2_sc, up2_sc, dq_sc, dk_sc, dv_sc, where_sm):
    f32 = jnp.float32
    bf16 = jnp.bfloat16
    run = 256
    rows = 2 * run
    scaling = HEAD_DIMENSION ** (-0.5)
    log2e = 1.4426950408889634
    nt = (((1,), (1,)), ((), ()))
    tn = (((0,), (0,)), ((), ()))
    nn = (((1,), (0,)), ((), ()))
    ctx = lax.axis_index("ctx")

    for s in range(16):
        where_sm[lax.shift_right_logical(pos_ref[s * run], 8)] = s
    doc = doc_ref[...]
    starts = [jnp.sum(jnp.where(doc < d, 1.0, 0.0)).astype(jnp.int32) for d in (1, 2, 3)]
    dk_sc[...] = jnp.zeros_like(dk_sc)
    dv_sc[...] = jnp.zeros_like(dv_sc)

    def one_run(t, carry):
        base = pos_ref[(ctx * 2 + t) * run]
        mine = pl.ds(pl.multiple_of(t * run, run), run)
        first = jnp.int32(0)
        for start in starts:
            first = jnp.where(start <= base, jnp.maximum(first, start), first)
        low = lax.shift_right_logical(first, 8)
        high = lax.shift_right_logical(base, 8) + 1
        q_pos = base + (lax.broadcasted_iota(jnp.int32, (1, rows), 1) & (run - 1))
        q_low = jnp.zeros_like(q_pos)
        for start in starts:
            q_low = jnp.where(start <= q_pos, jnp.maximum(q_low, start), q_low)
        for h in range(2):
            q2_sc[h * run:(h + 1) * run, :] = q_ref[mine, h * 128:(h + 1) * 128]
            up2_sc[h * run:(h + 1) * run, :] = up_ref[mine, h * 128:(h + 1) * 128]

        def keys_at(j):
            return pl.ds(pl.multiple_of(where_sm[j] * run, run), run)

        def scan_scores(j, peak):
            at = keys_at(j)
            score = lax.dot_general(kv_ref[0, at, :], q2_sc[...], nt, preferred_element_type=f32)
            k_pos = j * run + lax.broadcasted_iota(jnp.int32, (run, 1), 0)
            score = jnp.where((k_pos >= q_low) & (k_pos <= q_pos), score, -1e30)
            score_sc[j - low] = score
            grad_sc[j - low] = lax.dot_general(kv_ref[1, at, :], up2_sc[...], nt, preferred_element_type=f32)
            return jnp.maximum(peak, jnp.max(score, axis=0, keepdims=True))

        peak = lax.fori_loop(low, high, scan_scores, jnp.full((1, rows), -1e30, f32))

        def scan_sums(j, sums):
            total, delta = sums
            exponent = jnp.exp2((score_sc[j - low] - peak) * (scaling * log2e))
            score_sc[j - low] = exponent
            total = total + jnp.sum(exponent, axis=0, keepdims=True)
            delta = delta + jnp.sum(exponent * grad_sc[j - low], axis=0, keepdims=True)
            return total, delta

        zero = jnp.zeros((1, rows), f32)
        total, delta = lax.fori_loop(low, high, scan_sums, (zero, zero))
        inverse = 1.0 / total
        delta = delta * inverse
        dq_sc[...] = jnp.zeros_like(dq_sc)

        def scan_grads(j, c):
            at = keys_at(j)
            probs = score_sc[j - low] * inverse
            score_grad = (probs * (grad_sc[j - low] - delta)).astype(bf16)
            dv_sc[at, :] += lax.dot_general(probs.astype(bf16), up2_sc[...], nn, preferred_element_type=f32)
            dk_sc[at, :] += lax.dot_general(score_grad, q2_sc[...], nn, preferred_element_type=f32)
            dq_sc[...] += lax.dot_general(kv_ref[0, at, :], score_grad, tn, preferred_element_type=f32)
            return c

        lax.fori_loop(low, high, scan_grads, 0)
        cosine, sine = cos_ref[mine, :], sin_ref[mine, :]
        for h in range(2):
            grad = dq_sc[:, h * run:(h + 1) * run].T * scaling
            back = grad * cosine - pltpu.roll(grad, 64, 1) * sine
            qb_ref[mine, h * 128:(h + 1) * 128] = back.astype(bf16)
        return carry

    lax.fori_loop(0, 2, one_run, 0)

    def put_out(i, carry):
        at = pl.ds(pl.multiple_of(i * run, run), run)
        dkv_ref[0, at, :] = (dk_sc[at, :] * scaling).astype(bf16)
        dkv_ref[1, at, :] = dv_sc[at, :].astype(bf16)
        return carry

    lax.fori_loop(0, 16, put_out, 0)


def attend(positions, documents, query, upstream, key_value, cosine, sine):
    f32 = jnp.float32
    vmem = pl.BlockSpec(memory_space=pltpu.VMEM)
    return pl.pallas_call(
        attend_kernel,
        out_shape=(
            jax.ShapeDtypeStruct((512, 256), jnp.bfloat16),
            jax.ShapeDtypeStruct((2, 4096, 128), jnp.bfloat16),
        ),
        in_specs=[pl.BlockSpec(memory_space=pltpu.SMEM)] + [vmem] * 6,
        out_specs=(vmem, vmem),
        scratch_shapes=[
            pltpu.VMEM((16, 256, 512), f32),
            pltpu.VMEM((16, 256, 512), f32),
            pltpu.VMEM((512, 128), jnp.bfloat16),
            pltpu.VMEM((512, 128), jnp.bfloat16),
            pltpu.VMEM((128, 512), f32),
            pltpu.VMEM((4096, 128), f32),
            pltpu.VMEM((4096, 128), f32),
            pltpu.SMEM((16,), jnp.int32),
        ],
        compiler_params=pltpu.CompilerParams(vmem_limit_bytes=50 * 1024 * 1024),
        name="attend",
    )(positions, documents.reshape(32, 128), query, upstream, key_value.reshape(2, 4096, 128), cosine, sine)


MESH = pl.DeviceIdType.MESH
VMEM_LIMIT = 60 * 1024 * 1024


def places():
    ctx = lax.axis_index("ctx")
    tp = lax.axis_index("tp")
    y, x_lo = ctx // 2, lax.rem(ctx, 2)
    x_hi, z, core = tp // 8, lax.rem(tp // 2, 4), lax.rem(tp, 2)

    def ctx_at(pair, step):
        return lax.rem(y + step + 4, 4) * 2 + (1 - x_lo if pair else x_lo)

    def tp_at(pair, step, other=0):
        side = 1 - x_hi if pair else x_hi
        return side * 8 + lax.rem(z + step + 4, 4) * 2 + (1 - core if other else core)

    ctx_peers = [(ctx_at(1, 0), tp), (ctx_at(0, 1), tp), (ctx_at(0, -1), tp)]
    tp_peers = [(ctx, tp_at(1, 0)), (ctx, tp_at(0, 1)), (ctx, tp_at(0, -1))]
    twin = (ctx, tp_at(0, 0, 1))
    return ctx, tp, core, ctx_at, tp_at, ctx_peers, tp_peers, twin


def meet(peers):
    barrier = pltpu.get_barrier_semaphore()
    for peer in peers:
        pl.semaphore_signal(barrier, inc=1, device_id=peer, device_id_type=MESH)
    pl.semaphore_wait(barrier, len(peers))


def remote(src, dst, send, recv, n, peer):
    return pltpu.make_async_remote_copy(
        src_ref=src, dst_ref=dst, send_sem=send.at[n], recv_sem=recv.at[n],
        device_id=peer, device_id_type=MESH,
    )


class Gather:
    def __init__(self, block, rows, peers, send, recv):
        half = rows // 2

        def part(pair, step, h):
            return block(pair, step).at[pl.ds(h * half, half)]

        pair, after, before = peers
        self.out = [
            (block(0, 0), pair), (block(0, 0), after), (block(0, 0), before),
            (block(1, 0), after), (block(1, 0), before),
            (part(0, -1, 0), after), (part(0, 1, 1), before),
            (part(1, -1, 0), after), (part(1, 1, 1), before),
        ]
        self.into = [
            block(1, 0), block(0, -1), block(0, 1), block(1, -1), block(1, 1),
            part(0, 2, 0), part(0, 2, 1), part(1, 2, 0), part(1, 2, 1),
        ]
        self.sems = (send, recv)

    def start(self, *which):
        for n in which:
            ref, peer = self.out[n]
            remote(ref, ref, *self.sems, n, peer).start()

    def arrived(self, *which):
        for n in which:
            ref = self.into[n]
            remote(ref, ref, *self.sems, n, self.out[n][1]).wait_recv()

    def finish(self):
        for n, (ref, peer) in enumerate(self.out):
            remote(ref, ref, *self.sems, n, peer).wait_send()


class Share:
    order = [(0, 0), (1, 0), (0, -1), (0, 1), (1, -1), (1, 1), (0, 2), (1, 2)]

    def __init__(self, mine, theirs, twin, send, recv):
        self.mine = [mine(*p) for p in self.order]
        self.theirs = [theirs(*p) for p in self.order]
        self.twin = twin
        self.sems = (send, recv)

    def start(self, *which):
        for n in which:
            remote(self.mine[n], self.mine[n], *self.sems, n, self.twin).start()

    def arrived(self):
        for n, ref in enumerate(self.theirs):
            remote(ref, ref, *self.sems, n, self.twin).wait_recv()

    def finish(self):
        for n, ref in enumerate(self.mine):
            remote(ref, ref, *self.sems, n, self.twin).wait_send()


class Reduce:
    def __init__(self, block, rows, peers, halves, wholes, last, send, recv):
        half = rows // 2
        pair, after, before = peers

        def part(p, step, h):
            return block(p, step).at[pl.ds(h * half, half)]

        self.block = block
        self.part = part
        self.halves, self.wholes, self.last = halves, wholes, last
        self.out = [
            (part(1, 2, 0), halves.at[0], after), (part(1, 2, 1), halves.at[1], before),
            (part(0, 2, 0), halves.at[2], after), (part(0, 2, 1), halves.at[3], before),
            (block(1, 1), wholes.at[0], after), (block(1, -1), wholes.at[1], before),
            (block(0, 1), wholes.at[2], after), (block(0, -1), wholes.at[3], before),
            (block(1, 0), last, pair),
        ]
        self.sems = (send, recv)

    def start(self, *which):
        for n in which:
            src, dst, peer = self.out[n]
            remote(src, dst, *self.sems, n, peer).start()

    def arrived(self, *which):
        for n in which:
            src, dst, peer = self.out[n]
            remote(src, dst, *self.sems, n, peer).wait_recv()

    def finish(self):
        for n in range(9):
            src, dst, peer = self.out[n]
            remote(src, dst, *self.sems, n, peer).wait_send()

    def second(self, p):
        n = 0 if p else 2
        for k, (step, h) in enumerate(((1, 0), (-1, 1))):
            self.arrived(n + k)
            add_into(self.part(p, step, h), self.halves.at[n + k])
            self.start(4 + n + k)

    def third(self):
        self.arrived(4, 5)
        add_into(self.block(1, 0), self.wholes.at[0], self.wholes.at[1])
        self.start(8)

    def total(self, at):
        f32 = jnp.float32
        parts = [self.block(0, 0), self.wholes.at[2], self.wholes.at[3], self.last]
        return sum(r[at].astype(f32) for r in parts)


def add_into(dst, *terms):
    rows, cols = dst.shape
    tile = max(16, min(rows, 32768 // cols))

    def one(i, carry):
        at = pl.ds(pl.multiple_of(i * tile, tile), tile)
        total = dst[at, :].astype(jnp.float32)
        for t in terms:
            total = total + t[at, :].astype(jnp.float32)
        dst[at, :] = total.astype(dst.dtype)
        return carry

    lax.fori_loop(0, rows // tile, one, 0)


def chosen(t, values):
    at = values[0]
    for n, v in enumerate(values[1:]):
        at = jnp.where(t == n + 1, v, at)
    return at


def project_kernel(tok_ref, wq_ref, wk_ref, cos_ref, sin_ref, q_ref, kv_ref, tok_out, w_out,
                   tbuf, wbuf, kvbuf, acc, t_send, t_recv, c_send, c_recv, w_send, w_recv,
                   k_send, k_recv, f_send, f_recv, local):
    f32 = jnp.float32
    bf16 = jnp.bfloat16
    ctx, tp, core, ctx_at, tp_at, ctx_peers, tp_peers, twin = places()
    copies = [
        pltpu.make_async_copy(tok_ref, tbuf.at[tp], local.at[0]),
        pltpu.make_async_copy(wq_ref, wbuf.at[ctx, :, pl.ds(0, 256)], local.at[1]),
        pltpu.make_async_copy(wk_ref, wbuf.at[ctx, :, pl.ds(256, 128)], local.at[2]),
    ]
    for c in copies:
        c.start()
    meet(ctx_peers + tp_peers + [twin])
    toks = Gather(lambda p, d: tbuf.at[tp_at(p, d)], 32, tp_peers, t_send, t_recv)
    tshare = Share(lambda p, d: tbuf.at[tp_at(p, d)], lambda p, d: tbuf.at[tp_at(p, d, 1)], twin, c_send, c_recv)
    weights = Gather(lambda p, d: wbuf.at[ctx_at(p, d)], 512, ctx_peers, w_send, w_recv)
    copies[0].wait()
    toks.start(0, 1, 2)
    copies[1].wait()
    copies[2].wait()
    weights.start(0, 1, 2)
    tshare.start(0)

    toks.arrived(1, 2)
    toks.start(5, 6)
    tshare.start(2, 3)
    toks.arrived(0)
    toks.start(3, 4)
    tshare.start(1)
    weights.arrived(0)
    weights.start(3, 4)
    weights.arrived(1, 2)
    weights.start(5, 6)
    toks.arrived(5, 6)
    tshare.start(6)
    toks.arrived(3, 4)
    toks.start(7, 8)
    tshare.start(4, 5)
    toks.arrived(7, 8)
    tshare.start(7)
    weights.arrived(3, 4)
    weights.start(7, 8)
    tshare.arrived()
    out_tok = pltpu.make_async_copy(tbuf, tok_out, local.at[3])
    out_tok.start()

    def multiply(blocks, first):
        def one(i, carry):
            c = chosen(i // 2, blocks)
            m = lax.rem(i, 2)
            cols = pl.ds(pl.multiple_of(c * 512, 512), 512)
            left = tbuf[pl.ds(m * 8, 8), :, cols].reshape(256, 512)
            rows = pl.ds(pl.multiple_of(m * 256, 256), 256)
            acc[rows, :] += jnp.dot(left, wbuf[c], preferred_element_type=f32)
            return carry

        lax.fori_loop(0, 2 * len(blocks), one, 0)

    acc[...] = jnp.zeros_like(acc)
    multiply([ctx_at(0, 0), ctx_at(1, 0), ctx_at(0, -1), ctx_at(0, 1), ctx_at(1, -1), ctx_at(1, 1)], True)
    weights.arrived(5, 6)
    weights.arrived(7, 8)
    out_w = pltpu.make_async_copy(wbuf, w_out, local.at[4])
    out_w.start()
    multiply([ctx_at(0, 2), ctx_at(1, 2)], False)

    cosine, sine = cos_ref[...], sin_ref[...]
    held = acc[:, 256:384].astype(bf16).astype(f32)
    turned = held * cosine + pltpu.roll(held, 64, 1) * sine
    kvbuf[core, ctx] = jnp.where(core == 0, turned, held).astype(bf16)
    keys = Gather(lambda p, d: kvbuf.at[core, ctx_at(p, d)], 512, ctx_peers, k_send, k_recv)
    kshare = Share(lambda p, d: kvbuf.at[core, ctx_at(p, d)], lambda p, d: kvbuf.at[1 - core, ctx_at(p, d)], twin, f_send, f_recv)
    keys.start(0, 1, 2)
    kshare.start(0)
    for h in range(2):
        raw = acc[:, h * 128:(h + 1) * 128]
        q_ref[:, h * 128:(h + 1) * 128] = (raw * cosine + pltpu.roll(raw, 64, 1) * sine).astype(bf16)
    keys.arrived(0)
    keys.start(3, 4)
    kshare.start(1)
    keys.arrived(1, 2)
    keys.start(5, 6)
    kshare.start(2, 3)
    keys.arrived(3, 4)
    keys.start(7, 8)
    kshare.start(4, 5)
    keys.arrived(5, 6)
    kshare.start(6)
    keys.arrived(7, 8)
    kshare.start(7)
    kshare.arrived()
    out_kv = pltpu.make_async_copy(kvbuf, kv_ref, local.at[5])
    out_kv.start()
    toks.finish()
    tshare.finish()
    weights.finish()
    keys.finish()
    kshare.finish()
    out_tok.wait()
    out_w.wait()
    out_kv.wait()


def project(tokens, w_query, w_keyval, cosine, sine):
    bf16 = jnp.bfloat16
    vmem = pl.BlockSpec(memory_space=pltpu.VMEM)
    hbm = pl.BlockSpec(memory_space=pl.ANY)
    dma = pltpu.SemaphoreType.DMA
    return pl.pallas_call(
        project_kernel,
        out_shape=(
            jax.ShapeDtypeStruct((512, 256), bf16),
            jax.ShapeDtypeStruct((2, 8, 512, 128), bf16),
            jax.ShapeDtypeStruct((16, 32, 4096), bf16),
            jax.ShapeDtypeStruct((8, 512, 384), bf16),
        ),
        in_specs=[hbm, hbm, hbm, vmem, vmem],
        out_specs=(vmem, hbm, hbm, hbm),
        scratch_shapes=[
            pltpu.VMEM((16, 32, 4096), bf16),
            pltpu.VMEM((8, 512, 384), bf16),
            pltpu.VMEM((2, 8, 512, 128), bf16),
            pltpu.VMEM((512, 384), jnp.float32),
            dma((9,)), dma((9,)), dma((8,)), dma((8,)), dma((9,)), dma((9,)),
            dma((9,)), dma((9,)), dma((8,)), dma((8,)), dma((6,)),
        ],
        compiler_params=pltpu.CompilerParams(collective_id=0, has_side_effects=True, vmem_limit_bytes=VMEM_LIMIT),
        name="project",
    )(tokens, w_query, w_keyval, cosine, sine)


def reduce_kernel(tok_ref, w_ref, qb_ref, dkv_ref, cos_ref, sin_ref, tg_ref, gq_ref, gk_ref,
                  tbuf, wbuf, kv, kv_in, kv_halves, kv_wholes, kv_last, turned_q, kvg,
                  wg, wg_halves, wg_wholes, wg_last, px, pb, pb_in, tg_halves, tg_wholes, tg_last,
                  k_send, k_recv, w_send, w_recv, t_send, t_recv, e_send, e_recv, local):
    f32 = jnp.float32
    bf16 = jnp.bfloat16
    nt = (((1,), (1,)), ((), ()))
    ctx, tp, core, ctx_at, tp_at, ctx_peers, tp_peers, twin = places()
    copies = [
        pltpu.make_async_copy(dkv_ref.at[core], kv, local.at[0]),
        pltpu.make_async_copy(tok_ref, tbuf, local.at[1]),
        pltpu.make_async_copy(w_ref, wbuf, local.at[2]),
    ]
    for c in copies:
        c.start()
    meet(ctx_peers + tp_peers + [twin])
    swap = remote(dkv_ref.at[1 - core], kv_in, e_send, e_recv, 4, twin)
    swap.start()
    turned_q[...] = qb_ref[...].T
    copies[1].wait()

    def tok_cols(c):
        return tbuf[:, :, pl.ds(pl.multiple_of(c * 512, 512), 512)].reshape(512, 512)

    def query_terms(c, carry):
        wg[c, 0:256, :] = jnp.dot(turned_q[...], tok_cols(c), preferred_element_type=f32).astype(bf16)
        return carry

    keys = Reduce(lambda p, d: kv.at[ctx_at(p, d)], 512, ctx_peers, kv_halves, kv_wholes, kv_last, k_send, k_recv)
    copies[0].wait()
    swap.wait_recv()
    for d in (2, 1, -1, 0):
        for p in (1, 0):
            add_into(kv.at[ctx_at(p, d)], kv_in.at[ctx_at(p, d)])
        if d == 2:
            keys.start(0, 1, 2, 3)
    lax.fori_loop(0, 8, query_terms, 0)
    keys.second(1)
    keys.second(0)
    copies[2].wait()

    def query_part(c, carry):
        px[c] = lax.dot_general(qb_ref[...], wbuf[c, :, 0:256], nt, preferred_element_type=f32)
        return carry

    lax.fori_loop(0, 4, query_part, 0)
    keys.third()
    lax.fori_loop(4, 8, query_part, 0)
    keys.arrived(6, 7, 8)
    total = keys.total(...)
    back = total * cos_ref[...] - pltpu.roll(total, 64, 1) * sin_ref[...]
    total = jnp.where(core == 0, back, total)
    kvg[...] = total.astype(bf16)
    turned_q[0:128, :] = total.T.astype(bf16)

    order = [ctx_at(p, d) for d in (2, 1, -1, 0) for p in (1, 0)]

    def keyval_terms(i, carry):
        c = chosen(i, order)
        wg[c, 256:384, :] = jnp.dot(turned_q[0:128, :], tok_cols(c), preferred_element_type=f32).astype(bf16)
        return carry

    weights = Reduce(lambda p, d: wg.at[ctx_at(p, d)], 384, ctx_peers, wg_halves, wg_wholes, wg_last, w_send, w_recv)
    lax.fori_loop(0, 2, keyval_terms, 0)
    weights.start(0, 1, 2, 3)

    def keyval_part(c, carry):
        part = px[c] + lax.dot_general(kvg[...], wbuf[c, :, 256:384], nt, preferred_element_type=f32)
        part = part.astype(bf16).reshape(2, 4, 2, 32, 512)
        cols = pl.ds(pl.multiple_of(c * 512, 512), 512)
        for side in range(2):
            for level in range(4):
                for k in range(2):
                    pb[k, level, side, :, cols] = part[side, level, k]
        return carry

    lax.fori_loop(0, 8, keyval_part, 0)

    def level(d):
        return tp_at(0, d) // 2 - 4 * (tp // 8)

    steps = (2, 1, -1, 0)
    swaps = [
        remote(pb.at[1 - core, level(d)], pb_in.at[level(d)], e_send, e_recv, n, twin)
        for n, d in enumerate(steps)
    ]
    for s in swaps:
        s.start()
    lax.fori_loop(2, 8, keyval_terms, 0)
    side = tp // 8

    def tg_block(p, d):
        return pb.at[core, level(d), 1 - side if p else side]

    def merged(n):
        swaps[n].wait_recv()
        for p in (1, 0):
            add_into(tg_block(p, steps[n]), pb_in.at[level(steps[n]), 1 - side if p else side])

    toks = Reduce(tg_block, 32, tp_peers, tg_halves, tg_wholes, tg_last, t_send, t_recv)
    merged(0)
    toks.start(0, 1, 2, 3)
    merged(1)
    merged(2)
    merged(3)
    toks.second(1)
    weights.second(1)
    toks.second(0)
    weights.second(0)
    toks.third()
    weights.third()
    toks.arrived(6, 7, 8)
    tg_ref[...] = toks.total(...).astype(bf16)
    weights.arrived(6, 7, 8)
    for n in range(3):
        rows = slice(n * 128, (n + 1) * 128)
        turned = weights.total((rows, slice(None))).T
        if n < 2:
            gq_ref[:, n * 128:(n + 1) * 128] = turned
        else:
            gk_ref[...] = turned
    swap.wait_send()
    for s in swaps:
        s.wait_send()
    keys.finish()
    weights.finish()
    toks.finish()


def reduce(tok_full, w_full, query_back, dkv, cosine, sine):
    bf16 = jnp.bfloat16
    f32 = jnp.float32
    vmem = pl.BlockSpec(memory_space=pltpu.VMEM)
    hbm = pl.BlockSpec(memory_space=pl.ANY)
    dma = pltpu.SemaphoreType.DMA
    return pl.pallas_call(
        reduce_kernel,
        out_shape=(
            jax.ShapeDtypeStruct((32, 4096), bf16),
            jax.ShapeDtypeStruct((512, 256), f32),
            jax.ShapeDtypeStruct((512, 128), f32),
        ),
        in_specs=[hbm, hbm, vmem, hbm, vmem, vmem],
        out_specs=(vmem, vmem, vmem),
        scratch_shapes=[
            pltpu.VMEM((16, 32, 4096), bf16),
            pltpu.VMEM((8, 512, 384), bf16),
            pltpu.VMEM((8, 512, 128), bf16),
            pltpu.VMEM((8, 512, 128), bf16),
            pltpu.VMEM((4, 256, 128), bf16),
            pltpu.VMEM((4, 512, 128), bf16),
            pltpu.VMEM((512, 128), bf16),
            pltpu.VMEM((256, 512), bf16),
            pltpu.VMEM((512, 128), bf16),
            pltpu.VMEM((8, 384, 512), bf16),
            pltpu.VMEM((4, 192, 512), bf16),
            pltpu.VMEM((4, 384, 512), bf16),
            pltpu.VMEM((384, 512), bf16),
            pltpu.VMEM((8, 512, 512), f32),
            pltpu.VMEM((2, 4, 2, 32, 4096), bf16),
            pltpu.VMEM((4, 2, 32, 4096), bf16),
            pltpu.VMEM((4, 16, 4096), bf16),
            pltpu.VMEM((4, 32, 4096), bf16),
            pltpu.VMEM((32, 4096), bf16),
            dma((9,)), dma((9,)), dma((9,)), dma((9,)), dma((9,)), dma((9,)),
            dma((5,)), dma((5,)), dma((3,)),
        ],
        compiler_params=pltpu.CompilerParams(collective_id=1, has_side_effects=True, vmem_limit_bytes=VMEM_LIMIT),
        name="reduce",
    )(tok_full, w_full, query_back, dkv, cosine, sine)


def shards(tokens, upstream, w_query, w_keyval, positions, documents):
    ctx = lax.axis_index("ctx")
    my_pos = lax.dynamic_slice_in_dim(positions, ctx * 512, 512, 0)
    cosine, sine = rotation_tables(my_pos)
    sign = jnp.where(jnp.arange(HEAD_DIMENSION) < HEAD_DIMENSION // 2, -1.0, 1.0)
    sine = sine * sign
    query, key_value, tok_full, w_full = project(tokens, w_query, w_keyval, cosine, sine)
    query_back, dkv = attend(positions, documents, query, upstream, key_value, cosine, sine)
    return reduce(tok_full, w_full, query_back, dkv.reshape(2, 8, 512, 128), cosine, sine)


def solution(mesh):
    return jax.shard_map(
        shards,
        mesh=mesh,
        in_specs=(P(("ctx", "tp"), None), P("ctx", "tp"), P("ctx", "tp"), P("ctx", "tp"), P(), P()),
        out_specs=(P(("ctx", "tp"), None), P("ctx", "tp"), P("ctx", "tp")),
        check_vma=False,
    )
```

time: 328 us -> 142 us (0.43)
  waiting for transfers between devices: 162 us -> 0 us
  Pallas kernels: 7.04 us -> 127 us
  blocking collectives: 86.9 us -> 0 us
  other arithmetic: 27.5 us -> 2.74 us
  matrix products: 17.4 us -> 0 us
  between operations: 14 us -> 0.7 us
  starting transfers between devices: 5.28 us -> 0 us
  local copies, waits for them, and re-layouts: 8.42 us -> 12.5 us
    all_gather x2 -> x0, waiting for transfers between devices: 121 us -> none  [the longest x1 64.3 us: side_by_side(): lax.all_gather(both, axis, axis=dim, tiled=True)]
    pallas_call x0 -> x2, Pallas kernels: none -> 115 us  [the longest x1 57.7 us: project(): pl.pallas_call(project_kernel, out_shape=(jax.ShapeDtypeStruct((512, 256)...]
    all_to_all x2 -> x0, blocking collectives: 86.9 us -> none  [summed_on_arrival(): blocks = lax.all_to_all(cut_along(x, dim, count), axis, 0, 0, tiled=True)]
    reduce_scatter x1 -> x0, waiting for transfers between devices: 27.5 us -> none  [shards(): lax.psum_scatter((part_query + part_keyval).astype(jnp.bfloat16), 'tp', s...]
    dot_general x5 -> x0, matrix products: 17.4 us -> none  [the longest x1 4.91 us: shards(): query_raw = jnp.dot(gathered, query_full, preferred_element_type=f32)]
    all_to_all x1 -> x0, waiting for transfers between devices: 11.5 us -> none  [copy_for_each(): lax.all_to_all(jnp.broadcast_to(x[None], (count, *x.shape)), axis, 0, 0,...]
    concatenate x5 -> x1, other arithmetic: 11.5 us -> 0.98 us  [rotation_tables(): cosine = jnp.concatenate([jnp.cos(angles), jnp.cos(angles)], axis=1)]
    unnamed x20 -> x19, local copies, waits for them, and re-layouts: 3.3 us -> 12.5 us
  transfers between devices with their start and end apart: 6 -> 0, of which waited for: 5 -> 0; matrix products, arithmetic and copies ran while one was open for 10% -> 0% of each run, Pallas kernels for 0% -> 0%
where the time goes in v2:
time: 142 us; the launch traced here: 143 us
  Pallas kernels  127 us (89%)
  local copies, waits for them, and re-layouts  12.5 us (9%)
  other arithmetic  2.74 us (2%)
    pallas_call x1, Pallas kernels, project(): pl.pallas_call(project_kernel, out_shape=(jax.ShapeDtypeStruct((512, 256)...  57.7 us
    pallas_call x1, Pallas kernels, reduce(): pl.pallas_call(reduce_kernel, out_shape=(jax.ShapeDtypeStruct((32, 4096),...  56.9 us
    unnamed x19, local copies, waits for them, and re-layouts  12.5 us
    pallas_call x1, Pallas kernels, attend(): pl.pallas_call(attend_kernel, out_shape=(jax.ShapeDtypeStruct((512, 256),...  12.5 us

profile of v2, /device:TPU:0, one launch (start us, length us, event | category | flops | bytes accessed | tf_op | source)
XLA Modules:
  0.0 143.1 jit_solution(7971797116330983858)
XLA Ops:
  0.7 0.8 dynamic-slice_convert_fusion
  1.4 1.0 multiply_sine_fusion
  2.4 1.0 pad_maximum_fusion
  3.4 57.7 %project.1 = (bf16[512,256]{1,0:T(8,128)(2,1)}, bf16[2,8,512,128]{3,2,1,0:T(8,128)(2,1)}, bf16[16,32,4096]{2,1,0:T(8,128)(2,1)}, bf16[8,512,384]{2,1,0:T(8,128)(2,1)}) custom-call(bf16[32,4096]{1,0:T(8,128)(2,1)} %tok_ref.1, bf16[512,256]{1,0:T(8,128)(2,1)} %wq_ref.1, bf16[512,128]{1,0:T(8,128)(2,1)} %wk_ref.1, f32[512,128]{1,0:T(8,128)} %get-tuple-element.17.cos_ref, ...), custom_call_target="tpu_custom_call" | custom-call | tf_op jit(solution)/shard_map/project/pallas_call | solution.py:419
  61.1 0.0 copy-start
  61.1 0.9 copy-done
  62.1 0.0 copy-start.1
  62.1 0.9 copy-done.1
  63.0 0.0 copy-start.3
  63.0 0.9 copy-done.3
  64.0 0.0 copy-start.5
  64.0 0.9 copy-done.5
  64.9 0.0 copy-start.6
  64.9 0.7 copy-done.6
  65.6 0.0 copy-start.7
  65.6 0.7 copy-done.7
  66.4 12.5 %attend.1 = (bf16[512,256]{1,0:T(8,128)(2,1)S(1)}, bf16[2,4096,128]{2,1,0:T(8,128)(2,1)S(1)}) custom-call(s32[4096]{0:T(1024)S(1)} %copy-done.6, s32[32,128]{1,0:T(8,128)S(1)} %bitcast.4, bf16[512,256]{1,0:T(8,128)(2,1)S(1)} %copy-done.5, bf16[512,256]{1,0:T(8,128)(2,1)S(1)} %copy-done.3, bf16[2,4096,128]{2,1,0:T(8,128)(2,1)} %bitcast.5, ...), custom_call_target="tpu_custom_call" | custom-call | tf_op jit(solution)/shard_map/attend/pallas_call | solution.py:118
  78.9 0.0 copy-start.2
  78.9 1.4 copy-done.2
  80.3 0.0 copy-start.4
  80.3 0.7 copy-done.4
  81.0 56.9 %reduce.1 = (bf16[32,4096]{1,0:T(8,128)(2,1)}, f32[512,256]{1,0:T(8,128)}, f32[512,128]{1,0:T(8,128)}) custom-call(bf16[16,32,4096]{2,1,0:T(8,128)(2,1)} %get-tuple-element.9.tok_ref, bf16[8,512,384]{2,1,0:T(8,128)(2,1)} %get-tuple-element.10.w_ref, bf16[512,256]{1,0:T(8,128)(2,1)} %copy-done.4, bf16[2,8,512,128]{3,2,1,0:T(8,128)(2,1)} %bitcast.3, ...), custom_call_target="tpu_custom_call" | custom-call | tf_op jit(solution)/shard_map/reduce/pallas_call | solution.py:577
  137.9 1.7 %copy.12 = bf16[32,4096]{1,0:T(8,128)(2,1)} copy(bf16[32,4096]{1,0:T(8,128)(2,1)} %get-tuple-element.22) | data formatting | bytes 524288
  139.6 1.9 %copy.13 = f32[512,256]{1,0:T(8,128)} copy(f32[512,256]{1,0:T(8,128)} %get-tuple-element.23) | data formatting | bytes 1048576
  141.5 1.7 %copy.14 = f32[512,128]{1,0:T(8,128)} copy(f32[512,128]{1,0:T(8,128)} %get-tuple-element.24) | data formatting | bytes 524288
  (2 shorter events, 0.0 us)
Async XLA Ops:
  61.1 1.0 copy-start
  62.1 0.9 copy-start.1
  63.0 0.9 copy-start.3
  64.0 0.9 copy-start.5
  64.9 0.7 copy-start.6
  65.6 0.7 copy-start.7
  78.9 1.4 copy-start.2
  80.3 0.7 copy-start.4

commit v3 on v2

--- a/solution.py
+++ b/solution.py
@@ -9,15 +9,6 @@
 
 
 rope_base = 500000.0
-
-
-def rotation_tables(positions):
-    half_width = HEAD_DIMENSION // 2
-    frequency = rope_base ** (-(jnp.arange(half_width, dtype=jnp.float32) * 2.0 / HEAD_DIMENSION))
-    angles = positions.astype(jnp.float32)[:, None] * frequency[None, :]
-    cosine = jnp.concatenate([jnp.cos(angles), jnp.cos(angles)], axis=1)
-    sine = jnp.concatenate([jnp.sin(angles), jnp.sin(angles)], axis=1)
-    return (cosine, sine)
 
 
 def attend_kernel(pos_ref, doc_ref, q_ref, up_ref, kv_ref, cos_ref, sin_ref, qb_ref, dkv_ref,
@@ -133,7 +124,7 @@
             pltpu.VMEM((4096, 128), f32),
             pltpu.SMEM((16,), jnp.int32),
         ],
-        compiler_params=pltpu.CompilerParams(vmem_limit_bytes=50 * 1024 * 1024),
+        compiler_params=pltpu.CompilerParams(vmem_limit_bytes=60 * 1024 * 1024),
         name="attend",
     )(positions, documents.reshape(32, 128), query, upstream, key_value.reshape(2, 4096, 128), cosine, sine)
 
@@ -184,13 +175,14 @@
 
         pair, after, before = peers
         self.out = [
-            (block(0, 0), pair), (block(0, 0), after), (block(0, 0), before),
-            (block(1, 0), after), (block(1, 0), before),
+            (part(0, 0, 0), pair), (part(0, 0, 1), pair), (block(0, 0), after), (block(0, 0), before),
+            (part(1, 0, 0), after), (part(1, 0, 0), before), (part(1, 0, 1), after), (part(1, 0, 1), before),
             (part(0, -1, 0), after), (part(0, 1, 1), before),
             (part(1, -1, 0), after), (part(1, 1, 1), before),
         ]
         self.into = [
-            block(1, 0), block(0, -1), block(0, 1), block(1, -1), block(1, 1),
+            part(1, 0, 0), part(1, 0, 1), block(0, -1), block(0, 1),
+            part(1, -1, 0), part(1, 1, 0), part(1, -1, 1), part(1, 1, 1),
             part(0, 2, 0), part(0, 2, 1), part(1, 2, 0), part(1, 2, 1),
         ]
         self.sems = (send, recv)
@@ -208,6 +200,29 @@
     def finish(self):
         for n, (ref, peer) in enumerate(self.out):
             remote(ref, ref, *self.sems, n, peer).wait_send()
+
+
+class RingGather:
+    def __init__(self, block, rows, peers, send, recv):
+        half = rows // 2
+
+        def part(pair, step, h):
+            return block(pair, step).at[pl.ds(h * half, half)]
+
+        pair, after, before = peers
+        self.out = [
+            (block(0, 0), after), (block(0, 0), before), (part(0, -1, 0), after), (part(0, 1, 1), before),
+            (block(0, 0), pair), (block(0, -1), pair), (block(0, 1), pair), (part(0, 2, 0), pair), (part(0, 2, 1), pair),
+        ]
+        self.into = [
+            block(0, -1), block(0, 1), part(0, 2, 0), part(0, 2, 1),
+            block(1, 0), block(1, -1), block(1, 1), part(1, 2, 0), part(1, 2, 1),
+        ]
+        self.sems = (send, recv)
+
+    start = Gather.start
+    arrived = Gather.arrived
+    finish = Gather.finish
 
 
 class Share:
@@ -285,6 +300,50 @@
         return sum(r[at].astype(f32) for r in parts)
 
 
+class PairReduce:
+    steps = (2, 1, -1, 0)
+
+    def __init__(self, block, rows, peers, pairs, halves, wholes, send, recv):
+        half = rows // 2
+        pair, after, before = peers
+
+        def part(p, step, h):
+            return block(p, step).at[pl.ds(h * half, half)]
+
+        self.block = block
+        self.part = part
+        self.pairs, self.halves, self.wholes = pairs, halves, wholes
+        self.out = [(block(1, d), pairs.at[n], pair) for n, d in enumerate(self.steps)] + [
+            (part(0, 2, 0), halves.at[0], after), (part(0, 2, 1), halves.at[1], before),
+            (block(0, 1), wholes.at[0], after), (block(0, -1), wholes.at[1], before),
+        ]
+        self.sems = (send, recv)
+
+    start = Reduce.start
+    arrived = Reduce.arrived
+
+    def finish(self):
+        for n, (src, dst, peer) in enumerate(self.out):
+            remote(src, dst, *self.sems, n, peer).wait_send()
+
+    def paired(self, *which):
+        for n in which:
+            self.arrived(n)
+            add_into(self.block(0, self.steps[n]), self.pairs.at[n])
+
+    def second(self):
+        for k, (step, h) in enumerate(((1, 0), (-1, 1))):
+            self.arrived(4 + k)
+            add_into(self.part(0, step, h), self.halves.at[k])
+            self.start(6 + k)
+
+    def total(self, at):
+        f32 = jnp.float32
+        self.arrived(3, 6, 7)
+        parts = [self.block(0, 0), self.pairs.at[3], self.wholes.at[0], self.wholes.at[1]]
+        return sum(r[at].astype(f32) for r in parts)
+
+
 def add_into(dst, *terms):
     rows, cols = dst.shape
     tile = max(16, min(rows, 32768 // cols))
@@ -307,142 +366,198 @@
     return at
 
 
-def project_kernel(tok_ref, wq_ref, wk_ref, cos_ref, sin_ref, q_ref, kv_ref, tok_out, w_out,
-                   tbuf, wbuf, kvbuf, acc, t_send, t_recv, c_send, c_recv, w_send, w_recv,
-                   k_send, k_recv, f_send, f_recv, local):
+def project_kernel(pos_ref, freq_ref, tok_ref, wq_ref, wk_ref, q_ref, cos_ref, sin_ref, kv_ref, tok_out, wq_out, wk_out,
+                   tbuf, wqbuf, wkbuf, kvbuf, acc, acc_kv, t_send, t_recv, c_send, c_recv, wq_send, wq_recv, wk_send, wk_recv,
+                   k_send, k_recv, r_send, r_recv, f_send, f_recv, local):
     f32 = jnp.float32
     bf16 = jnp.bfloat16
     ctx, tp, core, ctx_at, tp_at, ctx_peers, tp_peers, twin = places()
     copies = [
-        pltpu.make_async_copy(tok_ref, tbuf.at[tp], local.at[0]),
-        pltpu.make_async_copy(wq_ref, wbuf.at[ctx, :, pl.ds(0, 256)], local.at[1]),
-        pltpu.make_async_copy(wk_ref, wbuf.at[ctx, :, pl.ds(256, 128)], local.at[2]),
+        pltpu.make_async_copy(wk_ref, wkbuf.at[ctx], local.at[0]),
+        pltpu.make_async_copy(tok_ref, tbuf.at[tp], local.at[1]),
+        pltpu.make_async_copy(wq_ref, wqbuf.at[ctx], local.at[2]),
     ]
     for c in copies:
         c.start()
     meet(ctx_peers + tp_peers + [twin])
     toks = Gather(lambda p, d: tbuf.at[tp_at(p, d)], 32, tp_peers, t_send, t_recv)
     tshare = Share(lambda p, d: tbuf.at[tp_at(p, d)], lambda p, d: tbuf.at[tp_at(p, d, 1)], twin, c_send, c_recv)
-    weights = Gather(lambda p, d: wbuf.at[ctx_at(p, d)], 512, ctx_peers, w_send, w_recv)
-    copies[0].wait()
-    toks.start(0, 1, 2)
-    copies[1].wait()
-    copies[2].wait()
-    weights.start(0, 1, 2)
+    wq = Gather(lambda p, d: wqbuf.at[ctx_at(p, d)], 512, ctx_peers, wq_send, wq_recv)
+    wk = Gather(lambda p, d: wkbuf.at[ctx_at(p, d)], 512, ctx_peers, wk_send, wk_recv)
+    for c in copies:
+        c.wait()
+    wk.start(0, 1)
+    toks.start(0, 1)
+    wk.start(2, 3)
+    toks.start(2, 3)
+    wq.start(2, 3, 0, 1)
     tshare.start(0)
 
-    toks.arrived(1, 2)
-    toks.start(5, 6)
+    row = lax.broadcasted_iota(jnp.int32, (512, 128), 0)
+    place = jnp.where(row < 256, pos_ref[ctx * 512], pos_ref[ctx * 512 + 256]) + (row & 255)
+    angle = place.astype(f32) * freq_ref[...]
+    cos_ref[...] = jnp.cos(angle)
+    sine = jnp.sin(angle)
+    sin_ref[...] = jnp.where(lax.broadcasted_iota(jnp.int32, (512, 128), 1) < 64, -sine, sine)
+    acc[...] = jnp.zeros_like(acc)
+    acc_kv[...] = jnp.zeros_like(acc_kv)
+
+    wk.arrived(0, 1)
+    wk.start(4, 5, 6, 7)
+    wk.arrived(2, 3)
+    wk.start(8, 9)
+    toks.arrived(2, 3)
+    toks.start(8, 9)
     tshare.start(2, 3)
     toks.arrived(0)
-    toks.start(3, 4)
+    toks.start(4, 5)
+    toks.arrived(1)
+    toks.start(6, 7)
     tshare.start(1)
-    weights.arrived(0)
-    weights.start(3, 4)
-    weights.arrived(1, 2)
-    weights.start(5, 6)
+    wq.arrived(2, 3)
+    wq.start(8, 9)
+    toks.arrived(8, 9)
+    tshare.start(6)
+    wk.arrived(4)
+    wk.start(10)
+    wk.arrived(7)
+    wk.start(11)
+    toks.arrived(4)
+    toks.start(10)
+    wq.arrived(0)
+    wq.start(4, 5)
+    toks.arrived(7)
+    toks.start(11)
     toks.arrived(5, 6)
-    tshare.start(6)
-    toks.arrived(3, 4)
-    toks.start(7, 8)
     tshare.start(4, 5)
-    toks.arrived(7, 8)
+    wq.arrived(1)
+    wq.start(6, 7)
+    wk.arrived(5, 6, 8, 9, 10, 11)
+    out_wk = pltpu.make_async_copy(wkbuf, wk_out, local.at[3])
+    out_wk.start()
+    toks.arrived(10, 11)
     tshare.start(7)
-    weights.arrived(3, 4)
-    weights.start(7, 8)
     tshare.arrived()
-    out_tok = pltpu.make_async_copy(tbuf, tok_out, local.at[3])
+    out_tok = pltpu.make_async_copy(tbuf, tok_out, local.at[4])
     out_tok.start()
 
-    def multiply(blocks, first):
+    def multiply(total, wbuf, blocks):
         def one(i, carry):
             c = chosen(i // 2, blocks)
             m = lax.rem(i, 2)
             cols = pl.ds(pl.multiple_of(c * 512, 512), 512)
             left = tbuf[pl.ds(m * 8, 8), :, cols].reshape(256, 512)
             rows = pl.ds(pl.multiple_of(m * 256, 256), 256)
-            acc[rows, :] += jnp.dot(left, wbuf[c], preferred_element_type=f32)
+            total[rows, :] += jnp.dot(left, wbuf[c], preferred_element_type=f32)
             return carry
 
         lax.fori_loop(0, 2 * len(blocks), one, 0)
 
-    acc[...] = jnp.zeros_like(acc)
-    multiply([ctx_at(0, 0), ctx_at(1, 0), ctx_at(0, -1), ctx_at(0, 1), ctx_at(1, -1), ctx_at(1, 1)], True)
-    weights.arrived(5, 6)
-    weights.arrived(7, 8)
-    out_w = pltpu.make_async_copy(wbuf, w_out, local.at[4])
-    out_w.start()
-    multiply([ctx_at(0, 2), ctx_at(1, 2)], False)
-
+    multiply(acc_kv, wkbuf, list(range(8)))
     cosine, sine = cos_ref[...], sin_ref[...]
-    held = acc[:, 256:384].astype(bf16).astype(f32)
+    held = acc_kv[...].astype(bf16).astype(f32)
     turned = held * cosine + pltpu.roll(held, 64, 1) * sine
     kvbuf[core, ctx] = jnp.where(core == 0, turned, held).astype(bf16)
-    keys = Gather(lambda p, d: kvbuf.at[core, ctx_at(p, d)], 512, ctx_peers, k_send, k_recv)
+    keys = Gather(lambda p, d: kvbuf.at[core, ctx_at(p, d), pl.ds(0, 256)], 256, ctx_peers, k_send, k_recv)
+    round_keys = RingGather(lambda p, d: kvbuf.at[core, ctx_at(p, d), pl.ds(256, 256)], 256, ctx_peers, r_send, r_recv)
     kshare = Share(lambda p, d: kvbuf.at[core, ctx_at(p, d)], lambda p, d: kvbuf.at[1 - core, ctx_at(p, d)], twin, f_send, f_recv)
-    keys.start(0, 1, 2)
+    keys.start(0, 1)
+    round_keys.start(0, 1)
+    keys.start(2, 3)
+    round_keys.start(4)
     kshare.start(0)
+    wq.arrived(4)
+    wq.start(10)
+    wq.arrived(7)
+    wq.start(11)
+    multiply(acc, wqbuf, [ctx_at(0, 0), ctx_at(1, 0), ctx_at(0, -1), ctx_at(0, 1)])
+    round_keys.arrived(0, 1)
+    round_keys.start(2, 3, 5, 6)
+    keys.arrived(0, 1)
+    keys.start(4, 5, 6, 7)
+    keys.arrived(2, 3)
+    keys.start(8, 9)
+    kshare.start(2, 3)
+    round_keys.arrived(4)
+    kshare.start(1)
+    wq.arrived(5, 6)
+    multiply(acc, wqbuf, [ctx_at(1, -1), ctx_at(1, 1)])
+    round_keys.arrived(2, 3)
+    round_keys.start(7, 8)
+    keys.arrived(4)
+    keys.start(10)
+    keys.arrived(7)
+    keys.start(11)
+    wq.arrived(8, 9, 10, 11)
+    out_wq = pltpu.make_async_copy(wqbuf, wq_out, local.at[5])
+    out_wq.start()
+    multiply(acc, wqbuf, [ctx_at(0, 2), ctx_at(1, 2)])
     for h in range(2):
         raw = acc[:, h * 128:(h + 1) * 128]
         q_ref[:, h * 128:(h + 1) * 128] = (raw * cosine + pltpu.roll(raw, 64, 1) * sine).astype(bf16)
-    keys.arrived(0)
-    keys.start(3, 4)
-    kshare.start(1)
-    keys.arrived(1, 2)
-    keys.start(5, 6)
-    kshare.start(2, 3)
-    keys.arrived(3, 4)
-    keys.start(7, 8)
+    keys.arrived(5, 6)
+    round_keys.arrived(5, 6)
     kshare.start(4, 5)
-    keys.arrived(5, 6)
+    keys.arrived(8, 9)
     kshare.start(6)
-    keys.arrived(7, 8)
+    keys.arrived(10, 11)
+    round_keys.arrived(7, 8)
     kshare.start(7)
     kshare.arrived()
-    out_kv = pltpu.make_async_copy(kvbuf, kv_ref, local.at[5])
+    out_kv = pltpu.make_async_copy(kvbuf, kv_ref, local.at[6])
     out_kv.start()
     toks.finish()
     tshare.finish()
-    weights.finish()
+    wq.finish()
+    wk.finish()
     keys.finish()
+    round_keys.finish()
     kshare.finish()
     out_tok.wait()
-    out_w.wait()
+    out_wq.wait()
+    out_wk.wait()
     out_kv.wait()
 
 
-def project(tokens, w_query, w_keyval, cosine, sine):
+def project(positions, frequency, tokens, w_query, w_keyval):
     bf16 = jnp.bfloat16
+    f32 = jnp.float32
     vmem = pl.BlockSpec(memory_space=pltpu.VMEM)
-    hbm = pl.BlockSpec(memory_space=pl.ANY)
+    hbm = pl.BlockSpec(memory_space=pltpu.HBM)
     dma = pltpu.SemaphoreType.DMA
     return pl.pallas_call(
         project_kernel,
         out_shape=(
             jax.ShapeDtypeStruct((512, 256), bf16),
+            jax.ShapeDtypeStruct((512, 128), f32),
+            jax.ShapeDtypeStruct((512, 128), f32),
             jax.ShapeDtypeStruct((2, 8, 512, 128), bf16),
             jax.ShapeDtypeStruct((16, 32, 4096), bf16),
-            jax.ShapeDtypeStruct((8, 512, 384), bf16),
+            jax.ShapeDtypeStruct((8, 512, 256), bf16),
+            jax.ShapeDtypeStruct((8, 512, 128), bf16),
         ),
-        in_specs=[hbm, hbm, hbm, vmem, vmem],
-        out_specs=(vmem, hbm, hbm, hbm),
+        in_specs=[pl.BlockSpec(memory_space=pltpu.SMEM), vmem, hbm, hbm, hbm],
+        out_specs=(vmem, vmem, vmem, hbm, hbm, hbm, hbm),
         scratch_shapes=[
             pltpu.VMEM((16, 32, 4096), bf16),
-            pltpu.VMEM((8, 512, 384), bf16),
+            pltpu.VMEM((8, 512, 256), bf16),
+            pltpu.VMEM((8, 512, 128), bf16),
             pltpu.VMEM((2, 8, 512, 128), bf16),
-            pltpu.VMEM((512, 384), jnp.float32),
-            dma((9,)), dma((9,)), dma((8,)), dma((8,)), dma((9,)), dma((9,)),
-            dma((9,)), dma((9,)), dma((8,)), dma((8,)), dma((6,)),
+            pltpu.VMEM((512, 256), f32),
+            pltpu.VMEM((512, 128), f32),
+            dma((12,)), dma((12,)), dma((8,)), dma((8,)), dma((12,)), dma((12,)), dma((12,)), dma((12,)),
+            dma((12,)), dma((12,)), dma((9,)), dma((9,)), dma((8,)), dma((8,)), dma((7,)),
         ],
         compiler_params=pltpu.CompilerParams(collective_id=0, has_side_effects=True, vmem_limit_bytes=VMEM_LIMIT),
         name="project",
-    )(tokens, w_query, w_keyval, cosine, sine)
-
-
-def reduce_kernel(tok_ref, w_ref, qb_ref, dkv_ref, cos_ref, sin_ref, tg_ref, gq_ref, gk_ref,
-                  tbuf, wbuf, kv, kv_in, kv_halves, kv_wholes, kv_last, turned_q, kvg,
-                  wg, wg_halves, wg_wholes, wg_last, px, pb, pb_in, tg_halves, tg_wholes, tg_last,
-                  k_send, k_recv, w_send, w_recv, t_send, t_recv, e_send, e_recv, local):
+    )(positions, frequency, tokens, w_query, w_keyval)
+
+
+def reduce_kernel(tok_ref, wq_ref, wk_ref, qb_ref, dkv_ref, cos_ref, sin_ref, tg_ref, sum_ref,
+                  tbuf, wqbuf, wkbuf, kv, kv_in, kv_halves, kv_wholes, kv_last, kp_pairs, kp_halves, kp_wholes, turned_q, kvg,
+                  wq, wq_halves, wq_wholes, wq_last, wp_pairs, wp_halves, wp_wholes, wk, wk_halves, wk_wholes, wk_last,
+                  px, pb, pb_in, pp, pp_in, tg_halves, tg_wholes, tg_last, tp_pairs, tp_halves, tp_wholes,
+                  k_send, k_recv, kp_send, kp_recv, tp_send, tp_recv, wp_send, wp_recv, wq_send, wq_recv, wk_send, wk_recv, t_send, t_recv, e_send, e_recv, local):
     f32 = jnp.float32
     bf16 = jnp.bfloat16
     nt = (((1,), (1,)), ((), ()))
@@ -450,176 +565,267 @@
     copies = [
         pltpu.make_async_copy(dkv_ref.at[core], kv, local.at[0]),
         pltpu.make_async_copy(tok_ref, tbuf, local.at[1]),
-        pltpu.make_async_copy(w_ref, wbuf, local.at[2]),
+        pltpu.make_async_copy(wq_ref, wqbuf, local.at[2]),
+        pltpu.make_async_copy(wk_ref, wkbuf, local.at[3]),
     ]
     for c in copies:
         c.start()
     meet(ctx_peers + tp_peers + [twin])
-    swap = remote(dkv_ref.at[1 - core], kv_in, e_send, e_recv, 4, twin)
-    swap.start()
+    side = tp // 8
+    steps = (2, 1, -1, 0)
+
+    def ring_of(d):
+        return lax.rem(ctx // 2 + d + 4, 4)
+
+    def pair_of(d):
+        return pl.ds(pl.multiple_of(ring_of(d) * 2, 2), 2)
+
+    swap = [
+        remote(dkv_ref.at[1 - core, pair_of(d)], kv_in.at[pair_of(d)], e_send, e_recv, 8 + n, twin)
+        for n, d in enumerate(steps)
+    ]
+    for s in swap:
+        s.start()
     turned_q[...] = qb_ref[...].T
-    copies[1].wait()
+    order = [ctx_at(p, d) for d in steps for p in (1, 0)]
 
     def tok_cols(c):
         return tbuf[:, :, pl.ds(pl.multiple_of(c * 512, 512), 512)].reshape(512, 512)
 
-    def query_terms(c, carry):
-        wg[c, 0:256, :] = jnp.dot(turned_q[...], tok_cols(c), preferred_element_type=f32).astype(bf16)
+    def query_terms(i, carry):
+        c = chosen(i, order)
+        wq[c] = jnp.dot(turned_q[...], tok_cols(c), preferred_element_type=f32).astype(bf16)
         return carry
 
-    keys = Reduce(lambda p, d: kv.at[ctx_at(p, d)], 512, ctx_peers, kv_halves, kv_wholes, kv_last, k_send, k_recv)
+    keys = Reduce(
+        lambda p, d: kv.at[ctx_at(p, d), pl.ds(0, 256)], 256, ctx_peers, kv_halves, kv_wholes, kv_last, k_send, k_recv
+    )
+    pair_keys = PairReduce(
+        lambda p, d: kv.at[ctx_at(p, d), pl.ds(256, 256)], 256, ctx_peers, kp_pairs, kp_halves, kp_wholes, kp_send, kp_recv
+    )
+    wq_sum = Reduce(
+        lambda p, d: wq.at[ctx_at(p, d), pl.ds(0, 128)], 128, ctx_peers, wq_halves, wq_wholes, wq_last, wq_send, wq_recv
+    )
+    wp_sum = PairReduce(
+        lambda p, d: wq.at[ctx_at(p, d), pl.ds(128, 128)], 128, ctx_peers, wp_pairs, wp_halves, wp_wholes, wp_send, wp_recv
+    )
+    wk_sum = Reduce(lambda p, d: wk.at[ctx_at(p, d)], 128, ctx_peers, wk_halves, wk_wholes, wk_last, wk_send, wk_recv)
+    copies[1].wait()
+    lax.fori_loop(0, 1, query_terms, 0)
+    wq_sum.start(0, 1)
+    wp_sum.start(0)
     copies[0].wait()
-    swap.wait_recv()
-    for d in (2, 1, -1, 0):
+    for n, d in enumerate(steps):
+        swap[n].wait_recv()
         for p in (1, 0):
             add_into(kv.at[ctx_at(p, d)], kv_in.at[ctx_at(p, d)])
+        pair_keys.start(n)
         if d == 2:
             keys.start(0, 1, 2, 3)
-    lax.fori_loop(0, 8, query_terms, 0)
+    lax.fori_loop(1, 2, query_terms, 0)
+    wq_sum.start(2, 3)
+    lax.fori_loop(2, 4, query_terms, 0)
+    wp_sum.start(1)
     keys.second(1)
     keys.second(0)
+    pair_keys.paired(0)
+    pair_keys.start(4, 5)
+    lax.fori_loop(4, 6, query_terms, 0)
+    pair_keys.paired(1, 2)
+    pair_keys.second()
+    wq_sum.second(1)
+    keys.third()
+    lax.fori_loop(6, 8, query_terms, 0)
+    wp_sum.start(2, 3)
     copies[2].wait()
 
     def query_part(c, carry):
-        px[c] = lax.dot_general(qb_ref[...], wbuf[c, :, 0:256], nt, preferred_element_type=f32)
+        px[c] = lax.dot_general(qb_ref[...], wqbuf[c], nt, preferred_element_type=f32)
         return carry
 
-    lax.fori_loop(0, 4, query_part, 0)
-    keys.third()
-    lax.fori_loop(4, 8, query_part, 0)
+    lax.fori_loop(0, 8, query_part, 0)
+    wq_sum.second(0)
+    copies[3].wait()
     keys.arrived(6, 7, 8)
-    total = keys.total(...)
+    total = jnp.concatenate([keys.total(...), pair_keys.total(...)], axis=0)
     back = total * cos_ref[...] - pltpu.roll(total, 64, 1) * sin_ref[...]
     total = jnp.where(core == 0, back, total)
     kvg[...] = total.astype(bf16)
-    turned_q[0:128, :] = total.T.astype(bf16)
-
-    order = [ctx_at(p, d) for d in (2, 1, -1, 0) for p in (1, 0)]
+
+    def level_of(d):
+        return lax.rem(tp // 2 + d + 4, 4)
+
+    out_parts, in_parts = (pb, pp), (pb_in, pp_in)
+    swaps = [
+        [
+            remote(out_parts[h].at[1 - core, level_of(d)], in_parts[h].at[level_of(d)], e_send, e_recv, 4 * h + n, twin)
+            for n, d in enumerate(steps)
+        ]
+        for h in range(2)
+    ]
+
+    def tg_block(h):
+        return lambda p, d: out_parts[h].at[core, level_of(d), 1 - side if p else side]
+
+    ring_toks = Reduce(tg_block(0), 32, tp_peers, tg_halves, tg_wholes, tg_last, t_send, t_recv)
+    pair_toks = PairReduce(tg_block(1), 32, tp_peers, tp_pairs, tp_halves, tp_wholes, tp_send, tp_recv)
+
+    def merged(h, n):
+        swaps[h][n].wait_recv()
+        for p in (1, 0):
+            add_into(tg_block(h)(p, steps[n]), in_parts[h].at[level_of(steps[n]), 1 - side if p else side])
+
+    def keyval_part(h, first):
+        def one(c, carry):
+            part = px[c] + lax.dot_general(kvg[...], wkbuf[c], nt, preferred_element_type=f32)
+            part = part.astype(bf16).reshape(2, 4, 2, 32, 512)
+            cols = pl.ds(pl.multiple_of((c - first) * 512, 512), 512)
+            for s in range(2):
+                for level in range(4):
+                    for k in range(2):
+                        out_parts[h][k, level, s, :, cols] = part[s, level, k]
+            return carry
+
+        return one
 
     def keyval_terms(i, carry):
         c = chosen(i, order)
-        wg[c, 256:384, :] = jnp.dot(turned_q[0:128, :], tok_cols(c), preferred_element_type=f32).astype(bf16)
+        wk[c] = jnp.dot(turned_q[0:128, :], tok_cols(c), preferred_element_type=f32).astype(bf16)
         return carry
 
-    weights = Reduce(lambda p, d: wg.at[ctx_at(p, d)], 384, ctx_peers, wg_halves, wg_wholes, wg_last, w_send, w_recv)
+    lax.fori_loop(0, 6, keyval_part(0, 0), 0)
+    for s in swaps[0]:
+        s.start()
+    turned_q[0:128, :] = total.T.astype(bf16)
     lax.fori_loop(0, 2, keyval_terms, 0)
-    weights.start(0, 1, 2, 3)
-
-    def keyval_part(c, carry):
-        part = px[c] + lax.dot_general(kvg[...], wbuf[c, :, 256:384], nt, preferred_element_type=f32)
-        part = part.astype(bf16).reshape(2, 4, 2, 32, 512)
-        cols = pl.ds(pl.multiple_of(c * 512, 512), 512)
-        for side in range(2):
-            for level in range(4):
-                for k in range(2):
-                    pb[k, level, side, :, cols] = part[side, level, k]
-        return carry
-
-    lax.fori_loop(0, 8, keyval_part, 0)
-
-    def level(d):
-        return tp_at(0, d) // 2 - 4 * (tp // 8)
-
-    steps = (2, 1, -1, 0)
-    swaps = [
-        remote(pb.at[1 - core, level(d)], pb_in.at[level(d)], e_send, e_recv, n, twin)
-        for n, d in enumerate(steps)
-    ]
-    for s in swaps:
+    wk_sum.start(0, 1, 2, 3)
+    lax.fori_loop(6, 8, keyval_part(1, 6), 0)
+    for s in swaps[1]:
         s.start()
+    merged(0, 0)
+    ring_toks.start(0, 1, 2, 3)
+    wp_sum.paired(0)
+    wp_sum.start(4, 5)
+    for n in range(4):
+        merged(1, n)
+        pair_toks.start(n)
+    wp_sum.paired(1, 2)
+    wp_sum.second()
     lax.fori_loop(2, 8, keyval_terms, 0)
-    side = tp // 8
-
-    def tg_block(p, d):
-        return pb.at[core, level(d), 1 - side if p else side]
-
-    def merged(n):
-        swaps[n].wait_recv()
-        for p in (1, 0):
-            add_into(tg_block(p, steps[n]), pb_in.at[level(steps[n]), 1 - side if p else side])
-
-    toks = Reduce(tg_block, 32, tp_peers, tg_halves, tg_wholes, tg_last, t_send, t_recv)
-    merged(0)
-    toks.start(0, 1, 2, 3)
-    merged(1)
-    merged(2)
-    merged(3)
-    toks.second(1)
-    weights.second(1)
-    toks.second(0)
-    weights.second(0)
-    toks.third()
-    weights.third()
-    toks.arrived(6, 7, 8)
-    tg_ref[...] = toks.total(...).astype(bf16)
-    weights.arrived(6, 7, 8)
-    for n in range(3):
-        rows = slice(n * 128, (n + 1) * 128)
-        turned = weights.total((rows, slice(None))).T
-        if n < 2:
-            gq_ref[:, n * 128:(n + 1) * 128] = turned
-        else:
-            gk_ref[...] = turned
-    swap.wait_send()
-    for s in swaps:
+    for n in (1, 2, 3):
+        merged(0, n)
+    ring_toks.second(1)
+    ring_toks.second(0)
+    wq_sum.third()
+    pair_toks.paired(0)
+    pair_toks.start(4, 5)
+    pair_toks.paired(1, 2)
+    pair_toks.second()
+    wk_sum.second(1)
+    wk_sum.second(0)
+    ring_toks.third()
+    wk_sum.third()
+    wq_sum.arrived(6, 7, 8)
+    sum_ref[0:128, :] = wq_sum.total(...)
+    sum_ref[128:256, :] = wp_sum.total(...)
+    tg_ref[:, 3072:4096] = pair_toks.total(...).astype(bf16)
+    ring_toks.arrived(6, 7, 8)
+    tg_ref[:, 0:3072] = ring_toks.total(...).astype(bf16)
+    wk_sum.arrived(6, 7, 8)
+    sum_ref[256:384, :] = wk_sum.total(...)
+    for s in swap + swaps[0] + swaps[1]:
         s.wait_send()
-    keys.finish()
-    weights.finish()
-    toks.finish()
-
-
-def reduce(tok_full, w_full, query_back, dkv, cosine, sine):
+    for r in (keys, pair_keys, wq_sum, wp_sum, wk_sum, ring_toks, pair_toks):
+        r.finish()
+
+
+def reduce(tok_full, wq_full, wk_full, query_back, dkv, cosine, sine):
     bf16 = jnp.bfloat16
     f32 = jnp.float32
     vmem = pl.BlockSpec(memory_space=pltpu.VMEM)
-    hbm = pl.BlockSpec(memory_space=pl.ANY)
+    hbm = pl.BlockSpec(memory_space=pltpu.HBM)
     dma = pltpu.SemaphoreType.DMA
     return pl.pallas_call(
         reduce_kernel,
         out_shape=(
             jax.ShapeDtypeStruct((32, 4096), bf16),
-            jax.ShapeDtypeStruct((512, 256), f32),
-            jax.ShapeDtypeStruct((512, 128), f32),
+            jax.ShapeDtypeStruct((384, 512), f32),
         ),
-        in_specs=[hbm, hbm, vmem, hbm, vmem, vmem],
-        out_specs=(vmem, vmem, vmem),
+        in_specs=[hbm, hbm, hbm, vmem, hbm, vmem, vmem],
+        out_specs=(vmem, vmem),
         scratch_shapes=[
             pltpu.VMEM((16, 32, 4096), bf16),
-            pltpu.VMEM((8, 512, 384), bf16),
+            pltpu.VMEM((8, 512, 256), bf16),
             pltpu.VMEM((8, 512, 128), bf16),
             pltpu.VMEM((8, 512, 128), bf16),
+            pltpu.VMEM((8, 512, 128), bf16),
+            pltpu.VMEM((4, 128, 128), bf16),
             pltpu.VMEM((4, 256, 128), bf16),
-            pltpu.VMEM((4, 512, 128), bf16),
-            pltpu.VMEM((512, 128), bf16),
+            pltpu.VMEM((256, 128), bf16),
+            pltpu.VMEM((4, 256, 128), bf16),
+            pltpu.VMEM((2, 128, 128), bf16),
+            pltpu.VMEM((2, 256, 128), bf16),
             pltpu.VMEM((256, 512), bf16),
             pltpu.VMEM((512, 128), bf16),
-            pltpu.VMEM((8, 384, 512), bf16),
-            pltpu.VMEM((4, 192, 512), bf16),
-            pltpu.VMEM((4, 384, 512), bf16),
-            pltpu.VMEM((384, 512), bf16),
+            pltpu.VMEM((8, 256, 512), bf16),
+            pltpu.VMEM((4, 64, 512), bf16),
+            pltpu.VMEM((4, 128, 512), bf16),
+            pltpu.VMEM((128, 512), bf16),
+            pltpu.VMEM((4, 128, 512), bf16),
+            pltpu.VMEM((2, 64, 512), bf16),
+            pltpu.VMEM((2, 128, 512), bf16),
+            pltpu.VMEM((8, 128, 512), bf16),
+            pltpu.VMEM((4, 64, 512), bf16),
+            pltpu.VMEM((4, 128, 512), bf16),
+            pltpu.VMEM((128, 512), bf16),
             pltpu.VMEM((8, 512, 512), f32),
-            pltpu.VMEM((2, 4, 2, 32, 4096), bf16),
-            pltpu.VMEM((4, 2, 32, 4096), bf16),
-            pltpu.VMEM((4, 16, 4096), bf16),
-            pltpu.VMEM((4, 32, 4096), bf16),
-            pltpu.VMEM((32, 4096), bf16),
+            pltpu.VMEM((2, 4, 2, 32, 3072), bf16),
+            pltpu.VMEM((4, 2, 32, 3072), bf16),
+            pltpu.VMEM((2, 4, 2, 32, 1024), bf16),
+            pltpu.VMEM((4, 2, 32, 1024), bf16),
+            pltpu.VMEM((4, 16, 3072), bf16),
+            pltpu.VMEM((4, 32, 3072), bf16),
+            pltpu.VMEM((32, 3072), bf16),
+            pltpu.VMEM((4, 32, 1024), bf16),
+            pltpu.VMEM((2, 16, 1024), bf16),
+            pltpu.VMEM((2, 32, 1024), bf16),
+            dma((9,)), dma((9,)), dma((8,)), dma((8,)), dma((8,)), dma((8,)), dma((8,)), dma((8,)),
             dma((9,)), dma((9,)), dma((9,)), dma((9,)), dma((9,)), dma((9,)),
-            dma((5,)), dma((5,)), dma((3,)),
+            dma((12,)), dma((12,)), dma((4,)),
         ],
         compiler_params=pltpu.CompilerParams(collective_id=1, has_side_effects=True, vmem_limit_bytes=VMEM_LIMIT),
         name="reduce",
-    )(tok_full, w_full, query_back, dkv, cosine, sine)
+    )(tok_full, wq_full, wk_full, query_back, dkv, cosine, sine)
+
+
+def finish_kernel(tg_ref, sum_ref, token_ref, gq_ref, gk_ref):
+    token_ref[...] = tg_ref[...]
+    gq_ref[...] = sum_ref[0:256, :].T
+    gk_ref[...] = sum_ref[256:384, :].T
+
+
+def finish(token_grad, weight_grad):
+    vmem = pl.BlockSpec(memory_space=pltpu.VMEM)
+    return pl.pallas_call(
+        finish_kernel,
+        out_shape=(
+            jax.ShapeDtypeStruct((32, 4096), jnp.bfloat16),
+            jax.ShapeDtypeStruct((512, 256), jnp.float32),
+            jax.ShapeDtypeStruct((512, 128), jnp.float32),
+        ),
+        in_specs=[vmem, vmem],
+        out_specs=(vmem, vmem, vmem),
+        name="finish",
+    )(token_grad, weight_grad)
 
 
 def shards(tokens, upstream, w_query, w_keyval, positions, documents):
-    ctx = lax.axis_index("ctx")
-    my_pos = lax.dynamic_slice_in_dim(positions, ctx * 512, 512, 0)
-    cosine, sine = rotation_tables(my_pos)
-    sign = jnp.where(jnp.arange(HEAD_DIMENSION) < HEAD_DIMENSION // 2, -1.0, 1.0)
-    sine = sine * sign
-    query, key_value, tok_full, w_full = project(tokens, w_query, w_keyval, cosine, sine)
+    half_width = HEAD_DIMENSION // 2
+    frequency = rope_base ** (-(jnp.arange(half_width, dtype=jnp.float32) * 2.0 / HEAD_DIMENSION))
+    frequency = jnp.concatenate([frequency, frequency])[None, :]
+    query, cosine, sine, key_value, tok_full, wq_full, wk_full = project(positions, frequency, tokens, w_query, w_keyval)
     query_back, dkv = attend(positions, documents, query, upstream, key_value, cosine, sine)
-    return reduce(tok_full, w_full, query_back, dkv.reshape(2, 8, 512, 128), cosine, sine)
+    return finish(*reduce(tok_full, wq_full, wk_full, query_back, dkv.reshape(2, 8, 512, 128), cosine, sine))
 
 
 def solution(mesh):

time: 142 us -> 118 us (0.83); the launches traced: 143 us -> 118 us
  local copies, waits for them, and re-layouts: 12.5 us -> 0 us
  Pallas kernels: 127 us -> 116 us
  other arithmetic: 2.74 us -> 0.6 us
    unnamed x19 -> x0, local copies, waits for them, and re-layouts: 12.5 us -> none
    pallas_call x1, Pallas kernels: 57.7 us -> 49.5 us  [project(): pl.pallas_call(project_kernel, out_shape=(jax.ShapeDtypeStruct((512, 256)...]
    pallas_call x1, Pallas kernels: 56.9 us -> 53.3 us  [reduce(): pl.pallas_call(reduce_kernel, out_shape=(jax.ShapeDtypeStruct((32, 4096),...]
    pallas_call x0 -> x1, Pallas kernels: none -> 2.38 us  [finish(): pl.pallas_call(finish_kernel, out_shape=(jax.ShapeDtypeStruct((32, 4096),...]
where the time goes in v3:
time: 118 us
  Pallas kernels  116 us (98%)
    pallas_call x1, Pallas kernels, reduce(): pl.pallas_call(reduce_kernel, out_shape=(jax.ShapeDtypeStruct((32, 4096),...  53.3 us
    pallas_call x1, Pallas kernels, project(): pl.pallas_call(project_kernel, out_shape=(jax.ShapeDtypeStruct((512, 256)...  49.5 us
    pallas_call x1, Pallas kernels, attend(): pl.pallas_call(attend_kernel, out_shape=(jax.ShapeDtypeStruct((512, 256),...  11.2 us
    pallas_call x1, Pallas kernels, finish(): pl.pallas_call(finish_kernel, out_shape=(jax.ShapeDtypeStruct((32, 4096),...  2.38 us

profile of v3, /device:TPU:0, one launch (start us, length us, event | category | flops | bytes accessed | tf_op | source)
XLA Modules:
  0.0 117.7 jit_solution(9760382481298924917)
XLA Ops:
  0.6 0.6 maximum_bitcast_fusion.freq_ref
  1.2 49.5 %project.1 = (bf16[512,256]{1,0:T(8,128)(2,1)}, f32[512,128]{1,0:T(8,128)}, f32[512,128]{1,0:T(8,128)}, bf16[2,8,512,128]{3,2,1,0:T(8,128)(2,1)}, bf16[16,32,409...) custom-call(s32[4096]{0:T(1024)} %pos_ref.3, f32[1,128]{1,0:T(1,128)} %maximum_bitcast_fusion.freq_ref, ...), custom_call_target="tpu_custom_call" | custom-call | tf_op jit(solution)/shard_map/project/pallas_call | solution.py:528
  50.7 11.2 %attend.1 = (bf16[512,256]{1,0:T(8,128)(2,1)}, bf16[2,4096,128]{2,1,0:T(8,128)(2,1)}) custom-call(s32[4096]{0:T(1024)} %pos_ref.3, s32[32,128]{1,0:T(8,128)} %bitcast.7, bf16[512,256]{1,0:T(8,128)(2,1)} %get-tuple-element.17.q_ref, bf16[512,256]{1,0:T(8,128)(2,1)} %up_ref.1, bf16[2,4096,128]{2,1,0:T(8,128)(2,1)} %bitcast.6, ...), custom_call_target="tpu_custom_call" | custom-call | tf_op jit(solution)/shard_map/attend/pallas_call | solution.py:109
  62.0 53.3 %reduce.1 = (bf16[32,4096]{1,0:T(8,128)(2,1)}, f32[384,512]{1,0:T(8,128)}) custom-call(bf16[16,32,4096]{2,1,0:T(8,128)(2,1)} %get-tuple-element.14.tok_ref, bf16[8,512,256]{2,1,0:T(8,128)(2,1)} %get-tuple-element.15.wq_ref, bf16[8,512,128]{2,1,0:T(8,128)(2,1)} %get-tuple-element.16.wk_ref, bf16[512,256]{1,0:T(8,128)(2,1)} %get-tuple-element.21.qb_ref, ...), custom_call_target="tpu_custom_call" | custom-call | tf_op jit(solution)/shard_map/reduce/pallas_call | solution.py:748
  115.3 2.4 %finish.1 = (bf16[32,4096]{1,0:T(8,128)(2,1)}, f32[512,256]{1,0:T(8,128)}, f32[512,128]{1,0:T(8,128)}) custom-call(bf16[32,4096]{1,0:T(8,128)(2,1)} %get-tuple-element.23.tg_ref, f32[384,512]{1,0:T(8,128)} %get-tuple-element.24.sum_ref), custom_call_target="tpu_custom_call" | custom-call | tf_op jit(solution)/shard_map/finish/pallas_call | solution.py:809
  (1 shorter events, 0.0 us)

commit v4 on v3

--- a/solution.py
+++ b/solution.py
@@ -1,5 +1,6 @@
 import jax
 import jax.numpy as jnp
+import numpy as np
 from jax import lax
 from jax.experimental import pallas as pl
 from jax.experimental.pallas import tpu as pltpu
@@ -50,41 +51,62 @@
         def keys_at(j):
             return pl.ds(pl.multiple_of(where_sm[j] * run, run), run)
 
-        def scan_scores(j, peak):
-            at = keys_at(j)
-            score = lax.dot_general(kv_ref[0, at, :], q2_sc[...], nt, preferred_element_type=f32)
-            k_pos = j * run + lax.broadcasted_iota(jnp.int32, (run, 1), 0)
-            score = jnp.where((k_pos >= q_low) & (k_pos <= q_pos), score, -1e30)
-            score_sc[j - low] = score
-            grad_sc[j - low] = lax.dot_general(kv_ref[1, at, :], up2_sc[...], nt, preferred_element_type=f32)
-            return jnp.maximum(peak, jnp.max(score, axis=0, keepdims=True))
-
-        peak = lax.fori_loop(low, high, scan_scores, jnp.full((1, rows), -1e30, f32))
-
-        def scan_sums(j, sums):
+        def in_pairs(one, carry):
+            at = low
+            for size in (4, 2, 1):
+                count = (high - at) // size
+                carry = lax.fori_loop(
+                    0, count, lambda i, c, at=at, size=size: one([at + size * i + n for n in range(size)], c), carry
+                )
+                at = at + count * size
+            return carry
+
+        def scan_scores(js, peak):
+            for j in js:
+                at = keys_at(j)
+                score = lax.dot_general(kv_ref[0, at, :], q2_sc[...], nt, preferred_element_type=f32)
+                k_pos = j * run + lax.broadcasted_iota(jnp.int32, (run, 1), 0)
+                score = jnp.where((k_pos >= q_low) & (k_pos <= q_pos), score, -1e30)
+                score_sc[j - low] = score
+                grad_sc[j - low] = lax.dot_general(kv_ref[1, at, :], up2_sc[...], nt, preferred_element_type=f32)
+                peak = jnp.maximum(peak, jnp.max(score, axis=0, keepdims=True))
+            return peak
+
+        peak = in_pairs(scan_scores, jnp.full((1, rows), -1e30, f32))
+
+        def scan_sums(js, sums):
             total, delta = sums
-            exponent = jnp.exp2((score_sc[j - low] - peak) * (scaling * log2e))
-            score_sc[j - low] = exponent
-            total = total + jnp.sum(exponent, axis=0, keepdims=True)
-            delta = delta + jnp.sum(exponent * grad_sc[j - low], axis=0, keepdims=True)
+            for j in js:
+                exponent = jnp.exp2((score_sc[j - low] - peak) * (scaling * log2e))
+                score_sc[j - low] = exponent
+                total = total + jnp.sum(exponent, axis=0, keepdims=True)
+                delta = delta + jnp.sum(exponent * grad_sc[j - low], axis=0, keepdims=True)
             return total, delta
 
         zero = jnp.zeros((1, rows), f32)
-        total, delta = lax.fori_loop(low, high, scan_sums, (zero, zero))
+        total, delta = in_pairs(scan_sums, (zero, zero))
         inverse = 1.0 / total
         delta = delta * inverse
         dq_sc[...] = jnp.zeros_like(dq_sc)
 
-        def scan_grads(j, c):
-            at = keys_at(j)
-            probs = score_sc[j - low] * inverse
-            score_grad = (probs * (grad_sc[j - low] - delta)).astype(bf16)
-            dv_sc[at, :] += lax.dot_general(probs.astype(bf16), up2_sc[...], nn, preferred_element_type=f32)
-            dk_sc[at, :] += lax.dot_general(score_grad, q2_sc[...], nn, preferred_element_type=f32)
-            dq_sc[...] += lax.dot_general(kv_ref[0, at, :], score_grad, tn, preferred_element_type=f32)
+        def scan_grads(js, c):
+            ats = [keys_at(j) for j in js]
+            dvs = [dv_sc[at, :] for at in ats]
+            dks = [dk_sc[at, :] for at in ats]
+            dq = dq_sc[...]
+            for n, j in enumerate(js):
+                probs = score_sc[j - low] * inverse
+                score_grad = (probs * (grad_sc[j - low] - delta)).astype(bf16)
+                dvs[n] += lax.dot_general(probs.astype(bf16), up2_sc[...], nn, preferred_element_type=f32)
+                dks[n] += lax.dot_general(score_grad, q2_sc[...], nn, preferred_element_type=f32)
+                dq += lax.dot_general(kv_ref[0, ats[n], :], score_grad, tn, preferred_element_type=f32)
+            dq_sc[...] = dq
+            for n, at in enumerate(ats):
+                dv_sc[at, :] = dvs[n]
+                dk_sc[at, :] = dks[n]
             return c
 
-        lax.fori_loop(low, high, scan_grads, 0)
+        in_pairs(scan_grads, 0)
         cosine, sine = cos_ref[mine, :], sin_ref[mine, :]
         for h in range(2):
             grad = dq_sc[:, h * run:(h + 1) * run].T * scaling
@@ -367,7 +389,7 @@
 
 
 def project_kernel(pos_ref, freq_ref, tok_ref, wq_ref, wk_ref, q_ref, cos_ref, sin_ref, kv_ref, tok_out, wq_out, wk_out,
-                   tbuf, wqbuf, wkbuf, kvbuf, acc, acc_kv, t_send, t_recv, c_send, c_recv, wq_send, wq_recv, wk_send, wk_recv,
+                   tbuf, wqbuf, wkbuf, kvbuf, acc, acc_kv, t_send, t_recv, c_send, c_recv, wa_send, wa_recv, wb_send, wb_recv, wk_send, wk_recv,
                    k_send, k_recv, r_send, r_recv, f_send, f_recv, local):
     f32 = jnp.float32
     bf16 = jnp.bfloat16
@@ -382,15 +404,18 @@
     meet(ctx_peers + tp_peers + [twin])
     toks = Gather(lambda p, d: tbuf.at[tp_at(p, d)], 32, tp_peers, t_send, t_recv)
     tshare = Share(lambda p, d: tbuf.at[tp_at(p, d)], lambda p, d: tbuf.at[tp_at(p, d, 1)], twin, c_send, c_recv)
-    wq = Gather(lambda p, d: wqbuf.at[ctx_at(p, d)], 512, ctx_peers, wq_send, wq_recv)
+    wqa = Gather(lambda p, d: wqbuf.at[ctx_at(p, d), pl.ds(0, 320)], 320, ctx_peers, wa_send, wa_recv)
+    wqb = RingGather(lambda p, d: wqbuf.at[ctx_at(p, d), pl.ds(320, 192)], 192, ctx_peers, wb_send, wb_recv)
     wk = Gather(lambda p, d: wkbuf.at[ctx_at(p, d)], 512, ctx_peers, wk_send, wk_recv)
     for c in copies:
         c.wait()
-    wk.start(0, 1)
     toks.start(0, 1)
     wk.start(2, 3)
     toks.start(2, 3)
-    wq.start(2, 3, 0, 1)
+    wk.start(0, 1)
+    wqb.start(0, 1)
+    wqa.start(2, 3, 0, 1)
+    wqb.start(4)
     tshare.start(0)
 
     row = lax.broadcasted_iota(jnp.int32, (512, 128), 0)
@@ -400,43 +425,49 @@
     sine = jnp.sin(angle)
     sin_ref[...] = jnp.where(lax.broadcasted_iota(jnp.int32, (512, 128), 1) < 64, -sine, sine)
     acc[...] = jnp.zeros_like(acc)
-    acc_kv[...] = jnp.zeros_like(acc_kv)
-
+
+    wk.arrived(2, 3)
+    wk.start(8, 9)
+    toks.arrived(0)
+    toks.start(4, 5)
+    wqb.arrived(0, 1)
+    wqb.start(5, 6)
+    toks.arrived(2, 3)
+    tshare.start(2, 3)
+    toks.arrived(1)
+    toks.start(6, 7)
+    toks.start(8, 9)
+    tshare.start(1)
     wk.arrived(0, 1)
     wk.start(4, 5, 6, 7)
-    wk.arrived(2, 3)
-    wk.start(8, 9)
-    toks.arrived(2, 3)
-    toks.start(8, 9)
-    tshare.start(2, 3)
-    toks.arrived(0)
-    toks.start(4, 5)
-    toks.arrived(1)
-    toks.start(6, 7)
-    tshare.start(1)
-    wq.arrived(2, 3)
-    wq.start(8, 9)
-    toks.arrived(8, 9)
-    tshare.start(6)
+    wqb.start(2, 3)
+    toks.arrived(4)
+    toks.start(10)
+    wqa.arrived(2, 3)
+    wqa.start(8, 9)
+    toks.arrived(7)
+    toks.start(11)
+    toks.arrived(5, 6)
+    tshare.start(4, 5)
+    wqa.arrived(0, 1)
+    wqa.start(4, 5, 6, 7)
     wk.arrived(4)
     wk.start(10)
     wk.arrived(7)
     wk.start(11)
-    toks.arrived(4)
-    toks.start(10)
-    wq.arrived(0)
-    wq.start(4, 5)
-    toks.arrived(7)
-    toks.start(11)
-    toks.arrived(5, 6)
-    tshare.start(4, 5)
-    wq.arrived(1)
-    wq.start(6, 7)
+    wqb.arrived(2, 3)
+    wqb.start(7, 8)
+    toks.arrived(8, 9)
+    tshare.start(6)
     wk.arrived(5, 6, 8, 9, 10, 11)
     out_wk = pltpu.make_async_copy(wkbuf, wk_out, local.at[3])
     out_wk.start()
     toks.arrived(10, 11)
     tshare.start(7)
+    wqa.arrived(4)
+    wqa.start(10)
+    wqa.arrived(7)
+    wqa.start(11)
     tshare.arrived()
     out_tok = pltpu.make_async_copy(tbuf, tok_out, local.at[4])
     out_tok.start()
@@ -453,7 +484,13 @@
 
         lax.fori_loop(0, 2 * len(blocks), one, 0)
 
-    multiply(acc_kv, wkbuf, list(range(8)))
+    def keyval(m, carry):
+        left = tbuf[pl.ds(m * 8, 8)].reshape(256, 4096)
+        rows = pl.ds(pl.multiple_of(m * 256, 256), 256)
+        acc_kv[rows, :] = jnp.dot(left, wkbuf[...].reshape(4096, 128), preferred_element_type=f32)
+        return carry
+
+    lax.fori_loop(0, 2, keyval, 0)
     cosine, sine = cos_ref[...], sin_ref[...]
     held = acc_kv[...].astype(bf16).astype(f32)
     turned = held * cosine + pltpu.roll(held, 64, 1) * sine
@@ -466,11 +503,8 @@
     keys.start(2, 3)
     round_keys.start(4)
     kshare.start(0)
-    wq.arrived(4)
-    wq.start(10)
-    wq.arrived(7)
-    wq.start(11)
-    multiply(acc, wqbuf, [ctx_at(0, 0), ctx_at(1, 0), ctx_at(0, -1), ctx_at(0, 1)])
+    wqa.arrived(8, 9)
+    multiply(acc, wqbuf, [ctx_at(0, 0), ctx_at(0, -1), ctx_at(0, 1), ctx_at(0, 2)])
     round_keys.arrived(0, 1)
     round_keys.start(2, 3, 5, 6)
     keys.arrived(0, 1)
@@ -480,18 +514,20 @@
     kshare.start(2, 3)
     round_keys.arrived(4)
     kshare.start(1)
-    wq.arrived(5, 6)
-    multiply(acc, wqbuf, [ctx_at(1, -1), ctx_at(1, 1)])
+    wqa.arrived(5, 6)
+    wqb.arrived(4, 5, 6)
+    multiply(acc, wqbuf, [ctx_at(1, 0), ctx_at(1, -1), ctx_at(1, 1)])
     round_keys.arrived(2, 3)
     round_keys.start(7, 8)
     keys.arrived(4)
     keys.start(10)
     keys.arrived(7)
     keys.start(11)
-    wq.arrived(8, 9, 10, 11)
+    wqa.arrived(10, 11)
+    wqb.arrived(7, 8)
     out_wq = pltpu.make_async_copy(wqbuf, wq_out, local.at[5])
     out_wq.start()
-    multiply(acc, wqbuf, [ctx_at(0, 2), ctx_at(1, 2)])
+    multiply(acc, wqbuf, [ctx_at(1, 2)])
     for h in range(2):
         raw = acc[:, h * 128:(h + 1) * 128]
         q_ref[:, h * 128:(h + 1) * 128] = (raw * cosine + pltpu.roll(raw, 64, 1) * sine).astype(bf16)
@@ -508,7 +544,8 @@
     out_kv.start()
     toks.finish()
     tshare.finish()
-    wq.finish()
+    wqa.finish()
+    wqb.finish()
     wk.finish()
     keys.finish()
     round_keys.finish()
@@ -545,7 +582,7 @@
             pltpu.VMEM((2, 8, 512, 128), bf16),
             pltpu.VMEM((512, 256), f32),
             pltpu.VMEM((512, 128), f32),
-            dma((12,)), dma((12,)), dma((8,)), dma((8,)), dma((12,)), dma((12,)), dma((12,)), dma((12,)),
+            dma((12,)), dma((12,)), dma((8,)), dma((8,)), dma((12,)), dma((12,)), dma((9,)), dma((9,)), dma((12,)), dma((12,)),
             dma((12,)), dma((12,)), dma((9,)), dma((9,)), dma((8,)), dma((8,)), dma((7,)),
         ],
         compiler_params=pltpu.CompilerParams(collective_id=0, has_side_effects=True, vmem_limit_bytes=VMEM_LIMIT),
@@ -556,7 +593,7 @@
 def reduce_kernel(tok_ref, wq_ref, wk_ref, qb_ref, dkv_ref, cos_ref, sin_ref, tg_ref, sum_ref,
                   tbuf, wqbuf, wkbuf, kv, kv_in, kv_halves, kv_wholes, kv_last, kp_pairs, kp_halves, kp_wholes, turned_q, kvg,
                   wq, wq_halves, wq_wholes, wq_last, wp_pairs, wp_halves, wp_wholes, wk, wk_halves, wk_wholes, wk_last,
-                  px, pb, pb_in, pp, pp_in, tg_halves, tg_wholes, tg_last, tp_pairs, tp_halves, tp_wholes,
+                  px, pb, pb_in, pp, pp_in, tg_halves, tg_wholes, tg_last, tp_halves, tp_wholes, tp_last,
                   k_send, k_recv, kp_send, kp_recv, tp_send, tp_recv, wp_send, wp_recv, wq_send, wq_recv, wk_send, wk_recv, t_send, t_recv, e_send, e_recv, local):
     f32 = jnp.float32
     bf16 = jnp.bfloat16
@@ -668,7 +705,7 @@
         return lambda p, d: out_parts[h].at[core, level_of(d), 1 - side if p else side]
 
     ring_toks = Reduce(tg_block(0), 32, tp_peers, tg_halves, tg_wholes, tg_last, t_send, t_recv)
-    pair_toks = PairReduce(tg_block(1), 32, tp_peers, tp_pairs, tp_halves, tp_wholes, tp_send, tp_recv)
+    late_toks = Reduce(tg_block(1), 32, tp_peers, tp_halves, tp_wholes, tp_last, tp_send, tp_recv)
 
     def merged(h, n):
         swaps[h][n].wait_recv()
@@ -706,36 +743,36 @@
     ring_toks.start(0, 1, 2, 3)
     wp_sum.paired(0)
     wp_sum.start(4, 5)
-    for n in range(4):
-        merged(1, n)
-        pair_toks.start(n)
+    merged(1, 0)
+    late_toks.start(0, 1, 2, 3)
     wp_sum.paired(1, 2)
     wp_sum.second()
     lax.fori_loop(2, 8, keyval_terms, 0)
     for n in (1, 2, 3):
         merged(0, n)
+        merged(1, n)
     ring_toks.second(1)
     ring_toks.second(0)
     wq_sum.third()
-    pair_toks.paired(0)
-    pair_toks.start(4, 5)
-    pair_toks.paired(1, 2)
-    pair_toks.second()
+    late_toks.second(1)
+    late_toks.second(0)
     wk_sum.second(1)
     wk_sum.second(0)
     ring_toks.third()
+    late_toks.third()
     wk_sum.third()
     wq_sum.arrived(6, 7, 8)
     sum_ref[0:128, :] = wq_sum.total(...)
     sum_ref[128:256, :] = wp_sum.total(...)
-    tg_ref[:, 3072:4096] = pair_toks.total(...).astype(bf16)
     ring_toks.arrived(6, 7, 8)
     tg_ref[:, 0:3072] = ring_toks.total(...).astype(bf16)
+    late_toks.arrived(6, 7, 8)
+    tg_ref[:, 3072:4096] = late_toks.total(...).astype(bf16)
     wk_sum.arrived(6, 7, 8)
     sum_ref[256:384, :] = wk_sum.total(...)
     for s in swap + swaps[0] + swaps[1]:
         s.wait_send()
-    for r in (keys, pair_keys, wq_sum, wp_sum, wk_sum, ring_toks, pair_toks):
+    for r in (keys, pair_keys, wq_sum, wp_sum, wk_sum, ring_toks, late_toks):
         r.finish()
 
 
@@ -786,10 +823,10 @@
             pltpu.VMEM((4, 16, 3072), bf16),
             pltpu.VMEM((4, 32, 3072), bf16),
             pltpu.VMEM((32, 3072), bf16),
+            pltpu.VMEM((4, 16, 1024), bf16),
             pltpu.VMEM((4, 32, 1024), bf16),
-            pltpu.VMEM((2, 16, 1024), bf16),
-            pltpu.VMEM((2, 32, 1024), bf16),
-            dma((9,)), dma((9,)), dma((8,)), dma((8,)), dma((8,)), dma((8,)), dma((8,)), dma((8,)),
+            pltpu.VMEM((32, 1024), bf16),
+            dma((9,)), dma((9,)), dma((8,)), dma((8,)), dma((9,)), dma((9,)), dma((8,)), dma((8,)),
             dma((9,)), dma((9,)), dma((9,)), dma((9,)), dma((9,)), dma((9,)),
             dma((12,)), dma((12,)), dma((4,)),
         ],
@@ -805,24 +842,28 @@
 
 
 def finish(token_grad, weight_grad):
-    vmem = pl.BlockSpec(memory_space=pltpu.VMEM)
     return pl.pallas_call(
         finish_kernel,
+        grid=(2,),
         out_shape=(
             jax.ShapeDtypeStruct((32, 4096), jnp.bfloat16),
             jax.ShapeDtypeStruct((512, 256), jnp.float32),
             jax.ShapeDtypeStruct((512, 128), jnp.float32),
         ),
-        in_specs=[vmem, vmem],
-        out_specs=(vmem, vmem, vmem),
+        in_specs=[pl.BlockSpec((32, 2048), lambda i: (0, i)), pl.BlockSpec((384, 256), lambda i: (0, i))],
+        out_specs=(
+            pl.BlockSpec((32, 2048), lambda i: (0, i)),
+            pl.BlockSpec((256, 256), lambda i: (i, 0)),
+            pl.BlockSpec((256, 128), lambda i: (i, 0)),
+        ),
         name="finish",
     )(token_grad, weight_grad)
 
 
 def shards(tokens, upstream, w_query, w_keyval, positions, documents):
-    half_width = HEAD_DIMENSION // 2
-    frequency = rope_base ** (-(jnp.arange(half_width, dtype=jnp.float32) * 2.0 / HEAD_DIMENSION))
-    frequency = jnp.concatenate([frequency, frequency])[None, :]
+    powers = np.arange(HEAD_DIMENSION // 2, dtype=np.float32) * np.float32(2.0 / HEAD_DIMENSION)
+    frequency = np.power(np.float32(rope_base), -powers).astype(np.float32)
+    frequency = jnp.asarray(np.concatenate([frequency, frequency])[None, :])
     query, cosine, sine, key_value, tok_full, wq_full, wk_full = project(positions, frequency, tokens, w_query, w_keyval)
     query_back, dkv = attend(positions, documents, query, upstream, key_value, cosine, sine)
     return finish(*reduce(tok_full, wq_full, wk_full, query_back, dkv.reshape(2, 8, 512, 128), cosine, sine))

time: 118 us -> 110 us (0.932)
  Pallas kernels: 116 us -> 109 us
    pallas_call x1, Pallas kernels: 49.5 us -> 46.9 us  [project(): pl.pallas_call(project_kernel, out_shape=(jax.ShapeDtypeStruct((512, 256)...]
    pallas_call x1, Pallas kernels: 53.3 us -> 50.9 us  [reduce(): pl.pallas_call(reduce_kernel, out_shape=(jax.ShapeDtypeStruct((32, 4096),...]
    pallas_call x1, Pallas kernels: 11.2 us -> 9.14 us  [attend(): pl.pallas_call(attend_kernel, out_shape=(jax.ShapeDtypeStruct((512, 256),...]
where the time goes in v4:
time: 110 us
  Pallas kernels  109 us (99%)
    pallas_call x1, Pallas kernels, reduce(): pl.pallas_call(reduce_kernel, out_shape=(jax.ShapeDtypeStruct((32, 4096),...  50.9 us
    pallas_call x1, Pallas kernels, project(): pl.pallas_call(project_kernel, out_shape=(jax.ShapeDtypeStruct((512, 256)...  46.9 us
    pallas_call x1, Pallas kernels, attend(): pl.pallas_call(attend_kernel, out_shape=(jax.ShapeDtypeStruct((512, 256),...  9.14 us

profile of v4, /device:TPU:0, one launch (start us, length us, event | category | flops | bytes accessed | tf_op | source)
XLA Modules:
  0.0 109.7 jit_solution(4723737926720029668)
XLA Ops:
  0.6 46.9 %project.1 = (bf16[512,256]{1,0:T(8,128)(2,1)}, f32[512,128]{1,0:T(8,128)}, f32[512,128]{1,0:T(8,128)}, bf16[2,8,512,128]{3,2,1,0:T(8,128)(2,1)}, bf16[16,32,409...) custom-call(s32[4096]{0:T(1024)} %pos_ref.3, f32[1,128]{1,0:T(1,128)} %constant.2.clone.freq_ref, ...), custom_call_target="tpu_custom_call" | custom-call | tf_op jit(solution)/shard_map/project/pallas_call | solution.py:565
  47.5 9.1 %attend.1 = (bf16[512,256]{1,0:T(8,128)(2,1)}, bf16[2,4096,128]{2,1,0:T(8,128)(2,1)}) custom-call(s32[4096]{0:T(1024)} %pos_ref.3, s32[32,128]{1,0:T(8,128)} %bitcast.5, bf16[512,256]{1,0:T(8,128)(2,1)} %get-tuple-element.17.q_ref, bf16[512,256]{1,0:T(8,128)(2,1)} %up_ref.1, bf16[2,4096,128]{2,1,0:T(8,128)(2,1)} %bitcast.4, ...), custom_call_target="tpu_custom_call" | custom-call | tf_op jit(solution)/shard_map/attend/pallas_call | solution.py:131
  56.7 50.9 %reduce.1 = (bf16[32,4096]{1,0:T(8,128)(2,1)}, f32[384,512]{1,0:T(8,128)}) custom-call(bf16[16,32,4096]{2,1,0:T(8,128)(2,1)} %get-tuple-element.14.tok_ref, bf16[8,512,256]{2,1,0:T(8,128)(2,1)} %get-tuple-element.15.wq_ref, bf16[8,512,128]{2,1,0:T(8,128)(2,1)} %get-tuple-element.16.wk_ref, bf16[512,256]{1,0:T(8,128)(2,1)} %get-tuple-element.21.qb_ref, ...), custom_call_target="tpu_custom_call" | custom-call | tf_op jit(solution)/shard_map/reduce/pallas_call | solution.py:785
  107.6 2.1 %finish.1 = (bf16[32,4096]{1,0:T(8,128)(2,1)}, f32[512,256]{1,0:T(8,128)}, f32[512,128]{1,0:T(8,128)}) custom-call(bf16[32,4096]{1,0:T(8,128)(2,1)} %get-tuple-element.23.tg_ref, f32[384,512]{1,0:T(8,128)} %get-tuple-element.24.sum_ref), custom_call_target="tpu_custom_call" | custom-call | tf_op jit(solution)/shard_map/finish/pallas_call | solution.py:845

commit v5 on v4

--- a/solution.py
+++ b/solution.py
@@ -174,11 +174,14 @@
     return ctx, tp, core, ctx_at, tp_at, ctx_peers, tp_peers, twin
 
 
-def meet(peers):
+def greet(peers):
     barrier = pltpu.get_barrier_semaphore()
     for peer in peers:
         pl.semaphore_signal(barrier, inc=1, device_id=peer, device_id_type=MESH)
-    pl.semaphore_wait(barrier, len(peers))
+
+
+def met(peers):
+    pl.semaphore_wait(pltpu.get_barrier_semaphore(), len(peers))
 
 
 def remote(src, dst, send, recv, n, peer):
@@ -260,9 +263,9 @@
         for n in which:
             remote(self.mine[n], self.mine[n], *self.sems, n, self.twin).start()
 
-    def arrived(self):
-        for n, ref in enumerate(self.theirs):
-            remote(ref, ref, *self.sems, n, self.twin).wait_recv()
+    def arrived(self, *which):
+        for n in which or range(8):
+            remote(self.theirs[n], self.theirs[n], *self.sems, n, self.twin).wait_recv()
 
     def finish(self):
         for n, ref in enumerate(self.mine):
@@ -368,7 +371,7 @@
 
 def add_into(dst, *terms):
     rows, cols = dst.shape
-    tile = max(16, min(rows, 32768 // cols))
+    tile = next(t for t in (256, 128, 64, 32, 16) if rows % t == 0 and (t * cols <= 32768 or t == 16))
 
     def one(i, carry):
         at = pl.ds(pl.multiple_of(i * tile, tile), tile)
@@ -389,8 +392,8 @@
 
 
 def project_kernel(pos_ref, freq_ref, tok_ref, wq_ref, wk_ref, q_ref, cos_ref, sin_ref, kv_ref, tok_out, wq_out, wk_out,
-                   tbuf, wqbuf, wkbuf, kvbuf, acc, acc_kv, t_send, t_recv, c_send, c_recv, wa_send, wa_recv, wb_send, wb_recv, wk_send, wk_recv,
-                   k_send, k_recv, r_send, r_recv, f_send, f_recv, local):
+                   tbuf, wqbuf, wkbuf, kvbuf, acc, acc_kv, pos_sc, freq_sc, cos_sc, sin_sc, t_send, t_recv, u_send, u_recv, c_send, c_recv, wa_send, wa_recv, wb_send, wb_recv, wk_send, wk_recv,
+                   k_send, k_recv, r_send, r_recv, f_send, f_recv, local, outs):
     f32 = jnp.float32
     bf16 = jnp.bfloat16
     ctx, tp, core, ctx_at, tp_at, ctx_peers, tp_peers, twin = places()
@@ -399,75 +402,88 @@
         pltpu.make_async_copy(tok_ref, tbuf.at[tp], local.at[1]),
         pltpu.make_async_copy(wq_ref, wqbuf.at[ctx], local.at[2]),
     ]
-    for c in copies:
+    small = [pltpu.make_async_copy(pos_ref, pos_sc, local.at[6]), pltpu.make_async_copy(freq_ref, freq_sc, local.at[7])]
+    greet(ctx_peers + tp_peers + [twin])
+    for c in copies + small:
         c.start()
-    meet(ctx_peers + tp_peers + [twin])
-    toks = Gather(lambda p, d: tbuf.at[tp_at(p, d)], 32, tp_peers, t_send, t_recv)
+    met(ctx_peers + tp_peers + [twin])
+    toks = Gather(lambda p, d: tbuf.at[tp_at(p, d), :, pl.ds(0, 3072)], 32, tp_peers, t_send, t_recv)
+    round_toks = RingGather(lambda p, d: tbuf.at[tp_at(p, d), :, pl.ds(3072, 1024)], 32, tp_peers, u_send, u_recv)
     tshare = Share(lambda p, d: tbuf.at[tp_at(p, d)], lambda p, d: tbuf.at[tp_at(p, d, 1)], twin, c_send, c_recv)
-    wqa = Gather(lambda p, d: wqbuf.at[ctx_at(p, d), pl.ds(0, 320)], 320, ctx_peers, wa_send, wa_recv)
-    wqb = RingGather(lambda p, d: wqbuf.at[ctx_at(p, d), pl.ds(320, 192)], 192, ctx_peers, wb_send, wb_recv)
+    wqa = Gather(lambda p, d: wqbuf.at[ctx_at(p, d), pl.ds(0, 416)], 416, ctx_peers, wa_send, wa_recv)
+    wqb = RingGather(lambda p, d: wqbuf.at[ctx_at(p, d), pl.ds(416, 96)], 96, ctx_peers, wb_send, wb_recv)
     wk = Gather(lambda p, d: wkbuf.at[ctx_at(p, d)], 512, ctx_peers, wk_send, wk_recv)
     for c in copies:
         c.wait()
     toks.start(0, 1)
     wk.start(2, 3)
+    round_toks.start(0, 1)
     toks.start(2, 3)
+    round_toks.start(4)
     wk.start(0, 1)
     wqb.start(0, 1)
-    wqa.start(2, 3, 0, 1)
-    wqb.start(4)
+    wqa.start(2, 3)
     tshare.start(0)
 
     row = lax.broadcasted_iota(jnp.int32, (512, 128), 0)
-    place = jnp.where(row < 256, pos_ref[ctx * 512], pos_ref[ctx * 512 + 256]) + (row & 255)
-    angle = place.astype(f32) * freq_ref[...]
-    cos_ref[...] = jnp.cos(angle)
+    for c in small:
+        c.wait()
+    begin = [pos_sc[pl.ds(ctx * 4 + 2 * t, 1), :][:, 0:1] for t in range(2)]
+    place = jnp.where(row < 256, begin[0], begin[1]) + (row & 255)
+    angle = place.astype(f32) * freq_sc[...]
+    cos_sc[...] = jnp.cos(angle)
     sine = jnp.sin(angle)
-    sin_ref[...] = jnp.where(lax.broadcasted_iota(jnp.int32, (512, 128), 1) < 64, -sine, sine)
+    sin_sc[...] = jnp.where(lax.broadcasted_iota(jnp.int32, (512, 128), 1) < 64, -sine, sine)
     acc[...] = jnp.zeros_like(acc)
 
+    round_toks.arrived(0, 1)
+    round_toks.start(2, 3, 5, 6)
     wk.arrived(2, 3)
     wk.start(8, 9)
     toks.arrived(0)
     toks.start(4, 5)
-    wqb.arrived(0, 1)
-    wqb.start(5, 6)
-    toks.arrived(2, 3)
-    tshare.start(2, 3)
     toks.arrived(1)
     toks.start(6, 7)
+    toks.arrived(2, 3)
     toks.start(8, 9)
+    tshare.start(2, 3)
+    round_toks.arrived(4)
     tshare.start(1)
+    wqa.arrived(2, 3)
+    round_toks.arrived(2, 3)
+    round_toks.start(7, 8)
+    wqa.start(0, 1)
+    wqa.start(8, 9)
+    wqb.start(4)
     wk.arrived(0, 1)
     wk.start(4, 5, 6, 7)
-    wqb.start(2, 3)
+    wqb.arrived(0, 1)
+    wqb.start(2, 3, 5, 6)
     toks.arrived(4)
     toks.start(10)
-    wqa.arrived(2, 3)
-    wqa.start(8, 9)
     toks.arrived(7)
     toks.start(11)
     toks.arrived(5, 6)
+    round_toks.arrived(5, 6)
     tshare.start(4, 5)
-    wqa.arrived(0, 1)
-    wqa.start(4, 5, 6, 7)
+    toks.arrived(8, 9)
+    tshare.start(6)
     wk.arrived(4)
     wk.start(10)
     wk.arrived(7)
     wk.start(11)
     wqb.arrived(2, 3)
     wqb.start(7, 8)
-    toks.arrived(8, 9)
-    tshare.start(6)
+    toks.arrived(10, 11)
+    round_toks.arrived(7, 8)
+    tshare.start(7)
     wk.arrived(5, 6, 8, 9, 10, 11)
     out_wk = pltpu.make_async_copy(wkbuf, wk_out, local.at[3])
     out_wk.start()
-    toks.arrived(10, 11)
-    tshare.start(7)
-    wqa.arrived(4)
-    wqa.start(10)
-    wqa.arrived(7)
-    wqa.start(11)
+    out_cos = pltpu.make_async_copy(cos_sc, cos_ref, local.at[6])
+    out_sin = pltpu.make_async_copy(sin_sc, sin_ref, local.at[7])
+    out_cos.start()
+    out_sin.start()
     tshare.arrived()
     out_tok = pltpu.make_async_copy(tbuf, tok_out, local.at[4])
     out_tok.start()
@@ -491,7 +507,7 @@
         return carry
 
     lax.fori_loop(0, 2, keyval, 0)
-    cosine, sine = cos_ref[...], sin_ref[...]
+    cosine, sine = cos_sc[...], sin_sc[...]
     held = acc_kv[...].astype(bf16).astype(f32)
     turned = held * cosine + pltpu.roll(held, 64, 1) * sine
     kvbuf[core, ctx] = jnp.where(core == 0, turned, held).astype(bf16)
@@ -503,6 +519,8 @@
     keys.start(2, 3)
     round_keys.start(4)
     kshare.start(0)
+    wqa.arrived(0, 1)
+    wqa.start(4, 5, 6, 7)
     wqa.arrived(8, 9)
     multiply(acc, wqbuf, [ctx_at(0, 0), ctx_at(0, -1), ctx_at(0, 1), ctx_at(0, 2)])
     round_keys.arrived(0, 1)
@@ -514,6 +532,10 @@
     kshare.start(2, 3)
     round_keys.arrived(4)
     kshare.start(1)
+    wqa.arrived(4)
+    wqa.start(10)
+    wqa.arrived(7)
+    wqa.start(11)
     wqa.arrived(5, 6)
     wqb.arrived(4, 5, 6)
     multiply(acc, wqbuf, [ctx_at(1, 0), ctx_at(1, -1), ctx_at(1, 1)])
@@ -531,18 +553,30 @@
     for h in range(2):
         raw = acc[:, h * 128:(h + 1) * 128]
         q_ref[:, h * 128:(h + 1) * 128] = (raw * cosine + pltpu.roll(raw, 64, 1) * sine).astype(bf16)
+    def block_out(mine, n):
+        p, d = Share.order[n]
+        plane = core if mine else 1 - core
+        at = ctx_at(p, d)
+        return pltpu.make_async_copy(kvbuf.at[plane, at], kv_ref.at[plane, at], outs.at[8 * mine + n])
+
+    for n in range(4):
+        block_out(1, n).start()
     keys.arrived(5, 6)
     round_keys.arrived(5, 6)
     kshare.start(4, 5)
     keys.arrived(8, 9)
     kshare.start(6)
+    for n in (4, 5, 6):
+        block_out(1, n).start()
     keys.arrived(10, 11)
     round_keys.arrived(7, 8)
     kshare.start(7)
-    kshare.arrived()
-    out_kv = pltpu.make_async_copy(kvbuf, kv_ref, local.at[6])
-    out_kv.start()
+    block_out(1, 7).start()
+    for n in range(8):
+        kshare.arrived(n)
+        block_out(0, n).start()
     toks.finish()
+    round_toks.finish()
     tshare.finish()
     wqa.finish()
     wqb.finish()
@@ -553,7 +587,11 @@
     out_tok.wait()
     out_wq.wait()
     out_wk.wait()
-    out_kv.wait()
+    out_cos.wait()
+    out_sin.wait()
+    for n in range(8):
+        block_out(0, n).wait()
+        block_out(1, n).wait()
 
 
 def project(positions, frequency, tokens, w_query, w_keyval):
@@ -573,8 +611,8 @@
             jax.ShapeDtypeStruct((8, 512, 256), bf16),
             jax.ShapeDtypeStruct((8, 512, 128), bf16),
         ),
-        in_specs=[pl.BlockSpec(memory_space=pltpu.SMEM), vmem, hbm, hbm, hbm],
-        out_specs=(vmem, vmem, vmem, hbm, hbm, hbm, hbm),
+        in_specs=[hbm] * 5,
+        out_specs=(vmem, hbm, hbm, hbm, hbm, hbm, hbm),
         scratch_shapes=[
             pltpu.VMEM((16, 32, 4096), bf16),
             pltpu.VMEM((8, 512, 256), bf16),
@@ -582,19 +620,28 @@
             pltpu.VMEM((2, 8, 512, 128), bf16),
             pltpu.VMEM((512, 256), f32),
             pltpu.VMEM((512, 128), f32),
-            dma((12,)), dma((12,)), dma((8,)), dma((8,)), dma((12,)), dma((12,)), dma((9,)), dma((9,)), dma((12,)), dma((12,)),
-            dma((12,)), dma((12,)), dma((9,)), dma((9,)), dma((8,)), dma((8,)), dma((7,)),
+            pltpu.VMEM((32, 128), jnp.int32),
+            pltpu.VMEM((1, 128), f32),
+            pltpu.VMEM((512, 128), f32),
+            pltpu.VMEM((512, 128), f32),
+            dma((12,)), dma((12,)), dma((9,)), dma((9,)), dma((8,)), dma((8,)),
+            dma((12,)), dma((12,)), dma((9,)), dma((9,)), dma((12,)), dma((12,)),
+            dma((12,)), dma((12,)), dma((9,)), dma((9,)), dma((8,)), dma((8,)), dma((8,)), dma((16,)),
         ],
         compiler_params=pltpu.CompilerParams(collective_id=0, has_side_effects=True, vmem_limit_bytes=VMEM_LIMIT),
         name="project",
-    )(positions, frequency, tokens, w_query, w_keyval)
+    )(positions.reshape(32, 128), frequency, tokens, w_query, w_keyval)
+
+
+TOKEN_PARTS = ((0, 3), (3, 3), (6, 2))
 
 
 def reduce_kernel(tok_ref, wq_ref, wk_ref, qb_ref, dkv_ref, cos_ref, sin_ref, tg_ref, sum_ref,
                   tbuf, wqbuf, wkbuf, kv, kv_in, kv_halves, kv_wholes, kv_last, kp_pairs, kp_halves, kp_wholes, turned_q, kvg,
                   wq, wq_halves, wq_wholes, wq_last, wp_pairs, wp_halves, wp_wholes, wk, wk_halves, wk_wholes, wk_last,
-                  px, pb, pb_in, pp, pp_in, tg_halves, tg_wholes, tg_last, tp_halves, tp_wholes, tp_last,
-                  k_send, k_recv, kp_send, kp_recv, tp_send, tp_recv, wp_send, wp_recv, wq_send, wq_recv, wk_send, wk_recv, t_send, t_recv, e_send, e_recv, local):
+                  qb, cos_sc, sin_sc, px, parts_out, parts_in, parts_halves, parts_wholes, parts_last,
+                  k_send, k_recv, kp_send, kp_recv, wp_send, wp_recv, wq_send, wq_recv, wk_send, wk_recv,
+                  t_send, t_recv, e_send, e_recv, local):
     f32 = jnp.float32
     bf16 = jnp.bfloat16
     nt = (((1,), (1,)), ((), ()))
@@ -604,10 +651,15 @@
         pltpu.make_async_copy(tok_ref, tbuf, local.at[1]),
         pltpu.make_async_copy(wq_ref, wqbuf, local.at[2]),
         pltpu.make_async_copy(wk_ref, wkbuf, local.at[3]),
+        pltpu.make_async_copy(cos_ref, cos_sc, local.at[4]),
+        pltpu.make_async_copy(sin_ref, sin_sc, local.at[5]),
     ]
+    first = pltpu.make_async_copy(qb_ref, qb, local.at[6])
+    greet(ctx_peers + tp_peers + [twin])
+    first.start()
     for c in copies:
         c.start()
-    meet(ctx_peers + tp_peers + [twin])
+    met(ctx_peers + tp_peers + [twin])
     side = tp // 8
     steps = (2, 1, -1, 0)
 
@@ -618,12 +670,13 @@
         return pl.ds(pl.multiple_of(ring_of(d) * 2, 2), 2)
 
     swap = [
-        remote(dkv_ref.at[1 - core, pair_of(d)], kv_in.at[pair_of(d)], e_send, e_recv, 8 + n, twin)
+        remote(dkv_ref.at[1 - core, pair_of(d)], kv_in.at[pair_of(d)], e_send, e_recv, 12 + n, twin)
         for n, d in enumerate(steps)
     ]
     for s in swap:
         s.start()
-    turned_q[...] = qb_ref[...].T
+    first.wait()
+    turned_q[...] = qb[...].T
     order = [ctx_at(p, d) for d in steps for p in (1, 0)]
 
     def tok_cols(c):
@@ -677,7 +730,7 @@
     copies[2].wait()
 
     def query_part(c, carry):
-        px[c] = lax.dot_general(qb_ref[...], wqbuf[c], nt, preferred_element_type=f32)
+        px[c] = lax.dot_general(qb[...], wqbuf[c], nt, preferred_element_type=f32)
         return carry
 
     lax.fori_loop(0, 8, query_part, 0)
@@ -685,34 +738,43 @@
     copies[3].wait()
     keys.arrived(6, 7, 8)
     total = jnp.concatenate([keys.total(...), pair_keys.total(...)], axis=0)
-    back = total * cos_ref[...] - pltpu.roll(total, 64, 1) * sin_ref[...]
+    copies[4].wait()
+    copies[5].wait()
+    back = total * cos_sc[...] - pltpu.roll(total, 64, 1) * sin_sc[...]
     total = jnp.where(core == 0, back, total)
     kvg[...] = total.astype(bf16)
 
     def level_of(d):
         return lax.rem(tp // 2 + d + 4, 4)
 
-    out_parts, in_parts = (pb, pp), (pb_in, pp_in)
+    count = len(TOKEN_PARTS)
     swaps = [
         [
-            remote(out_parts[h].at[1 - core, level_of(d)], in_parts[h].at[level_of(d)], e_send, e_recv, 4 * h + n, twin)
+            remote(parts_out[h].at[1 - core, level_of(d)], parts_in[h].at[level_of(d)], e_send, e_recv, 4 * h + n, twin)
             for n, d in enumerate(steps)
         ]
-        for h in range(2)
+        for h in range(count)
     ]
 
     def tg_block(h):
-        return lambda p, d: out_parts[h].at[core, level_of(d), 1 - side if p else side]
-
-    ring_toks = Reduce(tg_block(0), 32, tp_peers, tg_halves, tg_wholes, tg_last, t_send, t_recv)
-    late_toks = Reduce(tg_block(1), 32, tp_peers, tp_halves, tp_wholes, tp_last, tp_send, tp_recv)
-
-    def merged(h, n):
-        swaps[h][n].wait_recv()
-        for p in (1, 0):
-            add_into(tg_block(h)(p, steps[n]), in_parts[h].at[level_of(steps[n]), 1 - side if p else side])
-
-    def keyval_part(h, first):
+        return lambda p, d: parts_out[h].at[core, level_of(d), 1 - side if p else side]
+
+    toks = [
+        Reduce(
+            tg_block(h), 32, tp_peers, parts_halves[h], parts_wholes[h], parts_last[h], t_send.at[h], t_recv.at[h]
+        )
+        for h in range(count)
+    ]
+
+    def merged(h, *which):
+        for n in which:
+            swaps[h][n].wait_recv()
+            for p in (1, 0):
+                add_into(tg_block(h)(p, steps[n]), parts_in[h].at[level_of(steps[n]), 1 - side if p else side])
+
+    def keyval_part(h):
+        first, tiles = TOKEN_PARTS[h]
+
         def one(c, carry):
             part = px[c] + lax.dot_general(kvg[...], wkbuf[c], nt, preferred_element_type=f32)
             part = part.astype(bf16).reshape(2, 4, 2, 32, 512)
@@ -720,59 +782,62 @@
             for s in range(2):
                 for level in range(4):
                     for k in range(2):
-                        out_parts[h][k, level, s, :, cols] = part[s, level, k]
+                        parts_out[h][k, level, s, :, cols] = part[s, level, k]
             return carry
 
-        return one
+        lax.fori_loop(first, first + tiles, one, 0)
+        for s in swaps[h]:
+            s.start()
 
     def keyval_terms(i, carry):
         c = chosen(i, order)
         wk[c] = jnp.dot(turned_q[0:128, :], tok_cols(c), preferred_element_type=f32).astype(bf16)
         return carry
 
-    lax.fori_loop(0, 6, keyval_part(0, 0), 0)
-    for s in swaps[0]:
-        s.start()
+    keyval_part(0)
     turned_q[0:128, :] = total.T.astype(bf16)
     lax.fori_loop(0, 2, keyval_terms, 0)
     wk_sum.start(0, 1, 2, 3)
-    lax.fori_loop(6, 8, keyval_part(1, 6), 0)
-    for s in swaps[1]:
-        s.start()
+    keyval_part(1)
     merged(0, 0)
-    ring_toks.start(0, 1, 2, 3)
+    toks[0].start(0, 1, 2, 3)
+    keyval_part(2)
+    wq_sum.third()
+    merged(1, 0)
+    toks[1].start(0, 1, 2, 3)
     wp_sum.paired(0)
     wp_sum.start(4, 5)
-    merged(1, 0)
-    late_toks.start(0, 1, 2, 3)
+    merged(2, 0)
+    toks[2].start(0, 1, 2, 3)
+    merged(0, 1, 2, 3)
+    toks[0].second(1)
+    toks[0].second(0)
     wp_sum.paired(1, 2)
     wp_sum.second()
     lax.fori_loop(2, 8, keyval_terms, 0)
-    for n in (1, 2, 3):
-        merged(0, n)
-        merged(1, n)
-    ring_toks.second(1)
-    ring_toks.second(0)
-    wq_sum.third()
-    late_toks.second(1)
-    late_toks.second(0)
+    merged(1, 1, 2, 3)
+    toks[1].second(1)
+    toks[1].second(0)
     wk_sum.second(1)
     wk_sum.second(0)
-    ring_toks.third()
-    late_toks.third()
+    merged(2, 1, 2, 3)
+    toks[2].second(1)
+    toks[2].second(0)
+    for h in range(count):
+        toks[h].third()
     wk_sum.third()
     wq_sum.arrived(6, 7, 8)
     sum_ref[0:128, :] = wq_sum.total(...)
     sum_ref[128:256, :] = wp_sum.total(...)
-    ring_toks.arrived(6, 7, 8)
-    tg_ref[:, 0:3072] = ring_toks.total(...).astype(bf16)
-    late_toks.arrived(6, 7, 8)
-    tg_ref[:, 3072:4096] = late_toks.total(...).astype(bf16)
+    for h in range(count):
+        first, tiles = TOKEN_PARTS[h]
+        toks[h].arrived(6, 7, 8)
+        tg_ref[:, first * 512:(first + tiles) * 512] = toks[h].total(...).astype(bf16)
     wk_sum.arrived(6, 7, 8)
     sum_ref[256:384, :] = wk_sum.total(...)
-    for s in swap + swaps[0] + swaps[1]:
+    for s in swap + sum(swaps, []):
         s.wait_send()
-    for r in (keys, pair_keys, wq_sum, wp_sum, wk_sum, ring_toks, late_toks):
+    for r in [keys, pair_keys, wq_sum, wp_sum, wk_sum] + toks:
         r.finish()
 
 
@@ -788,7 +853,7 @@
             jax.ShapeDtypeStruct((32, 4096), bf16),
             jax.ShapeDtypeStruct((384, 512), f32),
         ),
-        in_specs=[hbm, hbm, hbm, vmem, hbm, vmem, vmem],
+        in_specs=[hbm] * 7,
         out_specs=(vmem, vmem),
         scratch_shapes=[
             pltpu.VMEM((16, 32, 4096), bf16),
@@ -815,20 +880,18 @@
             pltpu.VMEM((4, 64, 512), bf16),
             pltpu.VMEM((4, 128, 512), bf16),
             pltpu.VMEM((128, 512), bf16),
+            pltpu.VMEM((512, 256), bf16),
+            pltpu.VMEM((512, 128), f32),
+            pltpu.VMEM((512, 128), f32),
             pltpu.VMEM((8, 512, 512), f32),
-            pltpu.VMEM((2, 4, 2, 32, 3072), bf16),
-            pltpu.VMEM((4, 2, 32, 3072), bf16),
-            pltpu.VMEM((2, 4, 2, 32, 1024), bf16),
-            pltpu.VMEM((4, 2, 32, 1024), bf16),
-            pltpu.VMEM((4, 16, 3072), bf16),
-            pltpu.VMEM((4, 32, 3072), bf16),
-            pltpu.VMEM((32, 3072), bf16),
-            pltpu.VMEM((4, 16, 1024), bf16),
-            pltpu.VMEM((4, 32, 1024), bf16),
-            pltpu.VMEM((32, 1024), bf16),
-            dma((9,)), dma((9,)), dma((8,)), dma((8,)), dma((9,)), dma((9,)), dma((8,)), dma((8,)),
-            dma((9,)), dma((9,)), dma((9,)), dma((9,)), dma((9,)), dma((9,)),
-            dma((12,)), dma((12,)), dma((4,)),
+            [pltpu.VMEM((2, 4, 2, 32, 512 * n), bf16) for _, n in TOKEN_PARTS],
+            [pltpu.VMEM((4, 2, 32, 512 * n), bf16) for _, n in TOKEN_PARTS],
+            [pltpu.VMEM((4, 16, 512 * n), bf16) for _, n in TOKEN_PARTS],
+            [pltpu.VMEM((4, 32, 512 * n), bf16) for _, n in TOKEN_PARTS],
+            [pltpu.VMEM((32, 512 * n), bf16) for _, n in TOKEN_PARTS],
+            dma((9,)), dma((9,)), dma((8,)), dma((8,)), dma((8,)), dma((8,)),
+            dma((9,)), dma((9,)), dma((9,)), dma((9,)), dma((3, 9)), dma((3, 9)),
+            dma((16,)), dma((16,)), dma((7,)),
         ],
         compiler_params=pltpu.CompilerParams(collective_id=1, has_side_effects=True, vmem_limit_bytes=VMEM_LIMIT),
         name="reduce",

time: 110 us -> 111 us (level)
  Pallas kernels: 109 us -> 111 us
    pallas_call x1, Pallas kernels: 9.14 us -> 11.8 us  [attend(): pl.pallas_call(attend_kernel, out_shape=(jax.ShapeDtypeStruct((512, 256),...]
    pallas_call x1, Pallas kernels: 50.9 us -> 49.5 us  [reduce(): pl.pallas_call(reduce_kernel, out_shape=(jax.ShapeDtypeStruct((32, 4096),...]
where the time goes in v5:
time: 111 us
  Pallas kernels  111 us (100%)
    pallas_call x1, Pallas kernels, reduce(): pl.pallas_call(reduce_kernel, out_shape=(jax.ShapeDtypeStruct((32, 4096),...  49.5 us
    pallas_call x1, Pallas kernels, project(): pl.pallas_call(project_kernel, out_shape=(jax.ShapeDtypeStruct((512, 256)...  47.1 us
    pallas_call x1, Pallas kernels, attend(): pl.pallas_call(attend_kernel, out_shape=(jax.ShapeDtypeStruct((512, 256),...  11.8 us

profile of v5, /device:TPU:0, one launch (start us, length us, event | category | flops | bytes accessed | tf_op | source)
XLA Modules:
  0.0 111.2 jit_solution(12258408147480280965)
XLA Ops:
  0.6 47.1 %project.1 = (bf16[512,256]{1,0:T(8,128)(2,1)}, f32[512,128]{1,0:T(8,128)}, f32[512,128]{1,0:T(8,128)}, bf16[2,8,512,128]{3,2,1,0:T(8,128)(2,1)}, bf16[16,32,409...) custom-call(s32[32,128]{1,0:T(8,128)} %bitcast.6, f32[1,128]{1,0:T(1,128)} %constant.2.clone.freq_ref, ...), custom_call_target="tpu_custom_call" | custom-call | tf_op jit(solution)/shard_map/project/pallas_call | solution.py:603
  47.7 11.8 %attend.1 = (bf16[512,256]{1,0:T(8,128)(2,1)}, bf16[2,4096,128]{2,1,0:T(8,128)(2,1)}) custom-call(s32[4096]{0:T(1024)} %pos_ref.1, s32[32,128]{1,0:T(8,128)} %bitcast.7, bf16[512,256]{1,0:T(8,128)(2,1)} %get-tuple-element.17.q_ref, bf16[512,256]{1,0:T(8,128)(2,1)} %up_ref.1, bf16[2,4096,128]{2,1,0:T(8,128)(2,1)} %bitcast.5, ...), custom_call_target="tpu_custom_call" | custom-call | tf_op jit(solution)/shard_map/attend/pallas_call | solution.py:131
  59.5 49.5 %reduce.1 = (bf16[32,4096]{1,0:T(8,128)(2,1)}, f32[384,512]{1,0:T(8,128)}) custom-call(bf16[16,32,4096]{2,1,0:T(8,128)(2,1)} %get-tuple-element.14.tok_ref, bf16[8,512,256]{2,1,0:T(8,128)(2,1)} %get-tuple-element.15.wq_ref, bf16[8,512,128]{2,1,0:T(8,128)(2,1)} %get-tuple-element.16.wk_ref, bf16[512,256]{1,0:T(8,128)(2,1)} %get-tuple-element.21.qb_ref, ...), custom_call_target="tpu_custom_call" | custom-call | tf_op jit(solution)/shard_map/reduce/pallas_call | solution.py:850
  109.0 2.1 %finish.1 = (bf16[32,4096]{1,0:T(8,128)(2,1)}, f32[512,256]{1,0:T(8,128)}, f32[512,128]{1,0:T(8,128)}) custom-call(bf16[32,4096]{1,0:T(8,128)(2,1)} %get-tuple-element.23.tg_ref, f32[384,512]{1,0:T(8,128)} %get-tuple-element.24.sum_ref), custom_call_target="tpu_custom_call" | custom-call | tf_op jit(solution)/shard_map/finish/pallas_call | solution.py:908

commit v6 on v5

--- a/solution.py
+++ b/solution.py
@@ -633,13 +633,13 @@
     )(positions.reshape(32, 128), frequency, tokens, w_query, w_keyval)
 
 
-TOKEN_PARTS = ((0, 3), (3, 3), (6, 2))
+TOKEN_PARTS = ((0, 2), (2, 3), (5, 3))
 
 
 def reduce_kernel(tok_ref, wq_ref, wk_ref, qb_ref, dkv_ref, cos_ref, sin_ref, tg_ref, sum_ref,
                   tbuf, wqbuf, wkbuf, kv, kv_in, kv_halves, kv_wholes, kv_last, kp_pairs, kp_halves, kp_wholes, turned_q, kvg,
                   wq, wq_halves, wq_wholes, wq_last, wp_pairs, wp_halves, wp_wholes, wk, wk_halves, wk_wholes, wk_last,
-                  qb, cos_sc, sin_sc, px, parts_out, parts_in, parts_halves, parts_wholes, parts_last,
+                  qb, cos_sc, sin_sc, px, parts_out, parts_in, parts_halves, parts_wholes, parts_last, pair_parts,
                   k_send, k_recv, kp_send, kp_recv, wp_send, wp_recv, wq_send, wq_recv, wk_send, wk_recv,
                   t_send, t_recv, e_send, e_recv, local):
     f32 = jnp.float32
@@ -735,6 +735,8 @@
 
     lax.fori_loop(0, 8, query_part, 0)
     wq_sum.second(0)
+    wp_sum.paired(0)
+    wp_sum.start(4, 5)
     copies[3].wait()
     keys.arrived(6, 7, 8)
     total = jnp.concatenate([keys.total(...), pair_keys.total(...)], axis=0)
@@ -763,8 +765,11 @@
         Reduce(
             tg_block(h), 32, tp_peers, parts_halves[h], parts_wholes[h], parts_last[h], t_send.at[h], t_recv.at[h]
         )
-        for h in range(count)
+        for h in range(2)
     ]
+    pair_toks = PairReduce(
+        tg_block(2), 32, tp_peers, pair_parts, parts_halves[2], parts_wholes[2], t_send.at[2], t_recv.at[2]
+    )
 
     def merged(h, *which):
         for n in which:
@@ -796,48 +801,50 @@
 
     keyval_part(0)
     turned_q[0:128, :] = total.T.astype(bf16)
+    keyval_part(2)
+    merged(0, 0)
+    toks[0].start(0, 1, 2, 3)
     lax.fori_loop(0, 2, keyval_terms, 0)
     wk_sum.start(0, 1, 2, 3)
+    for n in range(4):
+        merged(2, n)
+        pair_toks.start(n)
     keyval_part(1)
-    merged(0, 0)
-    toks[0].start(0, 1, 2, 3)
-    keyval_part(2)
-    wq_sum.third()
     merged(1, 0)
     toks[1].start(0, 1, 2, 3)
-    wp_sum.paired(0)
-    wp_sum.start(4, 5)
-    merged(2, 0)
-    toks[2].start(0, 1, 2, 3)
     merged(0, 1, 2, 3)
     toks[0].second(1)
     toks[0].second(0)
     wp_sum.paired(1, 2)
     wp_sum.second()
     lax.fori_loop(2, 8, keyval_terms, 0)
+    pair_toks.paired(0)
+    pair_toks.start(4, 5)
     merged(1, 1, 2, 3)
     toks[1].second(1)
     toks[1].second(0)
     wk_sum.second(1)
     wk_sum.second(0)
-    merged(2, 1, 2, 3)
-    toks[2].second(1)
-    toks[2].second(0)
-    for h in range(count):
-        toks[h].third()
+    wq_sum.third()
+    pair_toks.paired(1, 2)
+    pair_toks.second()
+    toks[0].third()
+    toks[1].third()
     wk_sum.third()
     wq_sum.arrived(6, 7, 8)
     sum_ref[0:128, :] = wq_sum.total(...)
     sum_ref[128:256, :] = wp_sum.total(...)
-    for h in range(count):
+    for h in (0, 2, 1):
         first, tiles = TOKEN_PARTS[h]
-        toks[h].arrived(6, 7, 8)
-        tg_ref[:, first * 512:(first + tiles) * 512] = toks[h].total(...).astype(bf16)
+        if h < 2:
+            toks[h].arrived(6, 7, 8)
+        part = toks[h] if h < 2 else pair_toks
+        tg_ref[:, first * 512:(first + tiles) * 512] = part.total(...).astype(bf16)
     wk_sum.arrived(6, 7, 8)
     sum_ref[256:384, :] = wk_sum.total(...)
     for s in swap + sum(swaps, []):
         s.wait_send()
-    for r in [keys, pair_keys, wq_sum, wp_sum, wk_sum] + toks:
+    for r in [keys, pair_keys, wq_sum, wp_sum, wk_sum, pair_toks] + toks:
         r.finish()
 
 
@@ -889,6 +896,7 @@
             [pltpu.VMEM((4, 16, 512 * n), bf16) for _, n in TOKEN_PARTS],
             [pltpu.VMEM((4, 32, 512 * n), bf16) for _, n in TOKEN_PARTS],
             [pltpu.VMEM((32, 512 * n), bf16) for _, n in TOKEN_PARTS],
+            pltpu.VMEM((4, 32, 512 * TOKEN_PARTS[2][1]), bf16),
             dma((9,)), dma((9,)), dma((8,)), dma((8,)), dma((8,)), dma((8,)),
             dma((9,)), dma((9,)), dma((9,)), dma((9,)), dma((3, 9)), dma((3, 9)),
             dma((16,)), dma((16,)), dma((7,)),

time: 111 us -> 106 us (0.955)
  Pallas kernels: 111 us -> 105 us
    pallas_call x1, Pallas kernels: 49.5 us -> 46.3 us  [reduce(): pl.pallas_call(reduce_kernel, out_shape=(jax.ShapeDtypeStruct((32, 4096),...]
    pallas_call x1, Pallas kernels: 11.8 us -> 9.9 us  [attend(): pl.pallas_call(attend_kernel, out_shape=(jax.ShapeDtypeStruct((512, 256),...]
where the time goes in v6:
time: 106 us
  Pallas kernels  105 us (99%)
    pallas_call x1, Pallas kernels, project(): pl.pallas_call(project_kernel, out_shape=(jax.ShapeDtypeStruct((512, 256)...  47.1 us
    pallas_call x1, Pallas kernels, reduce(): pl.pallas_call(reduce_kernel, out_shape=(jax.ShapeDtypeStruct((32, 4096),...  46.3 us
    pallas_call x1, Pallas kernels, attend(): pl.pallas_call(attend_kernel, out_shape=(jax.ShapeDtypeStruct((512, 256),...  9.9 us
    pallas_call x1, Pallas kernels, finish(): pl.pallas_call(finish_kernel, grid=(2,), out_shape=(jax.ShapeDtypeStruct(...  2.15 us

profile of v6, /device:TPU:0, one launch (start us, length us, event | category | flops | bytes accessed | tf_op | source)
XLA Modules:
  0.0 106.0 jit_solution(15344751798639552023)
XLA Ops:
  0.6 47.1 %project.1 = (bf16[512,256]{1,0:T(8,128)(2,1)}, f32[512,128]{1,0:T(8,128)}, f32[512,128]{1,0:T(8,128)}, bf16[2,8,512,128]{3,2,1,0:T(8,128)(2,1)}, bf16[16,32,409...) custom-call(s32[32,128]{1,0:T(8,128)} %bitcast.6, f32[1,128]{1,0:T(1,128)} %constant.2.clone.freq_ref, ...), custom_call_target="tpu_custom_call" | custom-call | tf_op jit(solution)/shard_map/project/pallas_call | solution.py:603
  47.7 9.9 %attend.1 = (bf16[512,256]{1,0:T(8,128)(2,1)}, bf16[2,4096,128]{2,1,0:T(8,128)(2,1)}) custom-call(s32[4096]{0:T(1024)} %pos_ref.1, s32[32,128]{1,0:T(8,128)} %bitcast.7, bf16[512,256]{1,0:T(8,128)(2,1)} %get-tuple-element.17.q_ref, bf16[512,256]{1,0:T(8,128)(2,1)} %up_ref.1, bf16[2,4096,128]{2,1,0:T(8,128)(2,1)} %bitcast.5, ...), custom_call_target="tpu_custom_call" | custom-call | tf_op jit(solution)/shard_map/attend/pallas_call | solution.py:131
  57.6 46.3 %reduce.1 = (bf16[32,4096]{1,0:T(8,128)(2,1)}, f32[384,512]{1,0:T(8,128)}) custom-call(bf16[16,32,4096]{2,1,0:T(8,128)(2,1)} %get-tuple-element.14.tok_ref, bf16[8,512,256]{2,1,0:T(8,128)(2,1)} %get-tuple-element.15.wq_ref, bf16[8,512,128]{2,1,0:T(8,128)(2,1)} %get-tuple-element.16.wk_ref, bf16[512,256]{1,0:T(8,128)(2,1)} %get-tuple-element.21.qb_ref, ...), custom_call_target="tpu_custom_call" | custom-call | tf_op jit(solution)/shard_map/reduce/pallas_call | solution.py:857
  103.9 2.1 %finish.1 = (bf16[32,4096]{1,0:T(8,128)(2,1)}, f32[512,256]{1,0:T(8,128)}, f32[512,128]{1,0:T(8,128)}) custom-call(bf16[32,4096]{1,0:T(8,128)(2,1)} %get-tuple-element.23.tg_ref, f32[384,512]{1,0:T(8,128)} %get-tuple-element.24.sum_ref), custom_call_target="tpu_custom_call" | custom-call | tf_op jit(solution)/shard_map/finish/pallas_call | solution.py:916

commit v7 on v6

--- a/solution.py
+++ b/solution.py
@@ -407,11 +407,11 @@
     for c in copies + small:
         c.start()
     met(ctx_peers + tp_peers + [twin])
-    toks = Gather(lambda p, d: tbuf.at[tp_at(p, d), :, pl.ds(0, 3072)], 32, tp_peers, t_send, t_recv)
-    round_toks = RingGather(lambda p, d: tbuf.at[tp_at(p, d), :, pl.ds(3072, 1024)], 32, tp_peers, u_send, u_recv)
+    toks = Gather(lambda p, d: tbuf.at[tp_at(p, d), :, pl.ds(0, 3584)], 32, tp_peers, t_send, t_recv)
+    round_toks = RingGather(lambda p, d: tbuf.at[tp_at(p, d), :, pl.ds(3584, 512)], 32, tp_peers, u_send, u_recv)
     tshare = Share(lambda p, d: tbuf.at[tp_at(p, d)], lambda p, d: tbuf.at[tp_at(p, d, 1)], twin, c_send, c_recv)
-    wqa = Gather(lambda p, d: wqbuf.at[ctx_at(p, d), pl.ds(0, 416)], 416, ctx_peers, wa_send, wa_recv)
-    wqb = RingGather(lambda p, d: wqbuf.at[ctx_at(p, d), pl.ds(416, 96)], 96, ctx_peers, wb_send, wb_recv)
+    wqa = Gather(lambda p, d: wqbuf.at[ctx_at(p, d), pl.ds(0, 320)], 320, ctx_peers, wa_send, wa_recv)
+    wqb = RingGather(lambda p, d: wqbuf.at[ctx_at(p, d), pl.ds(320, 192)], 192, ctx_peers, wb_send, wb_recv)
     wk = Gather(lambda p, d: wkbuf.at[ctx_at(p, d)], 512, ctx_peers, wk_send, wk_recv)
     for c in copies:
         c.wait()
@@ -458,7 +458,7 @@
     wk.arrived(0, 1)
     wk.start(4, 5, 6, 7)
     wqb.arrived(0, 1)
-    wqb.start(2, 3, 5, 6)
+    wqb.start(2, 3)
     toks.arrived(4)
     toks.start(10)
     toks.arrived(7)
@@ -472,6 +472,7 @@
     wk.start(10)
     wk.arrived(7)
     wk.start(11)
+    wqb.start(5, 6)
     wqb.arrived(2, 3)
     wqb.start(7, 8)
     toks.arrived(10, 11)
@@ -484,6 +485,8 @@
     out_sin = pltpu.make_async_copy(sin_sc, sin_ref, local.at[7])
     out_cos.start()
     out_sin.start()
+    wqa.arrived(0, 1)
+    wqa.start(4, 5, 6, 7)
     tshare.arrived()
     out_tok = pltpu.make_async_copy(tbuf, tok_out, local.at[4])
     out_tok.start()
@@ -519,8 +522,6 @@
     keys.start(2, 3)
     round_keys.start(4)
     kshare.start(0)
-    wqa.arrived(0, 1)
-    wqa.start(4, 5, 6, 7)
     wqa.arrived(8, 9)
     multiply(acc, wqbuf, [ctx_at(0, 0), ctx_at(0, -1), ctx_at(0, 1), ctx_at(0, 2)])
     round_keys.arrived(0, 1)

time: 106 us -> 102 us (0.962)
  Pallas kernels: 105 us -> 102 us
    pallas_call x1, Pallas kernels: 46.3 us -> 44.4 us  [reduce(): pl.pallas_call(reduce_kernel, out_shape=(jax.ShapeDtypeStruct((32, 4096),...]
    pallas_call x1, Pallas kernels: 47.1 us -> 45.7 us  [project(): pl.pallas_call(project_kernel, out_shape=(jax.ShapeDtypeStruct((512, 256)...]
where the time goes in v7:
time: 102 us
  Pallas kernels  102 us (100%)
    pallas_call x1, Pallas kernels, project(): pl.pallas_call(project_kernel, out_shape=(jax.ShapeDtypeStruct((512, 256)...  45.7 us
    pallas_call x1, Pallas kernels, reduce(): pl.pallas_call(reduce_kernel, out_shape=(jax.ShapeDtypeStruct((32, 4096),...  44.4 us
    pallas_call x1, Pallas kernels, attend(): pl.pallas_call(attend_kernel, out_shape=(jax.ShapeDtypeStruct((512, 256),...  9.59 us
    pallas_call x1, Pallas kernels, finish(): pl.pallas_call(finish_kernel, grid=(2,), out_shape=(jax.ShapeDtypeStruct(...  2.15 us

profile of v7, /device:TPU:0, one launch (start us, length us, event | category | flops | bytes accessed | tf_op | source)
XLA Modules:
  0.0 102.5 jit_solution(2412650974030142132)
XLA Ops:
  0.6 45.7 %project.1 = (bf16[512,256]{1,0:T(8,128)(2,1)}, f32[512,128]{1,0:T(8,128)}, f32[512,128]{1,0:T(8,128)}, bf16[2,8,512,128]{3,2,1,0:T(8,128)(2,1)}, bf16[16,32,409...) custom-call(s32[32,128]{1,0:T(8,128)} %bitcast.6, f32[1,128]{1,0:T(1,128)} %constant.2.clone.freq_ref, ...), custom_call_target="tpu_custom_call" | custom-call | tf_op jit(solution)/shard_map/project/pallas_call | solution.py:604
  46.4 9.6 %attend.1 = (bf16[512,256]{1,0:T(8,128)(2,1)}, bf16[2,4096,128]{2,1,0:T(8,128)(2,1)}) custom-call(s32[4096]{0:T(1024)} %pos_ref.1, s32[32,128]{1,0:T(8,128)} %bitcast.7, bf16[512,256]{1,0:T(8,128)(2,1)} %get-tuple-element.17.q_ref, bf16[512,256]{1,0:T(8,128)(2,1)} %up_ref.1, bf16[2,4096,128]{2,1,0:T(8,128)(2,1)} %bitcast.5, ...), custom_call_target="tpu_custom_call" | custom-call | tf_op jit(solution)/shard_map/attend/pallas_call | solution.py:131
  56.0 44.4 %reduce.1 = (bf16[32,4096]{1,0:T(8,128)(2,1)}, f32[384,512]{1,0:T(8,128)}) custom-call(bf16[16,32,4096]{2,1,0:T(8,128)(2,1)} %get-tuple-element.14.tok_ref, bf16[8,512,256]{2,1,0:T(8,128)(2,1)} %get-tuple-element.15.wq_ref, bf16[8,512,128]{2,1,0:T(8,128)(2,1)} %get-tuple-element.16.wk_ref, bf16[512,256]{1,0:T(8,128)(2,1)} %get-tuple-element.21.qb_ref, ...), custom_call_target="tpu_custom_call" | custom-call | tf_op jit(solution)/shard_map/reduce/pallas_call | solution.py:858
  100.3 2.1 %finish.1 = (bf16[32,4096]{1,0:T(8,128)(2,1)}, f32[512,256]{1,0:T(8,128)}, f32[512,128]{1,0:T(8,128)}) custom-call(bf16[32,4096]{1,0:T(8,128)(2,1)} %get-tuple-element.23.tg_ref, f32[384,512]{1,0:T(8,128)} %get-tuple-element.24.sum_ref), custom_call_target="tpu_custom_call" | custom-call | tf_op jit(solution)/shard_map/finish/pallas_call | solution.py:917

commit v8 on v7

--- a/solution.py
+++ b/solution.py
@@ -716,9 +716,9 @@
     lax.fori_loop(1, 2, query_terms, 0)
     wq_sum.start(2, 3)
     lax.fori_loop(2, 4, query_terms, 0)
-    wp_sum.start(1)
     keys.second(1)
     keys.second(0)
+    wp_sum.start(1)
     pair_keys.paired(0)
     pair_keys.start(4, 5)
     lax.fori_loop(4, 6, query_terms, 0)
@@ -728,6 +728,9 @@
     keys.third()
     lax.fori_loop(6, 8, query_terms, 0)
     wp_sum.start(2, 3)
+    wq_sum.second(0)
+    wp_sum.paired(0)
+    wp_sum.start(4, 5)
     copies[2].wait()
 
     def query_part(c, carry):
@@ -735,9 +738,6 @@
         return carry
 
     lax.fori_loop(0, 8, query_part, 0)
-    wq_sum.second(0)
-    wp_sum.paired(0)
-    wp_sum.start(4, 5)
     copies[3].wait()
     keys.arrived(6, 7, 8)
     total = jnp.concatenate([keys.total(...), pair_keys.total(...)], axis=0)

time: 102 us -> 103 us (level); the launches traced: 102 us -> 102 us
    pallas_call x1, Pallas kernels: 9.59 us -> 8.48 us  [attend(): pl.pallas_call(attend_kernel, out_shape=(jax.ShapeDtypeStruct((512, 256),...]
where the time goes in v8:
time: 103 us; the launch traced here: 102 us
  Pallas kernels  101 us (98%)
    pallas_call x1, Pallas kernels, project(): pl.pallas_call(project_kernel, out_shape=(jax.ShapeDtypeStruct((512, 256)...  45.7 us
    pallas_call x1, Pallas kernels, reduce(): pl.pallas_call(reduce_kernel, out_shape=(jax.ShapeDtypeStruct((32, 4096),...  44.6 us
    pallas_call x1, Pallas kernels, attend(): pl.pallas_call(attend_kernel, out_shape=(jax.ShapeDtypeStruct((512, 256),...  8.48 us
    pallas_call x1, Pallas kernels, finish(): pl.pallas_call(finish_kernel, grid=(2,), out_shape=(jax.ShapeDtypeStruct(...  2.15 us

profile of v8, /device:TPU:0, one launch (start us, length us, event | category | flops | bytes accessed | tf_op | source)
XLA Modules:
  0.0 101.6 jit_solution(4159169479932453285)
XLA Ops:
  0.6 45.7 %project.1 = (bf16[512,256]{1,0:T(8,128)(2,1)}, f32[512,128]{1,0:T(8,128)}, f32[512,128]{1,0:T(8,128)}, bf16[2,8,512,128]{3,2,1,0:T(8,128)(2,1)}, bf16[16,32,409...) custom-call(s32[32,128]{1,0:T(8,128)} %bitcast.6, f32[1,128]{1,0:T(1,128)} %constant.2.clone.freq_ref, ...), custom_call_target="tpu_custom_call" | custom-call | tf_op jit(solution)/shard_map/project/pallas_call | solution.py:604
  46.4 8.5 %attend.1 = (bf16[512,256]{1,0:T(8,128)(2,1)}, bf16[2,4096,128]{2,1,0:T(8,128)(2,1)}) custom-call(s32[4096]{0:T(1024)} %pos_ref.1, s32[32,128]{1,0:T(8,128)} %bitcast.7, bf16[512,256]{1,0:T(8,128)(2,1)} %get-tuple-element.17.q_ref, bf16[512,256]{1,0:T(8,128)(2,1)} %up_ref.1, bf16[2,4096,128]{2,1,0:T(8,128)(2,1)} %bitcast.5, ...), custom_call_target="tpu_custom_call" | custom-call | tf_op jit(solution)/shard_map/attend/pallas_call | solution.py:131
  54.9 44.6 %reduce.1 = (bf16[32,4096]{1,0:T(8,128)(2,1)}, f32[384,512]{1,0:T(8,128)}) custom-call(bf16[16,32,4096]{2,1,0:T(8,128)(2,1)} %get-tuple-element.14.tok_ref, bf16[8,512,256]{2,1,0:T(8,128)(2,1)} %get-tuple-element.15.wq_ref, bf16[8,512,128]{2,1,0:T(8,128)(2,1)} %get-tuple-element.16.wk_ref, bf16[512,256]{1,0:T(8,128)(2,1)} %get-tuple-element.21.qb_ref, ...), custom_call_target="tpu_custom_call" | custom-call | tf_op jit(solution)/shard_map/reduce/pallas_call | solution.py:858
  99.4 2.1 %finish.1 = (bf16[32,4096]{1,0:T(8,128)(2,1)}, f32[512,256]{1,0:T(8,128)}, f32[512,128]{1,0:T(8,128)}) custom-call(bf16[32,4096]{1,0:T(8,128)(2,1)} %get-tuple-element.23.tg_ref, f32[384,512]{1,0:T(8,128)} %get-tuple-element.24.sum_ref), custom_call_target="tpu_custom_call" | custom-call | tf_op jit(solution)/shard_map/finish/pallas_call | solution.py:917
